TPU v7x, 32 devices: a whole 2x2x4 slice. The times are simulated.
32 devices in a mesh: chain: 16 (over z, y, core), aux: 2 (over x).
Axes of the slice: x: 2, y: 2, z: 4, core: 2. Of those that a mesh axis runs over, the one named last changes fastest.
Arguments:
- occupied: bfloat16 [2048, 1152], P('chain'), may hold values from -0.1875 to 0.1875
- virtual: bfloat16 [2048, 1152], P('chain'), may hold values from -0.1875 to 0.1875
- three_centre: bfloat16 [32, 2048, 1152], P('aux', 'chain'), may hold values from -6 to 6
- kernel: bfloat16 [32, 32], P('aux'), may hold values from -1 to 1
- profile: int32 [16], replicated, may hold values from 2 to 4
- atom_map: int32 [32], P('aux'), may hold values from 0 to 15
Outputs:
- band_gradient: float32 [2048, 1152], P(('chain', 'aux'))
- polarization: float32 [32, 32], P('aux')
All inputs are finite; a program needn't handle non-finite values.
Results may differ from a plain program's by a relative error of at most 0.0042.
Values may be sent and summed in bfloat16 or wider, within the bound.
No kernel may reach another device: no remote copies, remote signals or barrier semaphores. Data moves between devices by JAX's collectives and lax.ppermute only.
A program may use at most 128 MiB of HBM per device.

v0:
```python
import math

import jax
import jax.numpy as jnp
from jax import lax
from jax.sharding import PartitionSpec as P


def passed_along(block, axis, distance):
    devices = range(lax.axis_size(axis))
    route = [(i - distance, i) for i in devices if i - distance in devices]
    return lax.ppermute(block, axis, route)


def shift_blocks(matrix, offset, block_size):
    if offset == 0:
        return matrix
    padding = jnp.zeros(matrix.shape[:-1] + (abs(offset) * block_size,), matrix.dtype)
    if offset > 0:
        return jnp.concatenate([padding, matrix[..., : -offset * block_size]], -1)
    return jnp.concatenate([matrix[..., -offset * block_size :], padding], -1)


def body(occupied, virtual, three_centre, kernel, profile, atom_map):
    block_size = occupied.shape[0]
    band_cols = occupied.shape[1]
    slots_total = band_cols // block_size
    spread = (slots_total - 1) // 2
    nblocks = lax.axis_size("chain")
    position = lax.axis_index("chain")
    slot_ids = jnp.arange(slots_total, dtype=jnp.int32)
    block_ids = jnp.arange(nblocks, dtype=jnp.int32)
    others = position + slot_ids - spread
    neighbours = jnp.sum(jnp.where(block_ids[None, :] == others[:, None], profile[None, :], 0), 1)
    own_width = jnp.sum(jnp.where(block_ids == position, profile, 0))
    allowed = jnp.abs(slot_ids - spread) <= jnp.minimum(own_width, neighbours)
    column_keep = jnp.repeat(allowed, block_size)
    zero_half = jnp.zeros((), jnp.bfloat16)
    occ_masked = jnp.where(column_keep[None, :], occupied, zero_half)
    vir_masked = jnp.where(column_keep[None, :], virtual, zero_half)
    both_bands = jnp.stack([occ_masked, vir_masked])
    fetched = []
    for slot_index in range(slots_total):
        if slot_index == spread:
            fetched.append(both_bands)
        else:
            fetched.append(passed_along(both_bands, "chain", spread - slot_index))
    stack_occ = jnp.concatenate(
        [shift_blocks(fetched[k][0], k - spread, block_size) for k in range(slots_total)], 0
    )
    stack_vir = jnp.concatenate(
        [shift_blocks(fetched[k][1], k - spread, block_size) for k in range(slots_total)], 0
    )
    aux_here = three_centre.shape[0]
    aux_total = kernel.shape[1]
    screen = jnp.abs(atom_map - position) <= nblocks // 4
    local = jnp.where(column_keep[None, None, :] & screen[:, None, None], three_centre, zero_half)
    screened = local.reshape(aux_here * block_size, band_cols)
    coupled = jnp.dot(screened, stack_occ, preferred_element_type=jnp.float32).astype(jnp.bfloat16)
    coupled = coupled.reshape(aux_here, block_size * band_cols)
    partner = jnp.dot(screened, stack_vir, preferred_element_type=jnp.float32).astype(jnp.bfloat16)
    partner = partner.reshape(aux_here, block_size, band_cols)
    piece = lax.all_gather(partner, "aux", axis=0, tiled=True)
    piece_rows = piece.shape[0]
    columns = piece.reshape(piece_rows, block_size * band_cols)
    products = lax.dot_general(
        coupled, columns, (((1,), (1,)), ((), ())), preferred_element_type=jnp.float32
    )
    polar_part = products
    response_sum = jnp.dot(kernel, columns, preferred_element_type=jnp.float32)
    polar_part, response_sum = (polar_part, response_sum)
    polarization = lax.psum(polar_part, "chain") * (
        1.0 / math.sqrt(block_size * nblocks * band_cols)
    )
    response = response_sum.astype(jnp.bfloat16).reshape(aux_here * block_size, band_cols)
    partials = lax.dot_general(
        screened, response, (((0,), (0,)), ((), ())), preferred_element_type=jnp.float32
    )
    partials = partials.reshape(slots_total, block_size, band_cols)
    gathered_sum = partials[spread]
    for slot_index in range(slots_total):
        if slot_index != spread:
            moved = shift_blocks(partials[slot_index], spread - slot_index, block_size)
            gathered_sum = gathered_sum + passed_along(moved, "chain", slot_index - spread)
    gathered_sum = lax.psum_scatter(gathered_sum, "aux", scatter_dimension=0, tiled=True)
    scale_grad = 1.0 / math.sqrt(block_size * aux_total)
    band_gradient = (
        jnp.where(column_keep[None, :], gathered_sum, jnp.zeros((), jnp.float32)) * scale_grad
    )
    return (band_gradient, polarization)


def solution(mesh):
    placed = (
        P("chain", None),
        P("chain", None),
        P("aux", "chain", None),
        P("aux", None),
        P(),
        P("aux"),
    )
    return jax.shard_map(
        body,
        mesh=mesh,
        in_specs=placed,
        out_specs=(P(("chain", "aux"), None), P("aux", None)),
        check_vma=False,
    )
```

profile of v0, /device:TPU:0, one launch (start us, length us, event | category | flops | bytes accessed | tf_op | source)
XLA Modules:
  0.0 369.4 jit_solution(13112788531242796778)
XLA Ops:
  7.2 0.0 copy-start
  7.2 0.0 all-gather.2.cloned.1.call-start
  7.2 1.3 fusion.12
  8.5 0.8 select_reduce_fusion
  9.4 0.7 minimum_compare_fusion
  10.0 0.1 broadcast_bitcast_fusion
  10.1 1.1 fusion.9
  11.2 0.1 pad_maximum_fusion
  11.3 1.3 collective-permute-start.7
  12.6 1.3 collective-permute-start.6
  13.9 1.3 collective-permute-start.5
  15.2 1.3 collective-permute-start.4
  16.5 3.1 collective-permute-start.3
  19.6 0.7 abs_compare_fusion
  20.2 0.1 broadcast_and_fusion
  20.3 2.8 broadcast_select_fusion
  23.2 7.3 %collective-permute-done.7 = bf16[2,128,1152]{2,1,0:T(8,128)(2,1)S(1)} collective-permute-done((bf16[2,128,1152]{2,1,0:T(8,128)(2,1)S(1)}, bf16[2,128,1152]{2,1,0:T(8,128)(2,1)S(1)}, u32[]{:S(2)}, u32[]{:S(2)}) %collective-permute-start.7) | collective-permute-done | bytes 589856 | tf_op jit(solution)/shard_map/ppermute | solution.py:12
  30.4 2.8 collective-permute-start.2
  33.2 0.0 collective-permute-done.6
  33.3 6.0 %collective-permute-start.1 = (bf16[2,128,1152]{2,1,0:T(8,128)(2,1)S(1)}, bf16[2,128,1152]{2,1,0:T(8,128)(2,1)S(1)}, u32[]{:S(2)}, u32[]{:S(2)}) collective-permute-start(bf16[2,128,1152]{2,1,0:T(8,128)(2,1)S(1)} %pad_maximum_fusion), channel_id=1, source_target_pairs={{0,6},{2,8},{4,10},{6,12},{8,14},{10,16},{12,18},{14,20},{16,22},{... | collective-permute-start | bytes 1769480 | tf_op jit(solution)/shard_map/ppermute | solution.py:12
  39.3 0.0 collective-permute-done.5
  39.3 24.2 %collective-permute-start = (bf16[2,128,1152]{2,1,0:T(8,128)(2,1)S(1)}, bf16[2,128,1152]{2,1,0:T(8,128)(2,1)S(1)}, u32[]{:S(2)}, u32[]{:S(2)}) collective-permute-start(bf16[2,128,1152]{2,1,0:T(8,128)(2,1)S(1)} %pad_maximum_fusion), channel_id=1, source_target_pairs={{0,8},{2,10},{4,12},{6,14},{8,16},{10,18},{12,20},{14,22},{16,24},... | collective-permute-start | bytes 1769480 | tf_op jit(solution)/shard_map/ppermute | solution.py:12
  63.6 0.0 collective-permute-done.3
  63.7 4.2 %collective-permute-done.2 = bf16[2,128,1152]{2,1,0:T(8,128)(2,1)S(1)} collective-permute-done((bf16[2,128,1152]{2,1,0:T(8,128)(2,1)S(1)}, bf16[2,128,1152]{2,1,0:T(8,128)(2,1)S(1)}, u32[]{:S(2)}, u32[]{:S(2)}) %collective-permute-start.2) | collective-permute-done | bytes 589856 | tf_op jit(solution)/shard_map/ppermute | solution.py:12
  68.2 6.0 %collective-permute-done.1 = bf16[2,128,1152]{2,1,0:T(8,128)(2,1)S(1)} collective-permute-done((bf16[2,128,1152]{2,1,0:T(8,128)(2,1)S(1)}, bf16[2,128,1152]{2,1,0:T(8,128)(2,1)S(1)}, u32[]{:S(2)}, u32[]{:S(2)}) %collective-permute-start.1) | collective-permute-done | bytes 589856 | tf_op jit(solution)/shard_map/ppermute | solution.py:12
  74.4 0.0 copy-start.3
  74.4 0.0 copy-start.4
  74.7 0.6 copy-done.3
  75.3 0.1 copy-done.4
  75.4 0.1 fusion.8
  75.6 0.1 pad_dynamic-update-slice_fusion.3
  75.8 8.6 %convolution_convert_fusion.2 = bf16[2048,1152]{1,0:T(8,128)(2,1)} fusion(bf16[2048,1152]{1,0:T(8,128)(2,1)S(1)} %bitcast.58, bf16[1152,1152]{1,0:T(8,128)(2,1)S(1)} %pad_dynamic-update-slice_fusion.8), kind=kOutput, calls=%fused_computation.3 | convolution fusion | flops 5438177280 | bytes 12091392 | tf_op jit(solution)/shard_map/dot_general | solution.py:61
  84.4 0.0 all-gather.2.cloned.1.call-update
  84.4 0.2 reduce-scatter.2.cloned.1.call-start
  84.7 122.4 %all-gather.2.cloned.1.call-done = bf16[32,128,1152]{2,1,0:T(8,128)(2,1)} async-done(((bf16[16,128,1152]{2,1,0:T(8,128)(2,1)}), bf16[32,128,1152]{2,1,0:T(8,128)(2,1)}) %all-gather.2.cloned.1.call-update) | async-done | bytes 9437200 | tf_op jit(solution)/shard_map/all_gather | solution.py:63
  207.0 12.8 %copy.8 = bf16[4,8,128,1152]{3,1,2,0:T(8,128)(2,1)} copy(bf16[4,8,128,1152]{3,2,1,0:T(8,128)(2,1)} %bitcast.56) | data formatting | bytes 18874368
  219.8 7.2 %fusion = bf16[16,147456]{1,0:T(8,128)(2,1)} fusion(bf16[16,32]{1,0:T(8,128)(2,1)S(1)} %copy-done, bf16[32,147456]{1,0:T(8,128)(2,1)} %bitcast.54), kind=kOutput, calls=%fused_computation.1 | convolution fusion | flops 153354240 | bytes 14156800 | tf_op jit(solution)/shard_map/dot_general | solution.py:70
  227.0 5.3 %reshape.79 = bf16[2048,1152]{1,0:T(8,128)(2,1)} reshape(bf16[16,147456]{1,0:T(8,128)(2,1)} %fusion) | data formatting | bytes 9437184 | tf_op jit(solution)/shard_map/reshape | solution.py:75
  232.2 10.3 %fusion.17 = f32[1152,1152]{1,0:T(8,128)S(1)} fusion(bf16[2048,1152]{1,0:T(8,128)(2,1)} %bitcast.59, bf16[2048,1152]{1,0:T(8,128)(2,1)} %reshape.79), kind=kOutput, calls=%fused_computation.67 | convolution fusion | flops 5435817984 | bytes 14745600 | tf_op jit(solution)/shard_map/dot_general | solution.py:76
  242.6 0.1 fusion.14
  242.8 3.4 collective-permute-start.15
  246.2 1.3 collective-permute-start.8
  247.6 2.4 collective-permute-start.14
  250.0 1.3 collective-permute-start.9
  251.3 0.1 fusion.15
  251.5 4.3 %collective-permute-start.13 = (f32[128,1152]{1,0:T(8,128)S(1)}, f32[128,1152]{1,0:T(8,128)S(1)}, u32[]{:S(2)}, u32[]{:S(2)}) collective-permute-start(f32[128,1152]{1,0:T(8,128)S(1)} %concatenate.92), channel_id=1, source_target_pairs={{0,4},{2,6},{4,8},{6,10},{8,12},{10,14},{12,16},{14,18},{16,20},{1... | collective-permute-start | bytes 1769480 | tf_op jit(solution)/shard_map/ppermute | solution.py:12
  255.8 0.1 fusion.16
  256.0 3.8 %collective-permute-done.15 = f32[128,1152]{1,0:T(8,128)S(1)} collective-permute-done((f32[128,1152]{1,0:T(8,128)S(1)}, f32[128,1152]{1,0:T(8,128)S(1)}, u32[]{:S(2)}, u32[]{:S(2)}) %collective-permute-start.15) | collective-permute-done | bytes 589856 | tf_op jit(solution)/shard_map/ppermute | solution.py:12
  259.9 1.3 collective-permute-start.10
  261.2 3.1 collective-permute-done.8
  264.3 1.3 collective-permute-start.12
  265.6 0.0 collective-permute-done.14
  265.6 1.3 collective-permute-start.11
  267.1 27.6 %collective-permute-done.13 = f32[128,1152]{1,0:T(8,128)S(1)} collective-permute-done((f32[128,1152]{1,0:T(8,128)S(1)}, f32[128,1152]{1,0:T(8,128)S(1)}, u32[]{:S(2)}, u32[]{:S(2)}) %collective-permute-start.13) | collective-permute-done | bytes 589856 | tf_op jit(solution)/shard_map/ppermute | solution.py:12
  294.7 0.0 collective-permute-done.10
  294.7 0.0 collective-permute-done.12
  294.7 1.1 fusion.7
  295.8 0.0 reduce-scatter.2.cloned.1.call-update
  295.8 10.4 %convolution_convert_fusion.1 = bf16[2048,1152]{1,0:T(8,128)(2,1)} fusion(bf16[2048,1152]{1,0:T(8,128)(2,1)} %bitcast.60, bf16[1152,1152]{1,0:T(8,128)(2,1)S(1)} %pad_dynamic-update-slice_fusion), kind=kOutput, calls=%fused_computation.2 | convolution fusion | flops 5438177280 | bytes 12091392 | tf_op jit(solution)/shard_map/dot_general | solution.py:59
  306.2 5.3 %reshape.80 = bf16[16,147456]{1,0:T(8,128)(2,1)} reshape(bf16[2048,1152]{1,0:T(8,128)(2,1)} %convolution_convert_fusion.1) | data formatting | bytes 9437184 | tf_op jit(solution)/shard_map/reshape | solution.py:60
  311.5 7.8 %fusion.18 = f32[16,32]{1,0:T(8,128)S(1)} fusion(bf16[16,147456]{1,0:T(8,128)(2,1)} %reshape.80, bf16[32,147456]{1,0:T(8,128)(2,1)} %bitcast.55), kind=kOutput, calls=%fused_computation.68 | convolution fusion | flops 150994944 | bytes 14157824 | tf_op jit(solution)/shard_map/dot_general | solution.py:66
  319.3 40.9 %psum.7 = f32[16,32]{1,0:T(8,128)S(1)} all-reduce(f32[16,32]{1,0:T(8,128)S(1)} %fusion.18), channel_id=1, replica_groups=mesh['chain'=16,'aux'=2] {'chain'}, use_global_device_ids=true, to_apply=%region_3.4 | all-reduce | flops 512 | bytes 4096 | tf_op jit(solution)/shard_map/psum | solution.py:72
  360.3 0.6 broadcast_multiply_fusion
  360.9 1.7 select_multiply_fusion
  (58 shorter events, 1.4 us)
Async XLA Ops:
  7.2 212.6 %copy-start = (bf16[16,32]{1,0:T(8,128)(2,1)S(1)}, bf16[16,32]{1,0:T(8,128)(2,1)}, u32[]{:S(2)}) copy-start(bf16[16,32]{1,0:T(8,128)(2,1)} %param.9) | copy-start | bytes 3076
  7.2 199.8 %all-gather.2.cloned.1.call-start = ((), (), s32[]{:S(2)}) async-start(), calls=%async_computation.1 | async-start | bytes 14155776 | tf_op jit(solution)/shard_map/all_gather | solution.py:63
  11.3 19.1 %collective-permute-start.7 = (bf16[2,128,1152]{2,1,0:T(8,128)(2,1)S(1)}, bf16[2,128,1152]{2,1,0:T(8,128)(2,1)S(1)}, u32[]{:S(2)}, u32[]{:S(2)}) collective-permute-start(bf16[2,128,1152]{2,1,0:T(8,128)(2,1)S(1)} %pad_maximum_fusion), channel_id=1, source_target_pairs={{8,0},{10,2},{12,4},{14,6},{16,8},{18,10},{20,12},{22,14},{24,16},... | collective-permute-start | bytes 1769480 | tf_op jit(solution)/shard_map/ppermute | solution.py:12
  12.6 20.7 %collective-permute-start.6 = (bf16[2,128,1152]{2,1,0:T(8,128)(2,1)S(1)}, bf16[2,128,1152]{2,1,0:T(8,128)(2,1)S(1)}, u32[]{:S(2)}, u32[]{:S(2)}) collective-permute-start(bf16[2,128,1152]{2,1,0:T(8,128)(2,1)S(1)} %pad_maximum_fusion), channel_id=1, source_target_pairs={{6,0},{8,2},{10,4},{12,6},{14,8},{16,10},{18,12},{20,14},{22,16},{... | collective-permute-start | bytes 1769480 | tf_op jit(solution)/shard_map/ppermute | solution.py:12
  13.9 25.4 %collective-permute-start.5 = (bf16[2,128,1152]{2,1,0:T(8,128)(2,1)S(1)}, bf16[2,128,1152]{2,1,0:T(8,128)(2,1)S(1)}, u32[]{:S(2)}, u32[]{:S(2)}) collective-permute-start(bf16[2,128,1152]{2,1,0:T(8,128)(2,1)S(1)} %pad_maximum_fusion), channel_id=1, source_target_pairs={{4,0},{6,2},{8,4},{10,6},{12,8},{14,10},{16,12},{18,14},{20,16},{2... | collective-permute-start | bytes 1769480 | tf_op jit(solution)/shard_map/ppermute | solution.py:12
  15.2 48.4 %collective-permute-start.4 = (bf16[2,128,1152]{2,1,0:T(8,128)(2,1)S(1)}, bf16[2,128,1152]{2,1,0:T(8,128)(2,1)S(1)}, u32[]{:S(2)}, u32[]{:S(2)}) collective-permute-start(bf16[2,128,1152]{2,1,0:T(8,128)(2,1)S(1)} %pad_maximum_fusion), channel_id=1, source_target_pairs={{2,0},{4,2},{6,4},{8,6},{10,8},{12,10},{14,12},{16,14},{18,16},{20... | collective-permute-start | bytes 1769480 | tf_op jit(solution)/shard_map/ppermute | solution.py:12
  16.5 47.1 %collective-permute-start.3 = (bf16[2,128,1152]{2,1,0:T(8,128)(2,1)S(1)}, bf16[2,128,1152]{2,1,0:T(8,128)(2,1)S(1)}, u32[]{:S(2)}, u32[]{:S(2)}) collective-permute-start(bf16[2,128,1152]{2,1,0:T(8,128)(2,1)S(1)} %pad_maximum_fusion), channel_id=1, source_target_pairs={{0,2},{2,4},{4,6},{6,8},{8,10},{10,12},{12,14},{14,16},{16,18},{18... | collective-permute-start | bytes 1769480 | tf_op jit(solution)/shard_map/ppermute | solution.py:12
  23.1 52.6 %copy-start.2 = (bf16[16,128,1152]{2,1,0:T(8,128)(2,1)}, bf16[16,128,1152]{2,1,0:T(8,128)(2,1)S(1)}, u32[]{:S(2)}) copy-start(bf16[16,128,1152]{2,1,0:T(8,128)(2,1)S(1)} %broadcast_select_fusion) | copy-start | bytes 14155780
  30.4 37.5 %collective-permute-start.2 = (bf16[2,128,1152]{2,1,0:T(8,128)(2,1)S(1)}, bf16[2,128,1152]{2,1,0:T(8,128)(2,1)S(1)}, u32[]{:S(2)}, u32[]{:S(2)}) collective-permute-start(bf16[2,128,1152]{2,1,0:T(8,128)(2,1)S(1)} %pad_maximum_fusion), channel_id=1, source_target_pairs={{0,4},{2,6},{4,8},{6,10},{8,12},{10,14},{12,16},{14,18},{16,20},{1... | collective-permute-start | bytes 1769480 | tf_op jit(solution)/shard_map/ppermute | solution.py:12
  33.3 41.0 %collective-permute-start.1 = (bf16[2,128,1152]{2,1,0:T(8,128)(2,1)S(1)}, bf16[2,128,1152]{2,1,0:T(8,128)(2,1)S(1)}, u32[]{:S(2)}, u32[]{:S(2)}) collective-permute-start(bf16[2,128,1152]{2,1,0:T(8,128)(2,1)S(1)} %pad_maximum_fusion), channel_id=1, source_target_pairs={{0,6},{2,8},{4,10},{6,12},{8,14},{10,16},{12,18},{14,20},{16,22},{... | collective-permute-start | bytes 1769480 | tf_op jit(solution)/shard_map/ppermute | solution.py:12
  39.3 35.0 %collective-permute-start = (bf16[2,128,1152]{2,1,0:T(8,128)(2,1)S(1)}, bf16[2,128,1152]{2,1,0:T(8,128)(2,1)S(1)}, u32[]{:S(2)}, u32[]{:S(2)}) collective-permute-start(bf16[2,128,1152]{2,1,0:T(8,128)(2,1)S(1)} %pad_maximum_fusion), channel_id=1, source_target_pairs={{0,8},{2,10},{4,12},{6,14},{8,16},{10,18},{12,20},{14,22},{16,24},... | collective-permute-start | bytes 1769480 | tf_op jit(solution)/shard_map/ppermute | solution.py:12
  74.4 1.0 copy-start.3
  74.4 1.0 copy-start.4
  84.4 276.4 %reduce-scatter.2.cloned.1.call-start = ((), (), s32[]{:S(2)}) async-start(), calls=%async_computation.2 | async-start | bytes 884736 | tf_op jit(solution)/shard_map/reduce_scatter | solution.py:85
  242.8 17.1 %collective-permute-start.15 = (f32[128,1152]{1,0:T(8,128)S(1)}, f32[128,1152]{1,0:T(8,128)S(1)}, u32[]{:S(2)}, u32[]{:S(2)}) collective-permute-start(f32[128,1152]{1,0:T(8,128)S(1)} %concatenate.94), channel_id=1, source_target_pairs={{0,8},{2,10},{4,12},{6,14},{8,16},{10,18},{12,20},{14,22},{16,24},... | collective-permute-start | bytes 1769480 | tf_op jit(solution)/shard_map/ppermute | solution.py:12
  246.2 18.1 %collective-permute-start.8 = (f32[128,1152]{1,0:T(8,128)S(1)}, f32[128,1152]{1,0:T(8,128)S(1)}, u32[]{:S(2)}, u32[]{:S(2)}) collective-permute-start(f32[128,1152]{1,0:T(8,128)S(1)} %concatenate.87), channel_id=1, source_target_pairs={{8,0},{10,2},{12,4},{14,6},{16,8},{18,10},{20,12},{22,14},{24,16},... | collective-permute-start | bytes 1769480 | tf_op jit(solution)/shard_map/ppermute | solution.py:12
  247.6 18.1 %collective-permute-start.14 = (f32[128,1152]{1,0:T(8,128)S(1)}, f32[128,1152]{1,0:T(8,128)S(1)}, u32[]{:S(2)}, u32[]{:S(2)}) collective-permute-start(f32[128,1152]{1,0:T(8,128)S(1)} %concatenate.93), channel_id=1, source_target_pairs={{0,6},{2,8},{4,10},{6,12},{8,14},{10,16},{12,18},{14,20},{16,22},{... | collective-permute-start | bytes 1769480 | tf_op jit(solution)/shard_map/ppermute | solution.py:12
  250.0 17.0 %collective-permute-start.9 = (f32[128,1152]{1,0:T(8,128)S(1)}, f32[128,1152]{1,0:T(8,128)S(1)}, u32[]{:S(2)}, u32[]{:S(2)}) collective-permute-start(f32[128,1152]{1,0:T(8,128)S(1)} %concatenate.88), channel_id=1, source_target_pairs={{6,0},{8,2},{10,4},{12,6},{14,8},{16,10},{18,12},{20,14},{22,16},{... | collective-permute-start | bytes 1769480 | tf_op jit(solution)/shard_map/ppermute | solution.py:12
  251.5 43.2 %collective-permute-start.13 = (f32[128,1152]{1,0:T(8,128)S(1)}, f32[128,1152]{1,0:T(8,128)S(1)}, u32[]{:S(2)}, u32[]{:S(2)}) collective-permute-start(f32[128,1152]{1,0:T(8,128)S(1)} %concatenate.92), channel_id=1, source_target_pairs={{0,4},{2,6},{4,8},{6,10},{8,12},{10,14},{12,16},{14,18},{16,20},{1... | collective-permute-start | bytes 1769480 | tf_op jit(solution)/shard_map/ppermute | solution.py:12
  259.9 34.8 %collective-permute-start.10 = (f32[128,1152]{1,0:T(8,128)S(1)}, f32[128,1152]{1,0:T(8,128)S(1)}, u32[]{:S(2)}, u32[]{:S(2)}) collective-permute-start(f32[128,1152]{1,0:T(8,128)S(1)} %concatenate.89), channel_id=1, source_target_pairs={{4,0},{6,2},{8,4},{10,6},{12,8},{14,10},{16,12},{18,14},{20,16},{2... | collective-permute-start | bytes 1769480 | tf_op jit(solution)/shard_map/ppermute | solution.py:12
  264.3 30.4 %collective-permute-start.12 = (f32[128,1152]{1,0:T(8,128)S(1)}, f32[128,1152]{1,0:T(8,128)S(1)}, u32[]{:S(2)}, u32[]{:S(2)}) collective-permute-start(f32[128,1152]{1,0:T(8,128)S(1)} %concatenate.91), channel_id=1, source_target_pairs={{0,2},{2,4},{4,6},{6,8},{8,10},{10,12},{12,14},{14,16},{16,18},{18... | collective-permute-start | bytes 1769480 | tf_op jit(solution)/shard_map/ppermute | solution.py:12
  265.6 29.0 %collective-permute-start.11 = (f32[128,1152]{1,0:T(8,128)S(1)}, f32[128,1152]{1,0:T(8,128)S(1)}, u32[]{:S(2)}, u32[]{:S(2)}) collective-permute-start(f32[128,1152]{1,0:T(8,128)S(1)} %concatenate.90), channel_id=1, source_target_pairs={{2,0},{4,2},{6,4},{8,6},{10,8},{12,10},{14,12},{16,14},{18,16},{20... | collective-permute-start | bytes 1769480 | tf_op jit(solution)/shard_map/ppermute | solution.py:12
  311.5 51.1 %copy-start.1 = (bf16[16,32]{1,0:T(8,128)(2,1)S(1)}, bf16[16,32]{1,0:T(8,128)(2,1)}, u32[]{:S(2)}) copy-start(bf16[16,32]{1,0:T(8,128)(2,1)} %param.9) | copy-start | bytes 3076
Sparse Core Ops, SparseCore 0:
  84.5 122.4 all-gather.1
  295.9 25.7 reduce-scatter.1
where the time goes:
time: 370 us; the launch traced here: 369 us
  waiting for transfers between devices  174 us (47%)
  starting transfers between devices  58 us (16%)
  matrix products  44.4 us (12%)
  blocking collectives  40.9 us (11%)
  local copies, waits for them, and re-layouts  25.8 us (7%)
  between operations  14.7 us (4%)
  other arithmetic  11.1 us (3%)
    all_gather x1, waiting for transfers between devices, body(): piece = lax.all_gather(partner, 'aux', axis=0, tiled=True)  122 us
    ppermute x16, starting transfers between devices, passed_along(): return lax.ppermute(block, axis, route)  57.8 us
    ppermute x16, waiting for transfers between devices, passed_along(): return lax.ppermute(block, axis, route)  52.1 us
    psum x1, blocking collectives, body(): lax.psum(polar_part, 'chain')  40.9 us
    unnamed x24, local copies, waits for them, and re-layouts  13.9 us
    dot_general x1, matrix products, body(): jnp.dot(screened, stack_occ, preferred_element_type=jnp.float32)  10.4 us
    dot_general x1, matrix products, body(): lax.dot_general(screened, response, (((0,), (0,)), ((), ())), preferred_e...  10.3 us
    dot_general x1, matrix products, body(): jnp.dot(screened, stack_vir, preferred_element_type=jnp.float32)  8.63 us
  transfers between devices with their start and end apart: 18, of which 7 were waited for; matrix products, arithmetic and copies ran while one was open for 8% of the time, Pallas kernels for 0%

commit v1 on v0

v1 whole, which is shorter than its diff:
```python
import functools
import math

import jax
import jax.numpy as jnp
from jax import lax
from jax.experimental import pallas as pl
from jax.experimental.pallas import tpu as pltpu
from jax.sharding import PartitionSpec as P


F32 = jnp.float32
BF16 = jnp.bfloat16
SUB = 8
CHUNKS = 4
SPREAD = 4
SLOTS = 9
VMEM = pl.BlockSpec(memory_space=pltpu.VMEM)
SMEM = pl.BlockSpec(memory_space=pltpu.SMEM)
FIRST_COLUMN = {2: 0, -2: 1, 4: 0, -4: 3, 1: 0, 3: 0, -1: 1, -3: 1}
ODD = (-3, -1, 1, 3)


def columns_to(offset):
    return 6 if abs(offset) == 4 else 8


def passed_along(block, axis, distance):
    devices = range(lax.axis_size(axis))
    route = [(i - distance, i) for i in devices if i - distance in devices]
    return lax.ppermute(block, axis, route)


def swapped(block, axis, bit=1):
    return lax.ppermute(block, axis, [(i, i ^ bit) for i in range(lax.axis_size(axis))])


def permitted(prof_ref, nblocks, a, b):
    last = nblocks - 1
    inside = (a >= 0) & (a <= last) & (b >= 0) & (b <= last)
    wide_a = prof_ref[jnp.clip(a, 0, last)]
    wide_b = prof_ref[jnp.clip(b, 0, last)]
    return inside & (jnp.abs(a - b) <= jnp.minimum(wide_a, wide_b))


def run(kernel, operands, outs, flops=0, scratch=(), smem=0, grant=24):
    nbytes = sum(math.prod(s.shape) * s.dtype.itemsize for s in (*operands, *outs))
    return pl.pallas_call(
        kernel,
        out_shape=outs,
        in_specs=[SMEM] * smem + [VMEM] * (len(operands) - smem),
        out_specs=[VMEM] * len(outs),
        scratch_shapes=list(scratch),
        compiler_params=pltpu.CompilerParams(vmem_limit_bytes=grant * 1024 * 1024),
        cost_estimate=pl.CostEstimate(
            flops=int(flops), bytes_accessed=int(nbytes), transcendentals=0
        ),
    )(*operands)


def shaped(shape, dtype=BF16):
    return jax.ShapeDtypeStruct(shape, dtype)


def dot(a, b):
    return jnp.dot(a, b, preferred_element_type=F32)


def dot_rows(a, b):
    return lax.dot_general(a, b, (((0,), (0,)), ((), ())), preferred_element_type=F32)


def dot_columns(a, b):
    return lax.dot_general(a, b, (((1,), (1,)), ((), ())), preferred_element_type=F32)


def prepare_kernel(nblocks, at_ref, atom_ref, k_ref, keep_ref, send_ref):
    here, every = k_ref.shape
    position, half = at_ref[0], at_ref[1]
    rows = lax.broadcasted_iota(jnp.int32, (here, every), 0)
    alive = jnp.zeros((here, every), F32)
    for p in range(here):
        near = jnp.abs(atom_ref[p] - position) <= nblocks // 4
        alive = jnp.where((rows == p) & near, 1.0, alive)
    plain = k_ref[...].astype(F32) * alive
    turned = jnp.concatenate([plain[:, here:], plain[:, :here]], 1)
    keep_ref[:, :every] = jnp.where(half == 0, plain, turned)
    keep_ref[:, every:] = alive
    send_ref[:, :every] = jnp.where(half == 0, turned, plain)
    send_ref[:, every:] = alive


def screen_row(mine_ref, theirs_ref):
    every = mine_ref.shape[1] // 2
    alive = jnp.concatenate([mine_ref[:, every:], theirs_ref[:, every:]], 0)
    r = lax.broadcasted_iota(jnp.int32, (every, every), 0)
    c = lax.broadcasted_iota(jnp.int32, (every, every), 1)
    return jnp.sum(jnp.where(r == c, alive, 0.0), 0, keepdims=True), alive


def one_hot(rows, cols):
    r = lax.broadcasted_iota(jnp.int32, (rows, cols), 0)
    c = lax.broadcasted_iota(jnp.int32, (rows, cols), 1)
    return (r // SUB == c).astype(F32)


def same_row(size):
    r = lax.broadcasted_iota(jnp.int32, (size, size), 0)
    c = lax.broadcasted_iota(jnp.int32, (size, size), 1)
    return lax.rem(r, SUB) == lax.rem(c, SUB)


def mixing_matrix(mine_ref, theirs_ref):
    every = mine_ref.shape[1] // 2
    size = every * SUB
    row, _ = screen_row(mine_ref, theirs_ref)
    k = jnp.concatenate([mine_ref[:, :every], theirs_ref[:, :every]], 0) * row
    pick = one_hot(size, every).astype(BF16)
    wide = dot_columns(dot(pick, k.astype(BF16)).astype(BF16), pick)
    return jnp.where(same_row(size), wide, 0.0).astype(BF16)


def band_slots(delta, which):
    sizes = {1: (7, 8), 2: (5, 6), -1: (8, 7), -2: (6, 5)}[delta]
    count = sizes[which]
    first = SLOTS - count if delta > 0 else 0
    return first, count, sizes[0] * which


def pair_kernel(at_ref, own_ref, mid_ref, out1_ref, out2_ref):
    block = own_ref.shape[0]

    def fill(sign, pair):
        for distance, out in ((1, out1_ref), (2, out2_ref)):
            for which in range(2):
                first, count, start = band_slots(sign * distance, which)
                out[:, start * block : (start + count) * block] = pair[which][
                    :, first * block : (first + count) * block
                ]

    odd = lax.rem(at_ref[0], 2) == 1

    @pl.when(jnp.logical_not(odd))
    def _():
        fill(1, (own_ref, mid_ref))

    @pl.when(odd)
    def _():
        fill(-1, (mid_ref, own_ref))


def stack_kernel(nblocks, counts, at_ref, prof_ref, *refs):
    own_ref, mid_ref, hop1_ref, hop2_ref, near1_ref, near2_ref = refs[:6]
    owns = refs[6 : 6 + counts]
    stack_ref, outs = refs[6 + counts], refs[7 + counts :]
    block = own_ref.shape[0]
    position = at_ref[0]

    def build(parity, pair, below, above):
        for offset in range(-SPREAD, SPREAD + 1):
            delta, which = divmod(parity + offset, 2)
            rows = slice((offset + SPREAD) * block, (offset + SPREAD + 1) * block)
            other = position + offset
            row_ok = permitted(prof_ref, nblocks, position, other)
            for col in range(SLOTS):
                slot = col - offset
                columns = slice(col * block, (col + 1) * block)
                if not 0 <= slot < SLOTS:
                    stack_ref[rows, columns] = jnp.zeros((block, block), BF16)
                    continue
                if delta == 0:
                    source, at = pair[which], slot
                else:
                    first, _, start = band_slots(-delta, which)
                    source = (below if delta < 0 else above)[abs(delta) - 1]
                    at = start + slot - first
                ok = row_ok & permitted(prof_ref, nblocks, other, position + col - SPREAD)
                tile = source[:, at * block : (at + 1) * block]
                stack_ref[rows, columns] = jnp.where(ok, tile, jnp.zeros_like(tile))

    odd = lax.rem(position, 2) == 1
    hops, nears = (hop1_ref, hop2_ref), (near1_ref, near2_ref)

    @pl.when(jnp.logical_not(odd))
    def _():
        build(0, (own_ref, mid_ref), hops, nears)

    @pl.when(odd)
    def _():
        build(1, (mid_ref, own_ref), nears, hops)

    for own, out in zip(owns, outs):
        out[...] = dot(own[...], stack_ref[...]).astype(BF16)


def cut_kernel(rows, picks, at_ref, three_ref, *refs):
    outs, sem = refs[:-1], refs[-1]
    copies = []
    for (mine, first), out in zip(picks, outs):
        which = at_ref[1] if mine else 1 - at_ref[1]
        for g in range(out.shape[0]):
            start = pl.multiple_of(which * rows + (first + g) * SUB, SUB)
            copies.append(
                pltpu.make_async_copy(
                    three_ref.at[:, pl.ds(start, SUB), :], out.at[g], sem.at[len(copies)]
                )
            )
    for copy in copies:
        copy.start()
    for copy in copies:
        copy.wait()


def respond(mixed, po_ref, pr_ref, ro_ref, rr_ref):
    half = mixed.shape[0] // 2
    for g in range(po_ref.shape[0] // half):
        rows = slice(g * half, (g + 1) * half)
        partner = jnp.concatenate([po_ref[rows, :], pr_ref[rows, :]], 0)
        resp = dot(mixed, partner).astype(BF16)
        ro_ref[rows, :] = resp[:half]
        rr_ref[rows, :] = resp[half:]


def respond_kernel(mine_ref, theirs_ref, v_ref, s_ref, po_ref, pr_ref, ro_ref, rr_ref):
    pr_ref[...] = dot(s_ref[...], v_ref[...]).astype(BF16)
    respond(mixing_matrix(mine_ref, theirs_ref), po_ref, pr_ref, ro_ref, rr_ref)


def early_kernel(count, *refs):
    out_ref = refs[2 * count]
    for c in range(0, out_ref.shape[1], 384):
        columns = slice(c, c + 384)
        acc = None
        for s_ref, r_ref in zip(refs[:count], refs[count : 2 * count]):
            part = dot_rows(s_ref[...], r_ref[:, columns])
            acc = part if acc is None else acc + part
        out_ref[:, columns] = acc


def terms_of(offsets, early_ref, so_ref, sr_ref, ro_ref, rr_ref, block):
    take = [slice((d + SPREAD) * block, (d + SPREAD + 1) * block) for d in offsets]
    own = jnp.concatenate([so_ref[:, t] for t in take], 1)
    got = jnp.concatenate([sr_ref[:, t] for t in take], 1)
    total = dot_rows(own, ro_ref[...]) + dot_rows(got, rr_ref[...])
    return [total[n * block : (n + 1) * block] + early_ref[t, :] for n, t in enumerate(take)]


def placed_terms(ok, term, offset, first, count, block, dtype):
    tiles = []
    for c in range(first, first + count):
        source = c + offset
        if 0 <= source < SLOTS:
            tile = term[:, source * block : (source + 1) * block]
            tiles.append(jnp.where(ok, tile, jnp.zeros_like(tile)).astype(dtype))
        else:
            tiles.append(jnp.zeros((block, block), dtype))
    return tiles


def odd_kernel(
    nblocks, at_ref, prof_ref, mine_ref, theirs_ref, v_ref, s_ref, po_ref, so_ref, early_ref,
    pr_ref, ro_ref, rr_ref, pack_ref,
):
    respond_kernel(mine_ref, theirs_ref, v_ref, s_ref, po_ref, pr_ref, ro_ref, rr_ref)
    block = pack_ref.shape[1]
    position = at_ref[0]
    terms = terms_of(ODD, early_ref, so_ref, s_ref, ro_ref, rr_ref, block)
    for n, (offset, term) in enumerate(zip(ODD, terms)):
        ok = permitted(prof_ref, nblocks, position, position + offset)
        tiles = placed_terms(ok, term, offset, FIRST_COLUMN[offset], 8, block, BF16)
        for c, tile in enumerate(tiles):
            pack_ref[n, :, c * block : (c + 1) * block] = tile


def even_kernel(
    nblocks, at_ref, prof_ref, so_ref, s_ref, ro_ref, rr_ref, early_ref, own_ref, *out_refs
):
    block = own_ref.shape[0]
    position = at_ref[0]
    offsets = (0, 2, -2, 4, -4)
    terms = terms_of(offsets, early_ref, so_ref, s_ref, ro_ref, rr_ref, block)
    own_ref[...] = terms[0]
    for offset, term, out in zip(offsets[1:], terms[1:], out_refs):
        ok = permitted(prof_ref, nblocks, position, position + offset)
        first, count = FIRST_COLUMN[offset], columns_to(offset)
        for c, tile in enumerate(placed_terms(ok, term, offset, first, count, block, F32)):
            out[:, c * block : (c + 1) * block] = tile


def combine_kernel(at_ref, pack_ref, own_ref, u2_ref, d2_ref, u4_ref, d4_ref, *outs):
    block = own_ref.shape[0]
    ins = {0: own_ref, 2: u2_ref, -2: d2_ref, 4: u4_ref, -4: d4_ref}
    to = dict(zip((0, 2, -2, 4, -4), outs))
    odd = lax.rem(at_ref[0], 2) == 1

    def merge(sources):
        for offset, out in to.items():
            first = 0 if offset == 0 else FIRST_COLUMN[offset]
            for c in range(out.shape[1] // block):
                columns = slice(c * block, (c + 1) * block)
                value = ins[offset][:, columns]
                if offset in sources:
                    n = sources[offset]
                    at = c + first - FIRST_COLUMN[ODD[n]]
                    if 0 <= at < 8:
                        tile = pack_ref[n, :, at * block : (at + 1) * block]
                        value = value + tile.astype(F32)
                out[:, columns] = value.astype(out.dtype)

    @pl.when(jnp.logical_not(odd))
    def _():
        merge({-2: 0, 0: 1, 2: 2, 4: 3})

    @pl.when(odd)
    def _():
        merge({-4: 0, -2: 1, 0: 2, 2: 3})


def gather_kernel(at_ref, own_ref, u2_ref, d2_ref, u4_ref, d4_ref, keep_ref, send_ref):
    block = own_ref.shape[0]
    rows = keep_ref.shape[0]
    half = at_ref[1]
    parts = {2: u2_ref, -2: d2_ref, 4: u4_ref, -4: d4_ref}
    for target, which in ((send_ref, 1 - half), (keep_ref, half)):
        window = pl.ds(pl.multiple_of(which * rows, rows), rows)
        for c in range(SLOTS):
            columns = slice(c * block, (c + 1) * block)
            total = own_ref[window, columns]
            for offset, part in parts.items():
                at = c - FIRST_COLUMN[offset]
                if 0 <= at < columns_to(offset):
                    total = total + part[window, at * block : (at + 1) * block].astype(F32)
            target[:, columns] = total.astype(target.dtype)


def finish_kernel(nblocks, block, scale, at_ref, prof_ref, keep_ref, got_ref, out_ref):
    position = at_ref[0]
    for c in range(SLOTS):
        columns = slice(c * block, (c + 1) * block)
        ok = permitted(prof_ref, nblocks, position, position + c - SPREAD)
        value = (keep_ref[:, columns] + got_ref[:, columns].astype(F32)) * scale
        out_ref[:, columns] = jnp.where(ok, value, jnp.zeros_like(value))


def gram_of(size, x_ref, quads, total):
    half = size // 2
    for s_ref, co_ref, po_ref, pr_ref in quads:
        got = dot(s_ref[...], x_ref[...]).astype(BF16)
        for g in range(s_ref.shape[0] // half):
            rows = slice(g * half, (g + 1) * half)
            coupled = jnp.concatenate([co_ref[rows, :], got[rows]], 0)
            partner = jnp.concatenate([po_ref[rows, :], pr_ref[rows, :]], 0)
            part = dot_columns(coupled, partner)
            total = part if total is None else total + part
    return total


def gram_kernel(count, x_ref, *refs):
    quads = [refs[4 * c : 4 * c + 4] for c in range(count)]
    out_ref = refs[4 * count]
    out_ref[...] = gram_of(out_ref.shape[0], x_ref, quads, None)


def polar_kernel(at_ref, x_ref, s_ref, co_ref, po_ref, pr_ref, gram_ref, mine_ref, theirs_ref, keep_ref, send_ref):
    size = gram_ref.shape[0]
    here, every = keep_ref.shape
    total = gram_of(size, x_ref, [(s_ref, co_ref, po_ref, pr_ref)], gram_ref[...])
    by_row = jnp.sum(jnp.where(same_row(size), total, 0.0).reshape(every, SUB, size), 1)
    polar = jnp.dot(
        by_row, one_hot(size, every), preferred_element_type=F32, precision=lax.Precision.HIGHEST
    )
    row, alive = screen_row(mine_ref, theirs_ref)
    polar = polar * row * alive
    turned = jnp.concatenate([polar[:, here:], polar[:, :here]], 1)
    polar = jnp.where(at_ref[1] == 0, polar, turned)
    keep_ref[...] = polar[:here]
    send_ref[...] = polar[here:]


def step(occupied, virtual, three_centre, kernel, profile, atom_map):
    block, width = occupied.shape
    nblocks = lax.axis_size("chain")
    halves = lax.axis_size("aux")
    if halves != 2 or width != SLOTS * block or nblocks % 2:
        raise ValueError("unsupported mesh")
    position = lax.axis_index("chain")
    half = lax.axis_index("aux")
    here = three_centre.shape[0]
    every = kernel.shape[1]
    rows = block // halves
    groups = rows // SUB
    per_group = here * SUB
    per_chunk = groups // CHUNKS
    span = per_chunk * per_group
    at = jnp.stack([position, half]).astype(jnp.int32)

    def cut(picks, grant=24):
        shape = (per_chunk, here, SUB, width)
        call = pl.pallas_call(
            functools.partial(cut_kernel, rows, picks),
            out_shape=[shaped(shape)] * len(picks),
            in_specs=[SMEM, pl.BlockSpec(memory_space=pltpu.HBM)],
            out_specs=[VMEM] * len(picks),
            scratch_shapes=[pltpu.SemaphoreType.DMA((len(picks) * per_chunk,))],
            compiler_params=pltpu.CompilerParams(vmem_limit_bytes=grant * 1024 * 1024),
            cost_estimate=pl.CostEstimate(
                flops=0, bytes_accessed=4 * len(picks) * span * width, transcendentals=0
            ),
        )
        return [part.reshape(span, width) for part in call(at, three_centre)]

    def halo(band):
        mid = swapped(band, "chain")
        packs = run(
            pair_kernel,
            [at, band, mid],
            [shaped((block, 15 * block)), shaped((block, 11 * block))],
            smem=1,
        )
        hops = []
        for distance, pack in zip((2, 4), packs):
            up = [(i, i + distance) for i in range(0, nblocks - distance, 2)]
            down = [(i + distance, i) for i in range(1, nblocks - distance, 2)]
            hops.append(lax.ppermute(pack, "chain", up + down))
        return [band, mid, *hops, *[swapped(h, "chain") for h in hops]]

    starts = [c * per_chunk for c in range(CHUNKS)]
    sends = cut([(False, starts[0])])
    rest = cut([(False, f) for f in starts[1:]] + [(True, f) for f in starts])
    sends += rest[: CHUNKS - 1]
    own = rest[CHUNKS - 1 :]
    got = [swapped(part, "aux") for part in sends]
    near_vir = halo(virtual)
    near_occ = halo(occupied)

    mine, send = run(
        functools.partial(prepare_kernel, nblocks),
        [at, atom_map, kernel],
        [shaped((here, 2 * every), F32)] * 2,
        smem=2,
    )
    theirs = swapped(send, "aux")

    product = 2 * span * width * width
    vir_stack, *partner_own = run(
        functools.partial(stack_kernel, nblocks, CHUNKS),
        [at, profile, *near_vir, *own],
        [shaped((width, width))] + [shaped((span, width))] * CHUNKS,
        flops=CHUNKS * product,
        smem=2,
    )
    partner_got, resp_own, resp_got = [], [], []
    for c in range(CHUNKS - 1):
        pr, ro, rr = run(
            respond_kernel,
            [mine, theirs, vir_stack, got[c], partner_own[c]],
            [shaped((span, width))] * 3,
            flops=2 * product,
        )
        partner_got.append(pr)
        resp_own.append(ro)
        resp_got.append(rr)
    (early,) = run(
        functools.partial(early_kernel, 2 * (CHUNKS - 1)),
        [*own[:-1], *got[:-1], *resp_own, *resp_got],
        [shaped((width, width), F32)],
        flops=2 * (CHUNKS - 1) * product,
    )
    pr, ro, rr, pack = run(
        functools.partial(odd_kernel, nblocks),
        [at, profile, mine, theirs, vir_stack, got[-1], partner_own[-1], own[-1], early],
        [shaped((span, width))] * 3 + [shaped((len(ODD), block, 8 * block))],
        flops=2 * product,
        smem=2,
    )
    partner_got.append(pr)
    other_pack = swapped(pack, "chain")
    offsets = (2, -2, 4, -4)
    even = run(
        functools.partial(even_kernel, nblocks),
        [at, profile, own[-1], got[-1], ro, rr, early],
        [shaped((block, width), F32)]
        + [shaped((block, columns_to(d) * block), F32) for d in offsets],
        flops=product,
        smem=2,
    )
    mid, *sends = run(
        combine_kernel,
        [at, other_pack, *even],
        [shaped((block, width), F32)] + [shaped((block, columns_to(d) * block)) for d in offsets],
        smem=1,
    )
    arrived = [passed_along(s, "chain", d) for s, d in zip(sends, offsets)]
    keep, send = run(
        gather_kernel,
        [at, mid, *arrived],
        [shaped((rows, width), F32), shaped((rows, width))],
        smem=1,
    )
    (band_gradient,) = run(
        functools.partial(finish_kernel, nblocks, block, 1.0 / math.sqrt(block * every)),
        [at, profile, keep, swapped(send, "aux")],
        [shaped((rows, width), F32)],
        smem=2,
    )

    occ_stack, *coupled_own = run(
        functools.partial(stack_kernel, nblocks, CHUNKS),
        [at, profile, *near_occ, *own],
        [shaped((width, width))] + [shaped((span, width))] * CHUNKS,
        flops=CHUNKS * product,
        smem=2,
    )
    size = every * SUB
    quads = [q for c in range(CHUNKS - 1) for q in (got[c], coupled_own[c], partner_own[c], partner_got[c])]
    (gram,) = run(
        functools.partial(gram_kernel, CHUNKS - 1),
        [occ_stack, *quads],
        [shaped((size, size), F32)],
        flops=CHUNKS * product,
    )
    polar, send = run(
        polar_kernel,
        [at, occ_stack, got[-1], coupled_own[-1], partner_own[-1], partner_got[-1], gram, mine, theirs],
        [shaped((here, every), F32)] * 2,
        flops=2 * product,
        smem=1,
    )
    polar = polar + swapped(send, "aux")
    bit = 1
    while bit < nblocks:
        polar = polar + swapped(polar, "chain", bit)
        bit *= 2
    polarization = polar * (1.0 / math.sqrt(block * nblocks * width))
    return (band_gradient, polarization)


def solution(mesh):
    placed = (
        P("chain", None),
        P("chain", None),
        P("aux", "chain", None),
        P("aux", None),
        P(),
        P("aux"),
    )
    return jax.shard_map(
        step,
        mesh=mesh,
        in_specs=placed,
        out_specs=(P(("chain", "aux"), None), P("aux", None)),
        check_vma=False,
    )
```

time: 370 us -> 143 us (0.39)
  waiting for transfers between devices: 174 us -> 52.8 us
  matrix products: 44.4 us -> 0 us
  blocking collectives: 40.9 us -> 0 us
  Pallas kernels: 0 us -> 37.9 us
  local copies, waits for them, and re-layouts: 25.8 us -> 3.32 us
  between operations: 14.7 us -> 0.94 us
  starting transfers between devices: 58 us -> 46.6 us
  other arithmetic: 11.1 us -> 0.69 us
    all_gather x1 -> x0, waiting for transfers between devices: 122 us -> none  [body(): piece = lax.all_gather(partner, 'aux', axis=0, tiled=True)]
    ppermute x0 -> x22, waiting for transfers between devices: none -> 52.8 us  [the longest x18 39.9 us: swapped(): lax.ppermute(block, axis, [(i, i ^ bit) for i in range(lax.axis_size(axis...]
    ppermute x16 -> x4, waiting for transfers between devices: 52.1 us -> 0.01 us  [passed_along(): return lax.ppermute(block, axis, route)]
    ppermute x16 -> x4, starting transfers between devices: 57.8 us -> 9.23 us  [passed_along(): return lax.ppermute(block, axis, route)]
    dot_general x5 -> x0, matrix products: 44.4 us -> none  [the longest x1 10.4 us: body(): jnp.dot(screened, stack_occ, preferred_element_type=jnp.float32)]
    psum x1 -> x0, blocking collectives: 40.9 us -> none  [body(): lax.psum(polar_part, 'chain')]
    pallas_call x0 -> x18, Pallas kernels: none -> 37.9 us  [the longest x16 36.2 us: run(): pl.pallas_call(kernel, out_shape=outs, in_specs=[SMEM] * smem + [VMEM] *...]
    ppermute x0 -> x22, starting transfers between devices: none -> 37.3 us  [the longest x18 21 us: swapped(): lax.ppermute(block, axis, [(i, i ^ bit) for i in range(lax.axis_size(axis...]
  transfers between devices with their start and end apart: 18 -> 26, of which waited for: 7 -> 9; matrix products, arithmetic and copies ran while one was open for 8% -> 0% of each run, Pallas kernels for 0% -> 25%
where the time goes in v1:
time: 143 us; the launch traced here: 142 us
  waiting for transfers between devices  52.8 us (37%)
  starting transfers between devices  46.6 us (33%)
  Pallas kernels  37.9 us (27%)
  local copies, waits for them, and re-layouts  3.32 us (2%)
    ppermute x18, waiting for transfers between devices, swapped(): lax.ppermute(block, axis, [(i, i ^ bit) for i in range(lax.axis_size(axis...  39.9 us
    pallas_call x16, Pallas kernels, run(): pl.pallas_call(kernel, out_shape=outs, in_specs=[SMEM] * smem + [VMEM] *...  36.2 us
    ppermute x18, starting transfers between devices, swapped(): lax.ppermute(block, axis, [(i, i ^ bit) for i in range(lax.axis_size(axis...  21 us
    ppermute x4, starting transfers between devices, halo(): hops.append(lax.ppermute(pack, 'chain', up + down))  16.4 us
    ppermute x4, waiting for transfers between devices, halo(): hops.append(lax.ppermute(pack, 'chain', up + down))  12.9 us
    ppermute x4, starting transfers between devices, passed_along(): return lax.ppermute(block, axis, route)  9.23 us
    unnamed x14, local copies, waits for them, and re-layouts  3.32 us
  transfers between devices with their start and end apart: 26, of which 9 were waited for; matrix products, arithmetic and copies ran while one was open for 0% of the time, Pallas kernels for 25%

profile of v1, /device:TPU:0, one launch (start us, length us, event | category | flops | bytes accessed | tf_op | source)
XLA Modules:
  0.0 142.2 jit_solution(11058180551597794082)
XLA Ops:
  0.6 0.6 collective-permute-start.1
  1.2 0.1 pad_add_fusion.at_ref
  1.3 1.3 collective-permute-done.1.mid_ref.refs_1_
  2.6 1.0 copy-done.1
  3.6 0.6 shard_map.78
  4.2 4.8 %collective-permute-start.2 = (bf16[128,1920]{1,0:T(8,128)(2,1)S(1)}, bf16[128,1920]{1,0:T(8,128)(2,1)S(1)}, u32[]{:S(2)}, u32[]{:S(2)}) collective-permute-start(bf16[128,1920]{1,0:T(8,128)(2,1)S(1)} %get-tuple-element.54), channel_id=1, source_target_pairs={{0,4},{4,8},{8,12},{12,16},{16,20},{20,24},{24,28},{6,2},{10,6},{1... | collective-permute-start | bytes 1474568 | tf_op jit(solution)/shard_map/ppermute | solution.py:424
  9.0 0.0 copy-start.6
  9.0 0.0 copy-start.4
  9.0 3.5 %collective-permute-start.3 = (bf16[128,1408]{1,0:T(8,128)(2,1)S(1)}, bf16[128,1408]{1,0:T(8,128)(2,1)S(1)}, u32[]{:S(2)}, u32[]{:S(2)}) collective-permute-start(bf16[128,1408]{1,0:T(8,128)(2,1)S(1)} %get-tuple-element.55), channel_id=1, source_target_pairs={{0,8},{4,12},{8,16},{12,20},{16,24},{20,28},{10,2},{14,6},{18,10},... | collective-permute-start | bytes 1081352 | tf_op jit(solution)/shard_map/ppermute | solution.py:424
  12.5 8.1 %collective-permute-done.2.refs_2_ = bf16[128,1920]{1,0:T(8,128)(2,1)S(1)} collective-permute-done((bf16[128,1920]{1,0:T(8,128)(2,1)S(1)}, bf16[128,1920]{1,0:T(8,128)(2,1)S(1)}, u32[]{:S(2)}, u32[]{:S(2)}) %collective-permute-start.2) | collective-permute-done | bytes 491552 | tf_op jit(solution)/shard_map/ppermute | solution.py:424
  20.6 0.0 collective-permute-start.4
  20.6 0.5 collective-permute-start.16
  21.1 0.0 collective-permute-done.3.refs_3_
  21.1 0.0 collective-permute-start.5
  21.1 2.3 %copy-done = bf16[16,128,1152]{2,1,0:T(8,128)(2,1)S(1)} copy-done((bf16[16,128,1152]{2,1,0:T(8,128)(2,1)S(1)}, bf16[16,128,1152]{2,1,0:T(8,128)(2,1)}, u32[]{:S(2)}) %copy-start) | copy-done | bytes 4718616
  23.4 0.6 shard_map.81
  24.1 1.6 %collective-permute-start.7 = (bf16[256,1152]{1,0:T(8,128)(2,1)S(1)}, bf16[256,1152]{1,0:T(8,128)(2,1)S(1)}, u32[]{:S(2)}, u32[]{:S(2)}) collective-permute-start(bf16[256,1152]{1,0:T(8,128)(2,1)S(1)} %bitcast.14), channel_id=1, source_target_pairs={{0,1},{1,0},{2,3},{3,2},{4,5},{5,4},{6,7},{7,6},{8,9},{9,8},{10,11... | collective-permute-start | bytes 1769480 | tf_op jit(solution)/shard_map/ppermute | solution.py:35
  25.6 1.1 shard_map.79
  26.7 0.6 collective-permute-start.8
  27.3 1.5 %collective-permute-start.9 = (bf16[256,1152]{1,0:T(8,128)(2,1)S(1)}, bf16[256,1152]{1,0:T(8,128)(2,1)S(1)}, u32[]{:S(2)}, u32[]{:S(2)}) collective-permute-start(bf16[256,1152]{1,0:T(8,128)(2,1)S(1)} %bitcast.25), channel_id=1, source_target_pairs={{0,1},{1,0},{2,3},{3,2},{4,5},{5,4},{6,7},{7,6},{8,9},{9,8},{10,11... | collective-permute-start | bytes 1769480 | tf_op jit(solution)/shard_map/ppermute | solution.py:35
  28.8 0.7 shard_map.77
  29.5 0.6 shard_map.91
  30.1 0.0 collective-permute-done.5.refs_5_
  30.1 0.6 collective-permute-start
  30.7 1.5 %collective-permute-start.6 = (bf16[256,1152]{1,0:T(8,128)(2,1)S(1)}, bf16[256,1152]{1,0:T(8,128)(2,1)S(1)}, u32[]{:S(2)}, u32[]{:S(2)}) collective-permute-start(bf16[256,1152]{1,0:T(8,128)(2,1)S(1)} %bitcast.24), channel_id=1, source_target_pairs={{0,1},{1,0},{2,3},{3,2},{4,5},{5,4},{6,7},{7,6},{8,9},{9,8},{10,11... | collective-permute-start | bytes 1769480 | tf_op jit(solution)/shard_map/ppermute | solution.py:35
  32.2 4.7 %shard_map.80 = (bf16[1152,1152]{1,0:T(8,128)(2,1)S(1)}, bf16[256,1152]{1,0:T(8,128)(2,1)S(1)}, bf16[256,1152]{1,0:T(8,128)(2,1)S(1)}, bf16[256,1152]{1,0:T(8,128)(2,1)S(1)}, bf16[256,1152]{1,0:T(8,128)(2,1)S(1)}) custom-call(s32[2]{0:T(128)S(1)} %pad_add_fusion.at_ref, s32[16]{0:T(128)S(1)} %copy-done.4, bf16[128,1152]{1,0:T(8,128)(2,1)S(1)} %copy-done.2, ...), custom_call_target="tpu_custom_call" | custom-call | flops 2717908992 | bytes 9666632 | tf_op jit(solution)/shard_map/pallas_call | solution.py:48
  36.9 28.9 %collective-permute-done.theirs_ref = f32[16,64]{1,0:T(8,128)S(1)} collective-permute-done((f32[16,64]{1,0:T(8,128)S(1)}, f32[16,64]{1,0:T(8,128)S(1)}, u32[]{:S(2)}, u32[]{:S(2)}) %collective-permute-start) | collective-permute-done | bytes 4128 | tf_op jit(solution)/shard_map/ppermute | solution.py:35
  65.8 4.6 %collective-permute-start.17 = (bf16[128,1920]{1,0:T(8,128)(2,1)S(1)}, bf16[128,1920]{1,0:T(8,128)(2,1)S(1)}, u32[]{:S(2)}, u32[]{:S(2)}) collective-permute-start(bf16[128,1920]{1,0:T(8,128)(2,1)S(1)} %get-tuple-element.89), channel_id=1, source_target_pairs={{0,4},{4,8},{8,12},{12,16},{16,20},{20,24},{24,28},{6,2},{10,6},{1... | collective-permute-start | bytes 1474568 | tf_op jit(solution)/shard_map/ppermute | solution.py:424
  70.4 0.0 collective-permute-done.7.s_ref.refs_3_.refs_0_
  70.4 1.6 %shard_map.82 = (bf16[256,1152]{1,0:T(8,128)(2,1)S(1)}, bf16[256,1152]{1,0:T(8,128)(2,1)S(1)}, bf16[256,1152]{1,0:T(8,128)(2,1)S(1)}) custom-call(f32[16,64]{1,0:T(8,128)S(1)} %get-tuple-element.52.mine_ref, f32[16,64]{1,0:T(8,128)S(1)} %collective-permute-done.theirs_ref, bf16[1152,1152]{1,0:T(8,128)(2,1)S(1)} %get-tuple-element.60.v_ref, ...), custom_call_target="tpu_custom_call" | custom-call | flops 1358954496 | bytes 5611520 | tf_op jit(solution)/shard_map/pallas_call | solution.py:48
  72.0 0.0 collective-permute-done.8.s_ref.refs_4_
  72.0 1.6 %shard_map.83 = (bf16[256,1152]{1,0:T(8,128)(2,1)S(1)}, bf16[256,1152]{1,0:T(8,128)(2,1)S(1)}, bf16[256,1152]{1,0:T(8,128)(2,1)S(1)}) custom-call(f32[16,64]{1,0:T(8,128)S(1)} %get-tuple-element.52.mine_ref, f32[16,64]{1,0:T(8,128)S(1)} %collective-permute-done.theirs_ref, bf16[1152,1152]{1,0:T(8,128)(2,1)S(1)} %get-tuple-element.60.v_ref, ...), custom_call_target="tpu_custom_call" | custom-call | flops 1358954496 | bytes 5611520 | tf_op jit(solution)/shard_map/pallas_call | solution.py:48
  73.7 0.0 collective-permute-done.9.s_ref.refs_5_.refs_8_
  73.7 1.6 %shard_map.84 = (bf16[256,1152]{1,0:T(8,128)(2,1)S(1)}, bf16[256,1152]{1,0:T(8,128)(2,1)S(1)}, bf16[256,1152]{1,0:T(8,128)(2,1)S(1)}) custom-call(f32[16,64]{1,0:T(8,128)S(1)} %get-tuple-element.52.mine_ref, f32[16,64]{1,0:T(8,128)S(1)} %collective-permute-done.theirs_ref, bf16[1152,1152]{1,0:T(8,128)(2,1)S(1)} %get-tuple-element.60.v_ref, ...), custom_call_target="tpu_custom_call" | custom-call | flops 1358954496 | bytes 5611520 | tf_op jit(solution)/shard_map/pallas_call | solution.py:48
  75.4 5.7 %shard_map.85.early_ref = f32[1152,1152]{1,0:T(8,128)S(1)} custom-call(bf16[256,1152]{1,0:T(8,128)(2,1)S(1)} %bitcast.16, bf16[256,1152]{1,0:T(8,128)(2,1)S(1)} %bitcast.19, bf16[256,1152]{1,0:T(8,128)(2,1)S(1)} %bitcast.22, bf16[256,1152]{1,0:T(8,128)(2,1)S(1)} %collective-permute-done.7.s_ref.refs_3_.refs_0_, ...), custom_call_target="tpu_custom_call" | custom-call | flops 4076863488 | bytes 12386304 | tf_op jit(solution)/shard_map/pallas_call | solution.py:48
  81.1 0.0 collective-permute-done.6.s_ref
  81.1 2.9 %shard_map.86 = (bf16[256,1152]{1,0:T(8,128)(2,1)S(1)}, bf16[256,1152]{1,0:T(8,128)(2,1)S(1)}, bf16[256,1152]{1,0:T(8,128)(2,1)S(1)}, bf16[4,128,1024]{2,1,0:T(8,128)(2,1)S(1)}) custom-call(s32[2]{0:T(128)S(1)} %pad_add_fusion.at_ref, s32[16]{0:T(128)S(1)} %copy-done.4, f32[16,64]{1,0:T(8,128)S(1)} %get-tuple-element.52.mine_ref, ...), custom_call_target="tpu_custom_call" | custom-call | flops 1358954496 | bytes 12558408 | tf_op jit(solution)/shard_map/pallas_call | solution.py:48
  84.0 0.1 collective-permute-start.10
  84.1 3.5 %collective-permute-start.18 = (bf16[128,1408]{1,0:T(8,128)(2,1)S(1)}, bf16[128,1408]{1,0:T(8,128)(2,1)S(1)}, u32[]{:S(2)}, u32[]{:S(2)}) collective-permute-start(bf16[128,1408]{1,0:T(8,128)(2,1)S(1)} %get-tuple-element.90), channel_id=1, source_target_pairs={{0,8},{4,12},{8,16},{12,20},{16,24},{20,28},{10,2},{14,6},{18,10},... | collective-permute-start | bytes 1081352 | tf_op jit(solution)/shard_map/ppermute | solution.py:424
  87.6 0.1 collective-permute-start.19
  87.7 4.8 %collective-permute-done.18.refs_3_ = bf16[128,1408]{1,0:T(8,128)(2,1)S(1)} collective-permute-done((bf16[128,1408]{1,0:T(8,128)(2,1)S(1)}, bf16[128,1408]{1,0:T(8,128)(2,1)S(1)}, u32[]{:S(2)}, u32[]{:S(2)}) %collective-permute-start.18) | collective-permute-done | bytes 360480 | tf_op jit(solution)/shard_map/ppermute | solution.py:424
  92.5 0.3 collective-permute-start.20
  92.8 1.6 %shard_map.87 = (f32[128,1152]{1,0:T(8,128)S(1)}, f32[128,1024]{1,0:T(8,128)S(1)}, f32[128,1024]{1,0:T(8,128)S(1)}, f32[128,768]{1,0:T(8,128)S(1)}, f32[128,768]{1,0:T(8,128)S(1)}) custom-call(s32[2]{0:T(128)S(1)} %pad_add_fusion.at_ref, s32[16]{0:T(128)S(1)} %copy-done.4, bf16[256,1152]{1,0:T(8,128)(2,1)S(1)} %bitcast.12, ...), custom_call_target="tpu_custom_call" | custom-call | flops 679477248 | bytes 10092616 | tf_op jit(solution)/shard_map/pallas_call | solution.py:48
  94.4 4.9 %shard_map.92 = (bf16[1152,1152]{1,0:T(8,128)(2,1)S(1)}, bf16[256,1152]{1,0:T(8,128)(2,1)S(1)}, bf16[256,1152]{1,0:T(8,128)(2,1)S(1)}, bf16[256,1152]{1,0:T(8,128)(2,1)S(1)}, bf16[256,1152]{1,0:T(8,128)(2,1)S(1)}) custom-call(s32[2]{0:T(128)S(1)} %pad_add_fusion.at_ref, s32[16]{0:T(128)S(1)} %copy-done.4, bf16[128,1152]{1,0:T(8,128)(2,1)S(1)} %copy-done.3, ...), custom_call_target="tpu_custom_call" | custom-call | flops 2717908992 | bytes 9666632 | tf_op jit(solution)/shard_map/pallas_call | solution.py:48
  99.3 0.8 shard_map.88
  100.1 4.2 %collective-permute-start.13 = (bf16[128,768]{1,0:T(8,128)(2,1)S(1)}, bf16[128,768]{1,0:T(8,128)(2,1)S(1)}, u32[]{:S(2)}, u32[]{:S(2)}) collective-permute-start(bf16[128,768]{1,0:T(8,128)(2,1)S(1)} %get-tuple-element.85), channel_id=1, source_target_pairs={{0,8},{2,10},{4,12},{6,14},{8,16},{10,18},{12,20},{14,22},{16,24},... | collective-permute-start | bytes 589832 | tf_op jit(solution)/shard_map/ppermute | solution.py:31
  104.3 1.3 collective-permute-start.14
  105.6 2.5 %collective-permute-start.11 = (bf16[128,1024]{1,0:T(8,128)(2,1)S(1)}, bf16[128,1024]{1,0:T(8,128)(2,1)S(1)}, u32[]{:S(2)}, u32[]{:S(2)}) collective-permute-start(bf16[128,1024]{1,0:T(8,128)(2,1)S(1)} %get-tuple-element.83), channel_id=1, source_target_pairs={{0,4},{2,6},{4,8},{6,10},{8,12},{10,14},{12,16},{14,18},{16,20},{1... | collective-permute-start | bytes 786440 | tf_op jit(solution)/shard_map/ppermute | solution.py:31
  108.1 1.3 collective-permute-start.12
  109.4 4.1 %shard_map.93.gram_ref = f32[256,256]{1,0:T(8,128)S(1)} custom-call(bf16[1152,1152]{1,0:T(8,128)(2,1)S(1)} %get-tuple-element.91.x_ref, bf16[256,1152]{1,0:T(8,128)(2,1)S(1)} %collective-permute-done.7.s_ref.refs_3_.refs_0_, bf16[256,1152]{1,0:T(8,128)(2,1)S(1)} %get-tuple-element.94.refs_1_, bf16[256,1152]{1,0:T(8,128)(2,1)S(1)} %get-tuple-element.65.po_ref.refs_2_, ...), custom_call_target="tpu_custom_call" | custom-call | flops 2717908992 | bytes 9994240 | tf_op jit(solution)/shard_map/pallas_call | solution.py:48
  113.5 2.6 %shard_map.94 = (f32[16,32]{1,0:T(8,128)S(1)}, f32[16,32]{1,0:T(8,128)S(1)}) custom-call(s32[2]{0:T(128)S(1)} %pad_add_fusion.at_ref, bf16[1152,1152]{1,0:T(8,128)(2,1)S(1)} %get-tuple-element.91.x_ref, bf16[256,1152]{1,0:T(8,128)(2,1)S(1)} %collective-permute-done.6.s_ref, bf16[256,1152]{1,0:T(8,128)(2,1)S(1)} %get-tuple-element.92.co_ref, ...), custom_call_target="tpu_custom_call" | custom-call | flops 1358954496 | bytes 5287944 | tf_op jit(solution)/shard_map/pallas_call | solution.py:48
  116.1 1.5 %collective-permute-start.21 = (f32[16,32]{1,0:T(8,128)S(1)}, f32[16,32]{1,0:T(8,128)S(1)}, u32[]{:S(2)}, u32[]{:S(2)}) collective-permute-start(f32[16,32]{1,0:T(8,128)S(1)} %get-tuple-element.101), channel_id=1, source_target_pairs={{0,1},{1,0},{2,3},{3,2},{4,5},{5,4},{6,7},{7,6},{8,9},{9,8},{10,11... | collective-permute-start | bytes 6152 | tf_op jit(solution)/shard_map/ppermute | solution.py:35
  117.7 2.2 %collective-permute-done.21 = f32[16,32]{1,0:T(8,128)S(1)} collective-permute-done((f32[16,32]{1,0:T(8,128)S(1)}, f32[16,32]{1,0:T(8,128)S(1)}, u32[]{:S(2)}, u32[]{:S(2)}) %collective-permute-start.21) | collective-permute-done | bytes 2080 | tf_op jit(solution)/shard_map/ppermute | solution.py:35
  119.8 1.2 collective-permute-done.22
  121.0 4.2 %collective-permute-start.23 = (f32[16,32]{1,0:T(8,128)S(1)}, f32[16,32]{1,0:T(8,128)S(1)}, u32[]{:S(2)}, u32[]{:S(2)}) collective-permute-start(f32[16,32]{1,0:T(8,128)S(1)} %add.16), channel_id=1, source_target_pairs={{0,4},{2,6},{4,0},{6,2},{8,12},{10,14},{12,8},{14,10},{16,20},{18,... | collective-permute-start | bytes 6152 | tf_op jit(solution)/shard_map/ppermute | solution.py:35
  125.2 1.6 %collective-permute-done.23 = f32[16,32]{1,0:T(8,128)S(1)} collective-permute-done((f32[16,32]{1,0:T(8,128)S(1)}, f32[16,32]{1,0:T(8,128)S(1)}, u32[]{:S(2)}, u32[]{:S(2)}) %collective-permute-start.23) | collective-permute-done | bytes 2080 | tf_op jit(solution)/shard_map/ppermute | solution.py:35
  126.8 3.5 %collective-permute-start.24 = (f32[16,32]{1,0:T(8,128)S(1)}, f32[16,32]{1,0:T(8,128)S(1)}, u32[]{:S(2)}, u32[]{:S(2)}) collective-permute-start(f32[16,32]{1,0:T(8,128)S(1)} %add.17), channel_id=1, source_target_pairs={{0,8},{2,10},{4,12},{6,14},{8,0},{10,2},{12,4},{14,6},{16,24},{18,... | collective-permute-start | bytes 6152 | tf_op jit(solution)/shard_map/ppermute | solution.py:35
  130.3 1.6 %collective-permute-done.24 = f32[16,32]{1,0:T(8,128)S(1)} collective-permute-done((f32[16,32]{1,0:T(8,128)S(1)}, f32[16,32]{1,0:T(8,128)S(1)}, u32[]{:S(2)}, u32[]{:S(2)}) %collective-permute-start.24) | collective-permute-done | bytes 2080 | tf_op jit(solution)/shard_map/ppermute | solution.py:35
  131.9 3.0 %collective-permute-start.25 = (f32[16,32]{1,0:T(8,128)S(1)}, f32[16,32]{1,0:T(8,128)S(1)}, u32[]{:S(2)}, u32[]{:S(2)}) collective-permute-start(f32[16,32]{1,0:T(8,128)S(1)} %add.18), channel_id=1, source_target_pairs={{0,16},{2,18},{4,20},{6,22},{8,24},{10,26},{12,28},{14,30},{16,0},... | collective-permute-start | bytes 6152 | tf_op jit(solution)/shard_map/ppermute | solution.py:35
  135.0 0.7 shard_map.89
  135.6 1.6 %collective-permute-start.15 = (bf16[64,1152]{1,0:T(8,128)(2,1)S(1)}, bf16[64,1152]{1,0:T(8,128)(2,1)S(1)}, u32[]{:S(2)}, u32[]{:S(2)}) collective-permute-start(bf16[64,1152]{1,0:T(8,128)(2,1)S(1)} %get-tuple-element.88), channel_id=1, source_target_pairs={{0,1},{1,0},{2,3},{3,2},{4,5},{5,4},{6,7},{7,6},{8,9},{9,8},{10,11... | collective-permute-start | bytes 442376 | tf_op jit(solution)/shard_map/ppermute | solution.py:35
  137.2 0.6 add_multiply_fusion
  137.8 3.0 %collective-permute-done.15.got_ref = bf16[64,1152]{1,0:T(8,128)(2,1)S(1)} collective-permute-done((bf16[64,1152]{1,0:T(8,128)(2,1)S(1)}, bf16[64,1152]{1,0:T(8,128)(2,1)S(1)}, u32[]{:S(2)}, u32[]{:S(2)}) %collective-permute-start.15) | collective-permute-done | bytes 147488 | tf_op jit(solution)/shard_map/ppermute | solution.py:35
  140.9 1.3 shard_map.90
  (26 shorter events, 0.1 us)
Async XLA Ops:
  0.6 2.0 %collective-permute-start.1 = (bf16[128,1152]{1,0:T(8,128)(2,1)}, bf16[128,1152]{1,0:T(8,128)(2,1)S(1)}, u32[]{:S(2)}, u32[]{:S(2)}) collective-permute-start(bf16[128,1152]{1,0:T(8,128)(2,1)} %refs_0_.2), channel_id=1, source_target_pairs={{0,2},{2,0},{4,6},{6,4},{8,10},{10,8},{12,14},{14,12},{16,18},{18,... | collective-permute-start | bytes 884744 | tf_op jit(solution)/shard_map/ppermute | solution.py:35
  2.6 1.0 copy-start.1
  3.6 25.9 %copy-start.3 = (bf16[128,1152]{1,0:T(8,128)(2,1)S(1)}, bf16[128,1152]{1,0:T(8,128)(2,1)}, u32[]{:S(2)}) copy-start(bf16[128,1152]{1,0:T(8,128)(2,1)} %refs_0_.3) | copy-start | bytes 884740
  3.6 28.6 %copy-start.2 = (bf16[128,1152]{1,0:T(8,128)(2,1)S(1)}, bf16[128,1152]{1,0:T(8,128)(2,1)}, u32[]{:S(2)}) copy-start(bf16[128,1152]{1,0:T(8,128)(2,1)} %refs_0_.2) | copy-start | bytes 884740
  4.2 16.4 %collective-permute-start.2 = (bf16[128,1920]{1,0:T(8,128)(2,1)S(1)}, bf16[128,1920]{1,0:T(8,128)(2,1)S(1)}, u32[]{:S(2)}, u32[]{:S(2)}) collective-permute-start(bf16[128,1920]{1,0:T(8,128)(2,1)S(1)} %get-tuple-element.54), channel_id=1, source_target_pairs={{0,4},{4,8},{8,12},{12,16},{16,20},{20,24},{24,28},{6,2},{10,6},{1... | collective-permute-start | bytes 1474568 | tf_op jit(solution)/shard_map/ppermute | solution.py:424
  9.0 19.8 %copy-start.6 = (s32[16]{0:T(128)S(1)}, s32[16]{0:T(128)}, u32[]{:S(2)}) copy-start(s32[16]{0:T(128)} %atom_ref.1) | copy-start | bytes 196
  9.0 23.2 %copy-start.4 = (s32[16]{0:T(128)S(1)}, s32[16]{0:T(128)}, u32[]{:S(2)}) copy-start(s32[16]{0:T(128)} %prof_ref.9) | copy-start | bytes 196
  9.0 12.1 %collective-permute-start.3 = (bf16[128,1408]{1,0:T(8,128)(2,1)S(1)}, bf16[128,1408]{1,0:T(8,128)(2,1)S(1)}, u32[]{:S(2)}, u32[]{:S(2)}) collective-permute-start(bf16[128,1408]{1,0:T(8,128)(2,1)S(1)} %get-tuple-element.55), channel_id=1, source_target_pairs={{0,8},{4,12},{8,16},{12,20},{16,24},{20,28},{10,2},{14,6},{18,10},... | collective-permute-start | bytes 1081352 | tf_op jit(solution)/shard_map/ppermute | solution.py:424
  20.6 10.1 %collective-permute-start.4 = (bf16[128,1920]{1,0:T(8,128)(2,1)S(1)}, bf16[128,1920]{1,0:T(8,128)(2,1)S(1)}, u32[]{:S(2)}, u32[]{:S(2)}) collective-permute-start(bf16[128,1920]{1,0:T(8,128)(2,1)S(1)} %collective-permute-done.2.refs_2_), channel_id=1, source_target_pairs={{0,2},{2,0},{4,6},{6,4},{8,10},{10,8},{12,14},{14,12},{16,18},{18,... | collective-permute-start | bytes 1474568 | tf_op jit(solution)/shard_map/ppermute | solution.py:35
  20.6 6.7 %collective-permute-start.16 = (bf16[128,1152]{1,0:T(8,128)(2,1)}, bf16[128,1152]{1,0:T(8,128)(2,1)S(1)}, u32[]{:S(2)}, u32[]{:S(2)}) collective-permute-start(bf16[128,1152]{1,0:T(8,128)(2,1)} %refs_0_.3), channel_id=1, source_target_pairs={{0,2},{2,0},{4,6},{6,4},{8,10},{10,8},{12,14},{14,12},{16,18},{18,... | collective-permute-start | bytes 884744 | tf_op jit(solution)/shard_map/ppermute | solution.py:35
  21.1 9.0 %collective-permute-start.5 = (bf16[128,1408]{1,0:T(8,128)(2,1)S(1)}, bf16[128,1408]{1,0:T(8,128)(2,1)S(1)}, u32[]{:S(2)}, u32[]{:S(2)}) collective-permute-start(bf16[128,1408]{1,0:T(8,128)(2,1)S(1)} %collective-permute-done.3.refs_3_), channel_id=1, source_target_pairs={{0,2},{2,0},{4,6},{6,4},{8,10},{10,8},{12,14},{14,12},{16,18},{18,... | collective-permute-start | bytes 1081352 | tf_op jit(solution)/shard_map/ppermute | solution.py:35
  21.1 2.3 %copy-start = (bf16[16,128,1152]{2,1,0:T(8,128)(2,1)S(1)}, bf16[16,128,1152]{2,1,0:T(8,128)(2,1)}, u32[]{:S(2)}) copy-start(bf16[16,128,1152]{2,1,0:T(8,128)(2,1)} %three_ref.3) | copy-start | bytes 14155780
  23.4 5.4 %copy-start.5 = (bf16[16,32]{1,0:T(8,128)(2,1)S(1)}, bf16[16,32]{1,0:T(8,128)(2,1)}, u32[]{:S(2)}) copy-start(bf16[16,32]{1,0:T(8,128)(2,1)} %k_ref.1) | copy-start | bytes 3076
  24.1 46.3 %collective-permute-start.7 = (bf16[256,1152]{1,0:T(8,128)(2,1)S(1)}, bf16[256,1152]{1,0:T(8,128)(2,1)S(1)}, u32[]{:S(2)}, u32[]{:S(2)}) collective-permute-start(bf16[256,1152]{1,0:T(8,128)(2,1)S(1)} %bitcast.14), channel_id=1, source_target_pairs={{0,1},{1,0},{2,3},{3,2},{4,5},{5,4},{6,7},{7,6},{8,9},{9,8},{10,11... | collective-permute-start | bytes 1769480 | tf_op jit(solution)/shard_map/ppermute | solution.py:35
  26.7 45.3 %collective-permute-start.8 = (bf16[256,1152]{1,0:T(8,128)(2,1)S(1)}, bf16[256,1152]{1,0:T(8,128)(2,1)S(1)}, u32[]{:S(2)}, u32[]{:S(2)}) collective-permute-start(bf16[256,1152]{1,0:T(8,128)(2,1)S(1)} %bitcast.26), channel_id=1, source_target_pairs={{0,1},{1,0},{2,3},{3,2},{4,5},{5,4},{6,7},{7,6},{8,9},{9,8},{10,11... | collective-permute-start | bytes 1769480 | tf_op jit(solution)/shard_map/ppermute | solution.py:35
  27.3 46.4 %collective-permute-start.9 = (bf16[256,1152]{1,0:T(8,128)(2,1)S(1)}, bf16[256,1152]{1,0:T(8,128)(2,1)S(1)}, u32[]{:S(2)}, u32[]{:S(2)}) collective-permute-start(bf16[256,1152]{1,0:T(8,128)(2,1)S(1)} %bitcast.25), channel_id=1, source_target_pairs={{0,1},{1,0},{2,3},{3,2},{4,5},{5,4},{6,7},{7,6},{8,9},{9,8},{10,11... | collective-permute-start | bytes 1769480 | tf_op jit(solution)/shard_map/ppermute | solution.py:35
  30.1 35.7 %collective-permute-start = (f32[16,64]{1,0:T(8,128)S(1)}, f32[16,64]{1,0:T(8,128)S(1)}, u32[]{:S(2)}, u32[]{:S(2)}) collective-permute-start(f32[16,64]{1,0:T(8,128)S(1)} %get-tuple-element.53), channel_id=1, source_target_pairs={{0,1},{1,0},{2,3},{3,2},{4,5},{5,4},{6,7},{7,6},{8,9},{9,8},{10,11... | collective-permute-start | bytes 12296 | tf_op jit(solution)/shard_map/ppermute | solution.py:35
  30.7 50.4 %collective-permute-start.6 = (bf16[256,1152]{1,0:T(8,128)(2,1)S(1)}, bf16[256,1152]{1,0:T(8,128)(2,1)S(1)}, u32[]{:S(2)}, u32[]{:S(2)}) collective-permute-start(bf16[256,1152]{1,0:T(8,128)(2,1)S(1)} %bitcast.24), channel_id=1, source_target_pairs={{0,1},{1,0},{2,3},{3,2},{4,5},{5,4},{6,7},{7,6},{8,9},{9,8},{10,11... | collective-permute-start | bytes 1769480 | tf_op jit(solution)/shard_map/ppermute | solution.py:35
  65.8 21.8 %collective-permute-start.17 = (bf16[128,1920]{1,0:T(8,128)(2,1)S(1)}, bf16[128,1920]{1,0:T(8,128)(2,1)S(1)}, u32[]{:S(2)}, u32[]{:S(2)}) collective-permute-start(bf16[128,1920]{1,0:T(8,128)(2,1)S(1)} %get-tuple-element.89), channel_id=1, source_target_pairs={{0,4},{4,8},{8,12},{12,16},{16,20},{20,24},{24,28},{6,2},{10,6},{1... | collective-permute-start | bytes 1474568 | tf_op jit(solution)/shard_map/ppermute | solution.py:424
  84.0 15.3 %collective-permute-start.10 = (bf16[4,128,1024]{2,1,0:T(8,128)(2,1)S(1)}, bf16[4,128,1024]{2,1,0:T(8,128)(2,1)S(1)}, u32[]{:S(2)}, u32[]{:S(2)}) collective-permute-start(bf16[4,128,1024]{2,1,0:T(8,128)(2,1)S(1)} %get-tuple-element.74), channel_id=1, source_target_pairs={{0,2},{2,0},{4,6},{6,4},{8,10},{10,8},{12,14},{14,12},{16,18},{18,... | collective-permute-start | bytes 3145736 | tf_op jit(solution)/shard_map/ppermute | solution.py:35
  84.1 8.4 %collective-permute-start.18 = (bf16[128,1408]{1,0:T(8,128)(2,1)S(1)}, bf16[128,1408]{1,0:T(8,128)(2,1)S(1)}, u32[]{:S(2)}, u32[]{:S(2)}) collective-permute-start(bf16[128,1408]{1,0:T(8,128)(2,1)S(1)} %get-tuple-element.90), channel_id=1, source_target_pairs={{0,8},{4,12},{8,16},{12,20},{16,24},{20,28},{10,2},{14,6},{18,10},... | collective-permute-start | bytes 1081352 | tf_op jit(solution)/shard_map/ppermute | solution.py:424
  87.6 6.8 %collective-permute-start.19 = (bf16[128,1920]{1,0:T(8,128)(2,1)S(1)}, bf16[128,1920]{1,0:T(8,128)(2,1)S(1)}, u32[]{:S(2)}, u32[]{:S(2)}) collective-permute-start(bf16[128,1920]{1,0:T(8,128)(2,1)S(1)} %collective-permute-done.17.refs_2_), channel_id=1, source_target_pairs={{0,2},{2,0},{4,6},{6,4},{8,10},{10,8},{12,14},{14,12},{16,18},{18,... | collective-permute-start | bytes 1474568 | tf_op jit(solution)/shard_map/ppermute | solution.py:35
  92.5 1.9 %collective-permute-start.20 = (bf16[128,1408]{1,0:T(8,128)(2,1)S(1)}, bf16[128,1408]{1,0:T(8,128)(2,1)S(1)}, u32[]{:S(2)}, u32[]{:S(2)}) collective-permute-start(bf16[128,1408]{1,0:T(8,128)(2,1)S(1)} %collective-permute-done.18.refs_3_), channel_id=1, source_target_pairs={{0,2},{2,0},{4,6},{6,4},{8,10},{10,8},{12,14},{14,12},{16,18},{18,... | collective-permute-start | bytes 1081352 | tf_op jit(solution)/shard_map/ppermute | solution.py:35
  100.1 34.8 %collective-permute-start.13 = (bf16[128,768]{1,0:T(8,128)(2,1)S(1)}, bf16[128,768]{1,0:T(8,128)(2,1)S(1)}, u32[]{:S(2)}, u32[]{:S(2)}) collective-permute-start(bf16[128,768]{1,0:T(8,128)(2,1)S(1)} %get-tuple-element.85), channel_id=1, source_target_pairs={{0,8},{2,10},{4,12},{6,14},{8,16},{10,18},{12,20},{14,22},{16,24},... | collective-permute-start | bytes 589832 | tf_op jit(solution)/shard_map/ppermute | solution.py:31
  104.3 30.6 %collective-permute-start.14 = (bf16[128,768]{1,0:T(8,128)(2,1)S(1)}, bf16[128,768]{1,0:T(8,128)(2,1)S(1)}, u32[]{:S(2)}, u32[]{:S(2)}) collective-permute-start(bf16[128,768]{1,0:T(8,128)(2,1)S(1)} %get-tuple-element.86), channel_id=1, source_target_pairs={{8,0},{10,2},{12,4},{14,6},{16,8},{18,10},{20,12},{22,14},{24,16},... | collective-permute-start | bytes 589832 | tf_op jit(solution)/shard_map/ppermute | solution.py:31
  105.6 29.3 %collective-permute-start.11 = (bf16[128,1024]{1,0:T(8,128)(2,1)S(1)}, bf16[128,1024]{1,0:T(8,128)(2,1)S(1)}, u32[]{:S(2)}, u32[]{:S(2)}) collective-permute-start(bf16[128,1024]{1,0:T(8,128)(2,1)S(1)} %get-tuple-element.83), channel_id=1, source_target_pairs={{0,4},{2,6},{4,8},{6,10},{8,12},{10,14},{12,16},{14,18},{16,20},{1... | collective-permute-start | bytes 786440 | tf_op jit(solution)/shard_map/ppermute | solution.py:31
  108.1 26.9 %collective-permute-start.12 = (bf16[128,1024]{1,0:T(8,128)(2,1)S(1)}, bf16[128,1024]{1,0:T(8,128)(2,1)S(1)}, u32[]{:S(2)}, u32[]{:S(2)}) collective-permute-start(bf16[128,1024]{1,0:T(8,128)(2,1)S(1)} %get-tuple-element.84), channel_id=1, source_target_pairs={{4,0},{6,2},{8,4},{10,6},{12,8},{14,10},{16,12},{18,14},{20,16},{2... | collective-permute-start | bytes 786440 | tf_op jit(solution)/shard_map/ppermute | solution.py:31
  116.1 3.7 %collective-permute-start.21 = (f32[16,32]{1,0:T(8,128)S(1)}, f32[16,32]{1,0:T(8,128)S(1)}, u32[]{:S(2)}, u32[]{:S(2)}) collective-permute-start(f32[16,32]{1,0:T(8,128)S(1)} %get-tuple-element.101), channel_id=1, source_target_pairs={{0,1},{1,0},{2,3},{3,2},{4,5},{5,4},{6,7},{7,6},{8,9},{9,8},{10,11... | collective-permute-start | bytes 6152 | tf_op jit(solution)/shard_map/ppermute | solution.py:35
  119.8 1.2 collective-permute-start.22
  121.0 5.8 %collective-permute-start.23 = (f32[16,32]{1,0:T(8,128)S(1)}, f32[16,32]{1,0:T(8,128)S(1)}, u32[]{:S(2)}, u32[]{:S(2)}) collective-permute-start(f32[16,32]{1,0:T(8,128)S(1)} %add.16), channel_id=1, source_target_pairs={{0,4},{2,6},{4,0},{6,2},{8,12},{10,14},{12,8},{14,10},{16,20},{18,... | collective-permute-start | bytes 6152 | tf_op jit(solution)/shard_map/ppermute | solution.py:35
  126.8 5.1 %collective-permute-start.24 = (f32[16,32]{1,0:T(8,128)S(1)}, f32[16,32]{1,0:T(8,128)S(1)}, u32[]{:S(2)}, u32[]{:S(2)}) collective-permute-start(f32[16,32]{1,0:T(8,128)S(1)} %add.17), channel_id=1, source_target_pairs={{0,8},{2,10},{4,12},{6,14},{8,0},{10,2},{12,4},{14,6},{16,24},{18,... | collective-permute-start | bytes 6152 | tf_op jit(solution)/shard_map/ppermute | solution.py:35
  131.9 5.3 %collective-permute-start.25 = (f32[16,32]{1,0:T(8,128)S(1)}, f32[16,32]{1,0:T(8,128)S(1)}, u32[]{:S(2)}, u32[]{:S(2)}) collective-permute-start(f32[16,32]{1,0:T(8,128)S(1)} %add.18), channel_id=1, source_target_pairs={{0,16},{2,18},{4,20},{6,22},{8,24},{10,26},{12,28},{14,30},{16,0},... | collective-permute-start | bytes 6152 | tf_op jit(solution)/shard_map/ppermute | solution.py:35
  135.6 5.2 %collective-permute-start.15 = (bf16[64,1152]{1,0:T(8,128)(2,1)S(1)}, bf16[64,1152]{1,0:T(8,128)(2,1)S(1)}, u32[]{:S(2)}, u32[]{:S(2)}) collective-permute-start(bf16[64,1152]{1,0:T(8,128)(2,1)S(1)} %get-tuple-element.88), channel_id=1, source_target_pairs={{0,1},{1,0},{2,3},{3,2},{4,5},{5,4},{6,7},{7,6},{8,9},{9,8},{10,11... | collective-permute-start | bytes 442376 | tf_op jit(solution)/shard_map/ppermute | solution.py:35

commit v2 on v1

--- a/solution.py
+++ b/solution.py
@@ -12,7 +12,6 @@
 F32 = jnp.float32
 BF16 = jnp.bfloat16
 SUB = 8
-CHUNKS = 4
 SPREAD = 4
 SLOTS = 9
 VMEM = pl.BlockSpec(memory_space=pltpu.VMEM)
@@ -43,14 +42,13 @@
     return inside & (jnp.abs(a - b) <= jnp.minimum(wide_a, wide_b))
 
 
-def run(kernel, operands, outs, flops=0, scratch=(), smem=0, grant=24):
+def run(kernel, operands, outs, flops=0, smem=0, grant=24):
     nbytes = sum(math.prod(s.shape) * s.dtype.itemsize for s in (*operands, *outs))
     return pl.pallas_call(
         kernel,
         out_shape=outs,
         in_specs=[SMEM] * smem + [VMEM] * (len(operands) - smem),
         out_specs=[VMEM] * len(outs),
-        scratch_shapes=list(scratch),
         compiler_params=pltpu.CompilerParams(vmem_limit_bytes=grant * 1024 * 1024),
         cost_estimate=pl.CostEstimate(
             flops=int(flops), bytes_accessed=int(nbytes), transcendentals=0
@@ -110,14 +108,14 @@
     return lax.rem(r, SUB) == lax.rem(c, SUB)
 
 
-def mixing_matrix(mine_ref, theirs_ref):
+def mixing_kernel(mine_ref, theirs_ref, out_ref):
     every = mine_ref.shape[1] // 2
     size = every * SUB
     row, _ = screen_row(mine_ref, theirs_ref)
     k = jnp.concatenate([mine_ref[:, :every], theirs_ref[:, :every]], 0) * row
     pick = one_hot(size, every).astype(BF16)
     wide = dot_columns(dot(pick, k.astype(BF16)).astype(BF16), pick)
-    return jnp.where(same_row(size), wide, 0.0).astype(BF16)
+    out_ref[...] = jnp.where(same_row(size), wide, 0.0).astype(BF16)
 
 
 def band_slots(delta, which):
@@ -149,10 +147,9 @@
         fill(-1, (mid_ref, own_ref))
 
 
-def stack_kernel(nblocks, counts, at_ref, prof_ref, *refs):
+def stack_kernel(nblocks, at_ref, prof_ref, *refs):
     own_ref, mid_ref, hop1_ref, hop2_ref, near1_ref, near2_ref = refs[:6]
-    owns = refs[6 : 6 + counts]
-    stack_ref, outs = refs[6 + counts], refs[7 + counts :]
+    rows_ref, stack_ref, out_ref = refs[6:]
     block = own_ref.shape[0]
     position = at_ref[0]
 
@@ -189,8 +186,10 @@
     def _():
         build(1, (mid_ref, own_ref), nears, hops)
 
-    for own, out in zip(owns, outs):
-        out[...] = dot(own[...], stack_ref[...]).astype(BF16)
+    part = out_ref.shape[0] // 4
+    for n in range(4):
+        rows = slice(n * part, (n + 1) * part)
+        out_ref[rows, :] = dot(rows_ref[rows, :], stack_ref[...]).astype(BF16)
 
 
 def cut_kernel(rows, picks, at_ref, three_ref, *refs):
@@ -211,37 +210,38 @@
         copy.wait()
 
 
-def respond(mixed, po_ref, pr_ref, ro_ref, rr_ref):
-    half = mixed.shape[0] // 2
-    for g in range(po_ref.shape[0] // half):
+def respond_kernel(first, mixed_ref, v_ref, s_ref, po_ref, pr_ref, resp_ref):
+    pr_ref[...] = dot(s_ref[...], v_ref[...]).astype(BF16)
+    half = mixed_ref.shape[0] // 2
+    span = s_ref.shape[0]
+    for g in range(span // half):
         rows = slice(g * half, (g + 1) * half)
-        partner = jnp.concatenate([po_ref[rows, :], pr_ref[rows, :]], 0)
-        resp = dot(mixed, partner).astype(BF16)
-        ro_ref[rows, :] = resp[:half]
-        rr_ref[rows, :] = resp[half:]
-
-
-def respond_kernel(mine_ref, theirs_ref, v_ref, s_ref, po_ref, pr_ref, ro_ref, rr_ref):
-    pr_ref[...] = dot(s_ref[...], v_ref[...]).astype(BF16)
-    respond(mixing_matrix(mine_ref, theirs_ref), po_ref, pr_ref, ro_ref, rr_ref)
-
-
-def early_kernel(count, *refs):
-    out_ref = refs[2 * count]
-    for c in range(0, out_ref.shape[1], 384):
-        columns = slice(c, c + 384)
+        own_rows = slice(first + g * half, first + (g + 1) * half)
+        partner = jnp.concatenate([po_ref[own_rows, :], pr_ref[rows, :]], 0)
+        resp = dot(mixed_ref[...], partner).astype(BF16)
+        resp_ref[rows, :] = resp[:half]
+        resp_ref[span + g * half : span + (g + 1) * half, :] = resp[half:]
+
+
+def early_kernel(spans, so_ref, *refs):
+    count = len(spans)
+    out_ref = refs[-1]
+    third = out_ref.shape[0] // 3
+    for m in range(3):
+        cols = slice(m * third, (m + 1) * third)
         acc = None
-        for s_ref, r_ref in zip(refs[:count], refs[count : 2 * count]):
-            part = dot_rows(s_ref[...], r_ref[:, columns])
+        for rows, s_ref, resp_ref in zip(spans, refs[:count], refs[count:]):
+            both = jnp.concatenate([so_ref[rows, cols], s_ref[:, cols]], 0)
+            part = dot_rows(both, resp_ref[...])
             acc = part if acc is None else acc + part
-        out_ref[:, columns] = acc
-
-
-def terms_of(offsets, early_ref, so_ref, sr_ref, ro_ref, rr_ref, block):
+        out_ref[cols, :] = acc
+
+
+def terms_of(offsets, first, early_ref, so_ref, sr_ref, resp_ref, block):
     take = [slice((d + SPREAD) * block, (d + SPREAD + 1) * block) for d in offsets]
-    own = jnp.concatenate([so_ref[:, t] for t in take], 1)
-    got = jnp.concatenate([sr_ref[:, t] for t in take], 1)
-    total = dot_rows(own, ro_ref[...]) + dot_rows(got, rr_ref[...])
+    rows = slice(first, first + sr_ref.shape[0])
+    both = [jnp.concatenate([so_ref[rows, t], sr_ref[:, t]], 0) for t in take]
+    total = dot_rows(jnp.concatenate(both, 1), resp_ref[...])
     return [total[n * block : (n + 1) * block] + early_ref[t, :] for n, t in enumerate(take)]
 
 
@@ -258,13 +258,13 @@
 
 
 def odd_kernel(
-    nblocks, at_ref, prof_ref, mine_ref, theirs_ref, v_ref, s_ref, po_ref, so_ref, early_ref,
-    pr_ref, ro_ref, rr_ref, pack_ref,
+    nblocks, first, at_ref, prof_ref, mixed_ref, v_ref, s_ref, po_ref, so_ref, early_ref,
+    pr_ref, resp_ref, pack_ref,
 ):
-    respond_kernel(mine_ref, theirs_ref, v_ref, s_ref, po_ref, pr_ref, ro_ref, rr_ref)
+    respond_kernel(first, mixed_ref, v_ref, s_ref, po_ref, pr_ref, resp_ref)
     block = pack_ref.shape[1]
     position = at_ref[0]
-    terms = terms_of(ODD, early_ref, so_ref, s_ref, ro_ref, rr_ref, block)
+    terms = terms_of(ODD, first, early_ref, so_ref, s_ref, resp_ref, block)
     for n, (offset, term) in enumerate(zip(ODD, terms)):
         ok = permitted(prof_ref, nblocks, position, position + offset)
         tiles = placed_terms(ok, term, offset, FIRST_COLUMN[offset], 8, block, BF16)
@@ -273,17 +273,17 @@
 
 
 def even_kernel(
-    nblocks, at_ref, prof_ref, so_ref, s_ref, ro_ref, rr_ref, early_ref, own_ref, *out_refs
+    nblocks, first, at_ref, prof_ref, so_ref, s_ref, resp_ref, early_ref, own_ref, *out_refs
 ):
     block = own_ref.shape[0]
     position = at_ref[0]
     offsets = (0, 2, -2, 4, -4)
-    terms = terms_of(offsets, early_ref, so_ref, s_ref, ro_ref, rr_ref, block)
+    terms = terms_of(offsets, first, early_ref, so_ref, s_ref, resp_ref, block)
     own_ref[...] = terms[0]
     for offset, term, out in zip(offsets[1:], terms[1:], out_refs):
         ok = permitted(prof_ref, nblocks, position, position + offset)
-        first, count = FIRST_COLUMN[offset], columns_to(offset)
-        for c, tile in enumerate(placed_terms(ok, term, offset, first, count, block, F32)):
+        begin, count = FIRST_COLUMN[offset], columns_to(offset)
+        for c, tile in enumerate(placed_terms(ok, term, offset, begin, count, block, F32)):
             out[:, c * block : (c + 1) * block] = tile
 
 
@@ -333,7 +333,11 @@
             target[:, columns] = total.astype(target.dtype)
 
 
-def finish_kernel(nblocks, block, scale, at_ref, prof_ref, keep_ref, got_ref, out_ref):
+def finish_kernel(
+    nblocks, block, scale, polar_scale, at_ref, prof_ref, keep_ref, got_ref, pk_ref, pg_ref,
+    out_ref, polar_ref,
+):
+    polar_ref[...] = (pk_ref[...] + pg_ref[...]) * polar_scale
     position = at_ref[0]
     for c in range(SLOTS):
         columns = slice(c * block, (c + 1) * block)
@@ -342,29 +346,37 @@
         out_ref[:, columns] = jnp.where(ok, value, jnp.zeros_like(value))
 
 
-def gram_of(size, x_ref, quads, total):
+def gram_of(size, x_ref, co_ref, po_ref, chunks, total):
     half = size // 2
-    for s_ref, co_ref, po_ref, pr_ref in quads:
+    for first, s_ref, pr_ref in chunks:
         got = dot(s_ref[...], x_ref[...]).astype(BF16)
         for g in range(s_ref.shape[0] // half):
             rows = slice(g * half, (g + 1) * half)
-            coupled = jnp.concatenate([co_ref[rows, :], got[rows]], 0)
-            partner = jnp.concatenate([po_ref[rows, :], pr_ref[rows, :]], 0)
+            own_rows = slice(first + g * half, first + (g + 1) * half)
+            coupled = jnp.concatenate([co_ref[own_rows, :], got[rows]], 0)
+            partner = jnp.concatenate([po_ref[own_rows, :], pr_ref[rows, :]], 0)
             part = dot_columns(coupled, partner)
             total = part if total is None else total + part
     return total
 
 
-def gram_kernel(count, x_ref, *refs):
-    quads = [refs[4 * c : 4 * c + 4] for c in range(count)]
-    out_ref = refs[4 * count]
-    out_ref[...] = gram_of(out_ref.shape[0], x_ref, quads, None)
-
-
-def polar_kernel(at_ref, x_ref, s_ref, co_ref, po_ref, pr_ref, gram_ref, mine_ref, theirs_ref, keep_ref, send_ref):
+def chunk_refs(firsts, refs):
+    return list(zip(firsts, refs[::2], refs[1::2]))
+
+
+def gram_kernel(firsts, x_ref, co_ref, po_ref, *refs):
+    out_ref = refs[-1]
+    chunks = chunk_refs(firsts, refs[:-1])
+    out_ref[...] = gram_of(out_ref.shape[0], x_ref, co_ref, po_ref, chunks, None)
+
+
+def polar_kernel(firsts, at_ref, x_ref, co_ref, po_ref, gram_ref, mine_ref, theirs_ref, *refs):
+    out_ref = refs[-1]
     size = gram_ref.shape[0]
-    here, every = keep_ref.shape
-    total = gram_of(size, x_ref, [(s_ref, co_ref, po_ref, pr_ref)], gram_ref[...])
+    every = out_ref.shape[0]
+    here = every // 2
+    chunks = chunk_refs(firsts, refs[:-1])
+    total = gram_of(size, x_ref, co_ref, po_ref, chunks, gram_ref[...])
     by_row = jnp.sum(jnp.where(same_row(size), total, 0.0).reshape(every, SUB, size), 1)
     polar = jnp.dot(
         by_row, one_hot(size, every), preferred_element_type=F32, precision=lax.Precision.HIGHEST
@@ -372,9 +384,7 @@
     row, alive = screen_row(mine_ref, theirs_ref)
     polar = polar * row * alive
     turned = jnp.concatenate([polar[:, here:], polar[:, :here]], 1)
-    polar = jnp.where(at_ref[1] == 0, polar, turned)
-    keep_ref[...] = polar[:here]
-    send_ref[...] = polar[here:]
+    out_ref[...] = jnp.where(at_ref[1] == 0, polar, turned)
 
 
 def step(occupied, virtual, three_centre, kernel, profile, atom_map):
@@ -390,24 +400,30 @@
     rows = block // halves
     groups = rows // SUB
     per_group = here * SUB
-    per_chunk = groups // CHUNKS
-    span = per_chunk * per_group
+    most = -(-groups // 3)
+    sizes = (most, most, groups - 2 * most)
+    begins = (0, most, 2 * most)
+    firsts = [g * per_group for g in begins]
+    counts = [g * per_group for g in sizes]
     at = jnp.stack([position, half]).astype(jnp.int32)
 
-    def cut(picks, grant=24):
-        shape = (per_chunk, here, SUB, width)
+    integrals = pltpu.with_memory_space_constraint(three_centre, pltpu.HBM)
+
+    def cut(picks):
+        lengths = [count for _, _, count in picks]
         call = pl.pallas_call(
-            functools.partial(cut_kernel, rows, picks),
-            out_shape=[shaped(shape)] * len(picks),
+            functools.partial(cut_kernel, rows, [pick[:2] for pick in picks]),
+            out_shape=[shaped((count, here, SUB, width)) for count in lengths],
             in_specs=[SMEM, pl.BlockSpec(memory_space=pltpu.HBM)],
             out_specs=[VMEM] * len(picks),
-            scratch_shapes=[pltpu.SemaphoreType.DMA((len(picks) * per_chunk,))],
-            compiler_params=pltpu.CompilerParams(vmem_limit_bytes=grant * 1024 * 1024),
+            scratch_shapes=[pltpu.SemaphoreType.DMA((sum(lengths),))],
+            compiler_params=pltpu.CompilerParams(vmem_limit_bytes=24 * 1024 * 1024),
             cost_estimate=pl.CostEstimate(
-                flops=0, bytes_accessed=4 * len(picks) * span * width, transcendentals=0
+                flops=0, bytes_accessed=4 * sum(lengths) * per_group * width, transcendentals=0
             ),
         )
-        return [part.reshape(span, width) for part in call(at, three_centre)]
+        parts = call(at, integrals)
+        return [part.reshape(-1, width) for part in parts]
 
     def halo(band):
         mid = swapped(band, "chain")
@@ -424,12 +440,10 @@
             hops.append(lax.ppermute(pack, "chain", up + down))
         return [band, mid, *hops, *[swapped(h, "chain") for h in hops]]
 
-    starts = [c * per_chunk for c in range(CHUNKS)]
-    sends = cut([(False, starts[0])])
-    rest = cut([(False, f) for f in starts[1:]] + [(True, f) for f in starts])
-    sends += rest[: CHUNKS - 1]
-    own = rest[CHUNKS - 1 :]
-    got = [swapped(part, "aux") for part in sends]
+    sends = cut([(False, begins[0], sizes[0])])
+    rest = [(False, f, n) for f, n in zip(begins[1:], sizes[1:])]
+    *others, own = cut(rest + [(True, 0, groups)])
+    got = [swapped(part, "aux") for part in [*sends, *others]]
     near_vir = halo(virtual)
     near_occ = halo(occupied)
 
@@ -441,47 +455,57 @@
     )
     theirs = swapped(send, "aux")
 
-    product = 2 * span * width * width
-    vir_stack, *partner_own = run(
-        functools.partial(stack_kernel, nblocks, CHUNKS),
-        [at, profile, *near_vir, *own],
-        [shaped((width, width))] + [shaped((span, width))] * CHUNKS,
-        flops=CHUNKS * product,
-        smem=2,
-    )
-    partner_got, resp_own, resp_got = [], [], []
-    for c in range(CHUNKS - 1):
-        pr, ro, rr = run(
-            respond_kernel,
-            [mine, theirs, vir_stack, got[c], partner_own[c]],
-            [shaped((span, width))] * 3,
-            flops=2 * product,
+    (mixed,) = run(mixing_kernel, [mine, theirs], [shaped((every * SUB, every * SUB))])
+
+    per_row = 2 * width * width
+    own_flops = own.shape[0] * per_row
+
+    def contracted(near):
+        return run(
+            functools.partial(stack_kernel, nblocks),
+            [at, profile, *near, own],
+            [shaped((width, width)), shaped(own.shape)],
+            flops=own_flops,
+            smem=2,
+        )
+
+    vir_stack, partner_own = contracted(near_vir)
+    partner_got, responses = [], []
+    for c in range(2):
+        pr, resp = run(
+            functools.partial(respond_kernel, firsts[c]),
+            [mixed, vir_stack, got[c], partner_own],
+            [shaped((counts[c], width)), shaped((2 * counts[c], width))],
+            flops=2 * counts[c] * per_row,
         )
         partner_got.append(pr)
-        resp_own.append(ro)
-        resp_got.append(rr)
+        responses.append(resp)
     (early,) = run(
-        functools.partial(early_kernel, 2 * (CHUNKS - 1)),
-        [*own[:-1], *got[:-1], *resp_own, *resp_got],
+        functools.partial(early_kernel, [slice(f, f + n) for f, n in zip(firsts[:2], counts)]),
+        [own, *got[:2], *responses],
         [shaped((width, width), F32)],
-        flops=2 * (CHUNKS - 1) * product,
-    )
-    pr, ro, rr, pack = run(
-        functools.partial(odd_kernel, nblocks),
-        [at, profile, mine, theirs, vir_stack, got[-1], partner_own[-1], own[-1], early],
-        [shaped((span, width))] * 3 + [shaped((len(ODD), block, 8 * block))],
-        flops=2 * product,
+        flops=2 * firsts[2] * per_row,
+    )
+    pr, resp, pack = run(
+        functools.partial(odd_kernel, nblocks, firsts[2]),
+        [at, profile, mixed, vir_stack, got[2], partner_own, own, early],
+        [
+            shaped((counts[2], width)),
+            shaped((2 * counts[2], width)),
+            shaped((len(ODD), block, 8 * block)),
+        ],
+        flops=2 * counts[2] * per_row,
         smem=2,
     )
     partner_got.append(pr)
     other_pack = swapped(pack, "chain")
     offsets = (2, -2, 4, -4)
     even = run(
-        functools.partial(even_kernel, nblocks),
-        [at, profile, own[-1], got[-1], ro, rr, early],
+        functools.partial(even_kernel, nblocks, firsts[2]),
+        [at, profile, own, got[2], resp, early],
         [shaped((block, width), F32)]
         + [shaped((block, columns_to(d) * block), F32) for d in offsets],
-        flops=product,
+        flops=counts[2] * per_row,
         smem=2,
     )
     mid, *sends = run(
@@ -497,42 +521,41 @@
         [shaped((rows, width), F32), shaped((rows, width))],
         smem=1,
     )
-    (band_gradient,) = run(
-        functools.partial(finish_kernel, nblocks, block, 1.0 / math.sqrt(block * every)),
-        [at, profile, keep, swapped(send, "aux")],
-        [shaped((rows, width), F32)],
+    occ_stack, coupled_own = contracted(near_occ)
+    size = every * SUB
+    (gram,) = run(
+        functools.partial(gram_kernel, firsts[:2]),
+        [occ_stack, coupled_own, partner_own, got[0], partner_got[0], got[1], partner_got[1]],
+        [shaped((size, size), F32)],
+        flops=firsts[2] * per_row,
+    )
+    (polar,) = run(
+        functools.partial(polar_kernel, firsts[2:]),
+        [at, occ_stack, coupled_own, partner_own, gram, mine, theirs, got[2], partner_got[2]],
+        [shaped((every, every), F32)],
+        flops=counts[2] * per_row,
+        smem=1,
+    )
+    bits = [1 << n for n in range(nblocks.bit_length() - 1)]
+    first = bits.pop(min(2, len(bits) - 1))
+    polar = polar + swapped(polar, "chain", first)
+    polar = polar[:here] + swapped(polar[here:], "aux")
+    for n, bit in enumerate(bits):
+        other = swapped(polar, "chain", bit)
+        if n < len(bits) - 1:
+            polar = polar + other
+    return run(
+        functools.partial(
+            finish_kernel,
+            nblocks,
+            block,
+            1.0 / math.sqrt(block * every),
+            1.0 / math.sqrt(block * nblocks * width),
+        ),
+        [at, profile, keep, swapped(send, "aux"), polar, other],
+        [shaped((rows, width), F32), shaped((here, every), F32)],
         smem=2,
     )
-
-    occ_stack, *coupled_own = run(
-        functools.partial(stack_kernel, nblocks, CHUNKS),
-        [at, profile, *near_occ, *own],
-        [shaped((width, width))] + [shaped((span, width))] * CHUNKS,
-        flops=CHUNKS * product,
-        smem=2,
-    )
-    size = every * SUB
-    quads = [q for c in range(CHUNKS - 1) for q in (got[c], coupled_own[c], partner_own[c], partner_got[c])]
-    (gram,) = run(
-        functools.partial(gram_kernel, CHUNKS - 1),
-        [occ_stack, *quads],
-        [shaped((size, size), F32)],
-        flops=CHUNKS * product,
-    )
-    polar, send = run(
-        polar_kernel,
-        [at, occ_stack, got[-1], coupled_own[-1], partner_own[-1], partner_got[-1], gram, mine, theirs],
-        [shaped((here, every), F32)] * 2,
-        flops=2 * product,
-        smem=1,
-    )
-    polar = polar + swapped(send, "aux")
-    bit = 1
-    while bit < nblocks:
-        polar = polar + swapped(polar, "chain", bit)
-        bit *= 2
-    polarization = polar * (1.0 / math.sqrt(block * nblocks * width))
-    return (band_gradient, polarization)
 
 
 def solution(mesh):

time: 143 us -> 134 us (0.937)
  waiting for transfers between devices: 52.8 us -> 48.6 us
  starting transfers between devices: 46.6 us -> 43.1 us
  local copies, waits for them, and re-layouts: 3.32 us -> 1 us
  Pallas kernels: 37.9 us -> 40 us
    ppermute x18 -> x17, starting transfers between devices: 21 us -> 16.4 us  [swapped(): lax.ppermute(block, axis, [(i, i ^ bit) for i in range(lax.axis_size(axis...]
    ppermute x18 -> x17, waiting for transfers between devices: 39.9 us -> 35.8 us  [swapped(): lax.ppermute(block, axis, [(i, i ^ bit) for i in range(lax.axis_size(axis...]
    pallas_call x2, Pallas kernels: 1.71 us -> 4.42 us  [cut(): parts = call(at, integrals)]
    unnamed x14 -> x12, local copies, waits for them, and re-layouts: 3.32 us -> 0.99 us
    ppermute x4, starting transfers between devices: 9.23 us -> 11.5 us  [passed_along(): return lax.ppermute(block, axis, route)]
  transfers between devices with their start and end apart: 26 -> 25, of which waited for: 9 -> 9; matrix products, arithmetic and copies ran while one was open for 0% -> 0% of each run, Pallas kernels for 25% -> 28%
where the time goes in v2:
time: 134 us
  waiting for transfers between devices  48.6 us (36%)
  starting transfers between devices  43.1 us (32%)
  Pallas kernels  40 us (30%)
    ppermute x17, waiting for transfers between devices, swapped(): lax.ppermute(block, axis, [(i, i ^ bit) for i in range(lax.axis_size(axis...  35.8 us
    pallas_call x16, Pallas kernels, run(): pl.pallas_call(kernel, out_shape=outs, in_specs=[SMEM] * smem + [VMEM] *...  35.6 us
    ppermute x17, starting transfers between devices, swapped(): lax.ppermute(block, axis, [(i, i ^ bit) for i in range(lax.axis_size(axis...  16.4 us
    ppermute x4, starting transfers between devices, halo(): hops.append(lax.ppermute(pack, 'chain', up + down))  15.2 us
    ppermute x4, waiting for transfers between devices, halo(): hops.append(lax.ppermute(pack, 'chain', up + down))  12.8 us
    ppermute x4, starting transfers between devices, passed_along(): return lax.ppermute(block, axis, route)  11.5 us
    pallas_call x2, Pallas kernels, cut(): parts = call(at, integrals)  4.42 us
  transfers between devices with their start and end apart: 25, of which 9 were waited for; matrix products, arithmetic and copies ran while one was open for 0% of the time, Pallas kernels for 28%

profile of v2, /device:TPU:0, one launch (start us, length us, event | category | flops | bytes accessed | tf_op | source)
XLA Modules:
  0.0 133.8 jit_solution(13408943877055542264)
XLA Ops:
  0.6 0.6 collective-permute-start.1
  1.2 0.1 pad_add_fusion.at_ref
  1.3 1.3 %collective-permute-done.1.mid_ref.refs_1_ = bf16[128,1152]{1,0:T(8,128)(2,1)S(1)} collective-permute-done((bf16[128,1152]{1,0:T(8,128)(2,1)}, bf16[128,1152]{1,0:T(8,128)(2,1)S(1)}, u32[]{:S(2)}, u32[]{:S(2)}) %collective-permute-start.1) | collective-permute-done | bytes 294944 | tf_op jit(solution)/shard_map/ppermute | solution.py:34
  2.6 1.0 copy-done
  3.6 0.6 shard_map.79
  4.2 4.8 %collective-permute-start.2 = (bf16[128,1920]{1,0:T(8,128)(2,1)S(1)}, bf16[128,1920]{1,0:T(8,128)(2,1)S(1)}, u32[]{:S(2)}, u32[]{:S(2)}) collective-permute-start(bf16[128,1920]{1,0:T(8,128)(2,1)S(1)} %get-tuple-element.36), channel_id=1, source_target_pairs={{0,4},{4,8},{8,12},{12,16},{16,20},{20,24},{24,28},{6,2},{10,6},{1... | collective-permute-start | bytes 1474568 | tf_op jit(solution)/shard_map/ppermute | solution.py:440
  9.0 3.5 %collective-permute-start.3 = (bf16[128,1408]{1,0:T(8,128)(2,1)S(1)}, bf16[128,1408]{1,0:T(8,128)(2,1)S(1)}, u32[]{:S(2)}, u32[]{:S(2)}) collective-permute-start(bf16[128,1408]{1,0:T(8,128)(2,1)S(1)} %get-tuple-element.37), channel_id=1, source_target_pairs={{0,8},{4,12},{8,16},{12,20},{16,24},{20,28},{10,2},{14,6},{18,10},... | collective-permute-start | bytes 1081352 | tf_op jit(solution)/shard_map/ppermute | solution.py:440
  12.5 1.7 %shard_map.82 = bf16[3,16,8,1152]{3,2,1,0:T(8,128)(2,1)S(1)} custom-call(s32[2]{0:T(128)S(1)} %pad_add_fusion.at_ref, bf16[16,128,1152]{2,1,0:T(8,128)(2,1)} %three_ref.3), custom_call_target="tpu_custom_call" | custom-call | bytes 1769472 | tf_op jit(solution)/shard_map/pallas_call | solution.py:425
  14.2 0.0 copy-start.4
  14.2 0.0 copy-start.5
  14.2 0.0 copy-start.2
  14.2 0.0 copy-start.1
  14.3 0.0 copy-start.3
  14.3 1.6 %collective-permute-start.7 = (bf16[384,1152]{1,0:T(8,128)(2,1)S(1)}, bf16[384,1152]{1,0:T(8,128)(2,1)S(1)}, u32[]{:S(2)}, u32[]{:S(2)}) collective-permute-start(bf16[384,1152]{1,0:T(8,128)(2,1)S(1)} %bitcast.11), channel_id=1, source_target_pairs={{0,1},{1,0},{2,3},{3,2},{4,5},{5,4},{6,7},{7,6},{8,9},{9,8},{10,11... | collective-permute-start | bytes 2654216 | tf_op jit(solution)/shard_map/ppermute | solution.py:34
  15.8 4.7 %collective-permute-done.2.refs_2_ = bf16[128,1920]{1,0:T(8,128)(2,1)S(1)} collective-permute-done((bf16[128,1920]{1,0:T(8,128)(2,1)S(1)}, bf16[128,1920]{1,0:T(8,128)(2,1)S(1)}, u32[]{:S(2)}, u32[]{:S(2)}) %collective-permute-start.2) | collective-permute-done | bytes 491552 | tf_op jit(solution)/shard_map/ppermute | solution.py:440
  20.6 0.0 collective-permute-start.4
  20.6 2.7 %shard_map.80 = (bf16[3,16,8,1152]{3,2,1,0:T(8,128)(2,1)S(1)}, bf16[2,16,8,1152]{3,2,1,0:T(8,128)(2,1)S(1)}, bf16[8,16,8,1152]{3,2,1,0:T(8,128)(2,1)S(1)}) custom-call(s32[2]{0:T(128)S(1)} %pad_add_fusion.at_ref, bf16[16,128,1152]{2,1,0:T(8,128)(2,1)} %three_ref.3), custom_call_target="tpu_custom_call" | custom-call | bytes 7667712 | tf_op jit(solution)/shard_map/pallas_call | solution.py:425
  23.3 1.6 %collective-permute-start.8 = (bf16[384,1152]{1,0:T(8,128)(2,1)S(1)}, bf16[384,1152]{1,0:T(8,128)(2,1)S(1)}, u32[]{:S(2)}, u32[]{:S(2)}) collective-permute-start(bf16[384,1152]{1,0:T(8,128)(2,1)S(1)} %bitcast.12), channel_id=1, source_target_pairs={{0,1},{1,0},{2,3},{3,2},{4,5},{5,4},{6,7},{7,6},{8,9},{9,8},{10,11... | collective-permute-start | bytes 2654216 | tf_op jit(solution)/shard_map/ppermute | solution.py:34
  24.8 0.0 collective-permute-done.3.refs_3_
  24.8 0.2 collective-permute-start.5
  25.1 0.7 shard_map.77
  25.7 0.5 collective-permute-start
  26.3 26.6 %collective-permute-done.theirs_ref = f32[16,64]{1,0:T(8,128)S(1)} collective-permute-done((f32[16,64]{1,0:T(8,128)S(1)}, f32[16,64]{1,0:T(8,128)S(1)}, u32[]{:S(2)}, u32[]{:S(2)}) %collective-permute-start) | collective-permute-done | bytes 4128 | tf_op jit(solution)/shard_map/ppermute | solution.py:34
  52.8 1.9 %collective-permute-start.6 = (bf16[256,1152]{1,0:T(8,128)(2,1)S(1)}, bf16[256,1152]{1,0:T(8,128)(2,1)S(1)}, u32[]{:S(2)}, u32[]{:S(2)}) collective-permute-start(bf16[256,1152]{1,0:T(8,128)(2,1)S(1)} %bitcast.13), channel_id=1, source_target_pairs={{0,1},{1,0},{2,3},{3,2},{4,5},{5,4},{6,7},{7,6},{8,9},{9,8},{10,11... | collective-permute-start | bytes 1769480 | tf_op jit(solution)/shard_map/ppermute | solution.py:34
  54.8 0.4 shard_map.78.mixed_ref
  55.2 0.0 collective-permute-done.5.refs_5_
  55.2 0.1 collective-permute-start.15
  55.3 4.9 %shard_map.81 = (bf16[1152,1152]{1,0:T(8,128)(2,1)S(1)}, bf16[1024,1152]{1,0:T(8,128)(2,1)S(1)}) custom-call(s32[2]{0:T(128)S(1)} %pad_add_fusion.at_ref, s32[16]{0:T(128)S(1)} %copy-done.3, bf16[128,1152]{1,0:T(8,128)(2,1)S(1)} %copy-done.1, bf16[128,1152]{1,0:T(8,128)(2,1)S(1)} %collective-permute-done.1.mid_ref.refs_1_, ...), custom_call_target="tpu_custom_call" | custom-call | flops 2717908992 | bytes 9666632 | tf_op jit(solution)/shard_map/pallas_call | solution.py:47
  60.2 2.1 %shard_map.83 = (bf16[384,1152]{1,0:T(8,128)(2,1)S(1)}, bf16[768,1152]{1,0:T(8,128)(2,1)S(1)}) custom-call(bf16[256,256]{1,0:T(8,128)(2,1)S(1)} %shard_map.78.mixed_ref, bf16[1152,1152]{1,0:T(8,128)(2,1)S(1)} %get-tuple-element.39.v_ref, bf16[384,1152]{1,0:T(8,128)(2,1)S(1)} %collective-permute-done.7.s_ref.refs_0_, ...), custom_call_target="tpu_custom_call" | custom-call | flops 2038431744 | bytes 8683520 | tf_op jit(solution)/shard_map/pallas_call | solution.py:47
  62.3 0.0 collective-permute-done.8.s_ref.refs_1_.refs_2_
  62.3 2.1 %shard_map.84 = (bf16[384,1152]{1,0:T(8,128)(2,1)S(1)}, bf16[768,1152]{1,0:T(8,128)(2,1)S(1)}) custom-call(bf16[256,256]{1,0:T(8,128)(2,1)S(1)} %shard_map.78.mixed_ref, bf16[1152,1152]{1,0:T(8,128)(2,1)S(1)} %get-tuple-element.39.v_ref, bf16[384,1152]{1,0:T(8,128)(2,1)S(1)} %collective-permute-done.8.s_ref.refs_1_.refs_2_, ...), custom_call_target="tpu_custom_call" | custom-call | flops 2038431744 | bytes 8683520 | tf_op jit(solution)/shard_map/pallas_call | solution.py:47
  64.4 4.8 %shard_map.85.early_ref = f32[1152,1152]{1,0:T(8,128)S(1)} custom-call(bf16[1024,1152]{1,0:T(8,128)(2,1)S(1)} %bitcast.7, bf16[384,1152]{1,0:T(8,128)(2,1)S(1)} %collective-permute-done.7.s_ref.refs_0_, bf16[384,1152]{1,0:T(8,128)(2,1)S(1)} %collective-permute-done.8.s_ref.refs_1_.refs_2_, bf16[768,1152]{1,0:T(8,128)(2,1)S(1)} %get-tuple-element.43.refs_2_, ...), custom_call_target="tpu_custom_call" | custom-call | flops 4076863488 | bytes 12976128 | tf_op jit(solution)/shard_map/pallas_call | solution.py:47
  69.3 0.0 collective-permute-done.6.s_ref.refs_0_
  69.3 2.6 %shard_map.86 = (bf16[256,1152]{1,0:T(8,128)(2,1)S(1)}, bf16[512,1152]{1,0:T(8,128)(2,1)S(1)}, bf16[4,128,1024]{2,1,0:T(8,128)(2,1)S(1)}) custom-call(s32[2]{0:T(128)S(1)} %pad_add_fusion.at_ref, s32[16]{0:T(128)S(1)} %copy-done.3, bf16[256,256]{1,0:T(8,128)(2,1)S(1)} %shard_map.78.mixed_ref, bf16[1152,1152]{1,0:T(8,128)(2,1)S(1)} %get-tuple-element.39.v_ref, ...), custom_call_target="tpu_custom_call" | custom-call | flops 1358954496 | bytes 16220232 | tf_op jit(solution)/shard_map/pallas_call | solution.py:47
  71.9 0.5 collective-permute-start.9
  72.5 0.0 collective-permute-done.15.mid_ref.refs_1_
  72.5 0.6 shard_map.90
  73.1 3.4 %collective-permute-start.16 = (bf16[128,1920]{1,0:T(8,128)(2,1)S(1)}, bf16[128,1920]{1,0:T(8,128)(2,1)S(1)}, u32[]{:S(2)}, u32[]{:S(2)}) collective-permute-start(bf16[128,1920]{1,0:T(8,128)(2,1)S(1)} %get-tuple-element.59), channel_id=1, source_target_pairs={{0,4},{4,8},{8,12},{12,16},{16,20},{20,24},{24,28},{6,2},{10,6},{1... | collective-permute-start | bytes 1474568 | tf_op jit(solution)/shard_map/ppermute | solution.py:440
  76.6 3.5 %collective-permute-start.17 = (bf16[128,1408]{1,0:T(8,128)(2,1)S(1)}, bf16[128,1408]{1,0:T(8,128)(2,1)S(1)}, u32[]{:S(2)}, u32[]{:S(2)}) collective-permute-start(bf16[128,1408]{1,0:T(8,128)(2,1)S(1)} %get-tuple-element.60), channel_id=1, source_target_pairs={{0,8},{4,12},{8,16},{12,20},{16,24},{20,28},{10,2},{14,6},{18,10},... | collective-permute-start | bytes 1081352 | tf_op jit(solution)/shard_map/ppermute | solution.py:440
  80.0 8.1 %collective-permute-done.16.refs_2_ = bf16[128,1920]{1,0:T(8,128)(2,1)S(1)} collective-permute-done((bf16[128,1920]{1,0:T(8,128)(2,1)S(1)}, bf16[128,1920]{1,0:T(8,128)(2,1)S(1)}, u32[]{:S(2)}, u32[]{:S(2)}) %collective-permute-start.16) | collective-permute-done | bytes 491552 | tf_op jit(solution)/shard_map/ppermute | solution.py:440
  88.1 0.5 collective-permute-start.19
  88.6 1.6 %shard_map.87 = (f32[128,1152]{1,0:T(8,128)S(1)}, f32[128,1024]{1,0:T(8,128)S(1)}, f32[128,1024]{1,0:T(8,128)S(1)}, f32[128,768]{1,0:T(8,128)S(1)}, f32[128,768]{1,0:T(8,128)S(1)}) custom-call(s32[2]{0:T(128)S(1)} %pad_add_fusion.at_ref, s32[16]{0:T(128)S(1)} %copy-done.3, bf16[1024,1152]{1,0:T(8,128)(2,1)S(1)} %bitcast.9, ...), custom_call_target="tpu_custom_call" | custom-call | flops 679477248 | bytes 11862088 | tf_op jit(solution)/shard_map/pallas_call | solution.py:47
  90.2 0.0 collective-permute-done.9.pack_ref
  90.2 1.1 shard_map.88
  91.3 4.4 %collective-permute-start.10 = (bf16[128,1024]{1,0:T(8,128)(2,1)S(1)}, bf16[128,1024]{1,0:T(8,128)(2,1)S(1)}, u32[]{:S(2)}, u32[]{:S(2)}) collective-permute-start(bf16[128,1024]{1,0:T(8,128)(2,1)S(1)} %get-tuple-element.53), channel_id=1, source_target_pairs={{0,4},{2,6},{4,8},{6,10},{8,12},{10,14},{12,16},{14,18},{16,20},{1... | collective-permute-start | bytes 786440 | tf_op jit(solution)/shard_map/ppermute | solution.py:30
  95.7 1.3 collective-permute-start.11
  97.0 0.0 collective-permute-done.19.refs_5_
  97.0 4.7 %shard_map.91 = (bf16[1152,1152]{1,0:T(8,128)(2,1)S(1)}, bf16[1024,1152]{1,0:T(8,128)(2,1)S(1)}) custom-call(s32[2]{0:T(128)S(1)} %pad_add_fusion.at_ref, s32[16]{0:T(128)S(1)} %copy-done.3, bf16[128,1152]{1,0:T(8,128)(2,1)S(1)} %copy-done.2, bf16[128,1152]{1,0:T(8,128)(2,1)S(1)} %collective-permute-done.15.mid_ref.refs_1_, ...), custom_call_target="tpu_custom_call" | custom-call | flops 2717908992 | bytes 9666632 | tf_op jit(solution)/shard_map/pallas_call | solution.py:47
  101.7 4.5 %collective-permute-start.12 = (bf16[128,768]{1,0:T(8,128)(2,1)S(1)}, bf16[128,768]{1,0:T(8,128)(2,1)S(1)}, u32[]{:S(2)}, u32[]{:S(2)}) collective-permute-start(bf16[128,768]{1,0:T(8,128)(2,1)S(1)} %get-tuple-element.55), channel_id=1, source_target_pairs={{0,8},{2,10},{4,12},{6,14},{8,16},{10,18},{12,20},{14,22},{16,24},... | collective-permute-start | bytes 589832 | tf_op jit(solution)/shard_map/ppermute | solution.py:30
  106.3 1.3 collective-permute-start.13
  107.6 4.8 %shard_map.92.gram_ref = f32[256,256]{1,0:T(8,128)S(1)} custom-call(bf16[1152,1152]{1,0:T(8,128)(2,1)S(1)} %get-tuple-element.61.x_ref, bf16[1024,1152]{1,0:T(8,128)(2,1)S(1)} %get-tuple-element.62.co_ref, bf16[1024,1152]{1,0:T(8,128)(2,1)S(1)} %get-tuple-element.41.po_ref, bf16[384,1152]{1,0:T(8,128)(2,1)S(1)} %collective-permute-done.7.s_ref.refs_0_, ...), custom_call_target="tpu_custom_call" | custom-call | flops 2038431744 | bytes 11173888 | tf_op jit(solution)/shard_map/pallas_call | solution.py:47
  112.4 2.6 %shard_map.93 = f32[32,32]{1,0:T(8,128)S(1)} custom-call(s32[2]{0:T(128)S(1)} %pad_add_fusion.at_ref, bf16[1152,1152]{1,0:T(8,128)(2,1)S(1)} %get-tuple-element.61.x_ref, bf16[1024,1152]{1,0:T(8,128)(2,1)S(1)} %get-tuple-element.62.co_ref, bf16[1024,1152]{1,0:T(8,128)(2,1)S(1)} %get-tuple-element.41.po_ref, f32[256,256]{1,0:T(8,128)S(1)} %shard_map.92.gram_ref, ...), custom_call_target="tpu_custom_call" | custom-call | flops 679477248 | bytes 8826888 | tf_op jit(solution)/shard_map/pallas_call | solution.py:47
  115.0 2.7 %collective-permute-start.20 = (f32[32,32]{1,0:T(8,128)S(1)}, f32[32,32]{1,0:T(8,128)S(1)}, u32[]{:S(2)}, u32[]{:S(2)}) collective-permute-start(f32[32,32]{1,0:T(8,128)S(1)} %shard_map.93), channel_id=1, source_target_pairs={{0,8},{2,10},{4,12},{6,14},{8,0},{10,2},{12,4},{14,6},{16,24},{18,... | collective-permute-start | bytes 12296 | tf_op jit(solution)/shard_map/ppermute | solution.py:34
  117.7 1.7 %collective-permute-done.20 = f32[32,32]{1,0:T(8,128)S(1)} collective-permute-done((f32[32,32]{1,0:T(8,128)S(1)}, f32[32,32]{1,0:T(8,128)S(1)}, u32[]{:S(2)}, u32[]{:S(2)}) %collective-permute-start.20) | collective-permute-done | bytes 4128 | tf_op jit(solution)/shard_map/ppermute | solution.py:34
  119.4 0.5 collective-permute-start.21
  119.9 0.7 shard_map.89
  120.6 1.6 %collective-permute-start.14 = (bf16[64,1152]{1,0:T(8,128)(2,1)S(1)}, bf16[64,1152]{1,0:T(8,128)(2,1)S(1)}, u32[]{:S(2)}, u32[]{:S(2)}) collective-permute-start(bf16[64,1152]{1,0:T(8,128)(2,1)S(1)} %get-tuple-element.58), channel_id=1, source_target_pairs={{0,1},{1,0},{2,3},{3,2},{4,5},{5,4},{6,7},{7,6},{8,9},{9,8},{10,11... | collective-permute-start | bytes 442376 | tf_op jit(solution)/shard_map/ppermute | solution.py:34
  122.2 0.8 collective-permute-done.21
  123.1 1.2 collective-permute-done.22
  124.2 1.6 %collective-permute-start.23 = (f32[16,32]{1,0:T(8,128)S(1)}, f32[16,32]{1,0:T(8,128)S(1)}, u32[]{:S(2)}, u32[]{:S(2)}) collective-permute-start(f32[16,32]{1,0:T(8,128)S(1)} %add.14), channel_id=1, source_target_pairs={{0,4},{2,6},{4,0},{6,2},{8,12},{10,14},{12,8},{14,10},{16,20},{18,... | collective-permute-start | bytes 6152 | tf_op jit(solution)/shard_map/ppermute | solution.py:34
  125.8 2.1 %collective-permute-done.23 = f32[16,32]{1,0:T(8,128)S(1)} collective-permute-done((f32[16,32]{1,0:T(8,128)S(1)}, f32[16,32]{1,0:T(8,128)S(1)}, u32[]{:S(2)}, u32[]{:S(2)}) %collective-permute-start.23) | collective-permute-done | bytes 2080 | tf_op jit(solution)/shard_map/ppermute | solution.py:34
  127.9 2.5 %collective-permute-start.24 = (f32[16,32]{1,0:T(8,128)S(1)}, f32[16,32]{1,0:T(8,128)S(1)}, u32[]{:S(2)}, u32[]{:S(2)}) collective-permute-start(f32[16,32]{1,0:T(8,128)S(1)} %add.15.pk_ref), channel_id=1, source_target_pairs={{0,16},{2,18},{4,20},{6,22},{8,24},{10,26},{12,28},{14,30},{16,0},... | collective-permute-start | bytes 6152 | tf_op jit(solution)/shard_map/ppermute | solution.py:34
  130.4 2.1 %collective-permute-done.24.pg_ref = f32[16,32]{1,0:T(8,128)S(1)} collective-permute-done((f32[16,32]{1,0:T(8,128)S(1)}, f32[16,32]{1,0:T(8,128)S(1)}, u32[]{:S(2)}, u32[]{:S(2)}) %collective-permute-start.24) | collective-permute-done | bytes 2080 | tf_op jit(solution)/shard_map/ppermute | solution.py:34
  132.5 1.3 shard_map.94
  (22 shorter events, 0.1 us)
Async XLA Ops:
  0.6 2.0 %collective-permute-start.1 = (bf16[128,1152]{1,0:T(8,128)(2,1)}, bf16[128,1152]{1,0:T(8,128)(2,1)S(1)}, u32[]{:S(2)}, u32[]{:S(2)}) collective-permute-start(bf16[128,1152]{1,0:T(8,128)(2,1)} %refs_0_.2), channel_id=1, source_target_pairs={{0,2},{2,0},{4,6},{6,4},{8,10},{10,8},{12,14},{14,12},{16,18},{18,... | collective-permute-start | bytes 884744 | tf_op jit(solution)/shard_map/ppermute | solution.py:34
  2.6 1.0 copy-start
  4.2 16.4 %collective-permute-start.2 = (bf16[128,1920]{1,0:T(8,128)(2,1)S(1)}, bf16[128,1920]{1,0:T(8,128)(2,1)S(1)}, u32[]{:S(2)}, u32[]{:S(2)}) collective-permute-start(bf16[128,1920]{1,0:T(8,128)(2,1)S(1)} %get-tuple-element.36), channel_id=1, source_target_pairs={{0,4},{4,8},{8,12},{12,16},{16,20},{20,24},{24,28},{6,2},{10,6},{1... | collective-permute-start | bytes 1474568 | tf_op jit(solution)/shard_map/ppermute | solution.py:440
  9.0 15.8 %collective-permute-start.3 = (bf16[128,1408]{1,0:T(8,128)(2,1)S(1)}, bf16[128,1408]{1,0:T(8,128)(2,1)S(1)}, u32[]{:S(2)}, u32[]{:S(2)}) collective-permute-start(bf16[128,1408]{1,0:T(8,128)(2,1)S(1)} %get-tuple-element.37), channel_id=1, source_target_pairs={{0,8},{4,12},{8,16},{12,20},{16,24},{20,28},{10,2},{14,6},{18,10},... | collective-permute-start | bytes 1081352 | tf_op jit(solution)/shard_map/ppermute | solution.py:440
  14.2 10.9 %copy-start.4 = (bf16[16,32]{1,0:T(8,128)(2,1)S(1)}, bf16[16,32]{1,0:T(8,128)(2,1)}, u32[]{:S(2)}) copy-start(bf16[16,32]{1,0:T(8,128)(2,1)} %k_ref.1) | copy-start | bytes 3076
  14.2 10.9 %copy-start.5 = (s32[16]{0:T(128)S(1)}, s32[16]{0:T(128)}, u32[]{:S(2)}) copy-start(s32[16]{0:T(128)} %atom_ref.1) | copy-start | bytes 196
  14.2 40.9 %copy-start.2 = (bf16[128,1152]{1,0:T(8,128)(2,1)S(1)}, bf16[128,1152]{1,0:T(8,128)(2,1)}, u32[]{:S(2)}) copy-start(bf16[128,1152]{1,0:T(8,128)(2,1)} %refs_0_.3) | copy-start | bytes 884740
  14.2 41.0 %copy-start.1 = (bf16[128,1152]{1,0:T(8,128)(2,1)S(1)}, bf16[128,1152]{1,0:T(8,128)(2,1)}, u32[]{:S(2)}) copy-start(bf16[128,1152]{1,0:T(8,128)(2,1)} %refs_0_.2) | copy-start | bytes 884740
  14.3 41.0 %copy-start.3 = (s32[16]{0:T(128)S(1)}, s32[16]{0:T(128)}, u32[]{:S(2)}) copy-start(s32[16]{0:T(128)} %prof_ref.9) | copy-start | bytes 196
  14.3 45.9 %collective-permute-start.7 = (bf16[384,1152]{1,0:T(8,128)(2,1)S(1)}, bf16[384,1152]{1,0:T(8,128)(2,1)S(1)}, u32[]{:S(2)}, u32[]{:S(2)}) collective-permute-start(bf16[384,1152]{1,0:T(8,128)(2,1)S(1)} %bitcast.11), channel_id=1, source_target_pairs={{0,1},{1,0},{2,3},{3,2},{4,5},{5,4},{6,7},{7,6},{8,9},{9,8},{10,11... | collective-permute-start | bytes 2654216 | tf_op jit(solution)/shard_map/ppermute | solution.py:34
  20.6 34.7 %collective-permute-start.4 = (bf16[128,1920]{1,0:T(8,128)(2,1)S(1)}, bf16[128,1920]{1,0:T(8,128)(2,1)S(1)}, u32[]{:S(2)}, u32[]{:S(2)}) collective-permute-start(bf16[128,1920]{1,0:T(8,128)(2,1)S(1)} %collective-permute-done.2.refs_2_), channel_id=1, source_target_pairs={{0,2},{2,0},{4,6},{6,4},{8,10},{10,8},{12,14},{14,12},{16,18},{18,... | collective-permute-start | bytes 1474568 | tf_op jit(solution)/shard_map/ppermute | solution.py:34
  23.3 39.0 %collective-permute-start.8 = (bf16[384,1152]{1,0:T(8,128)(2,1)S(1)}, bf16[384,1152]{1,0:T(8,128)(2,1)S(1)}, u32[]{:S(2)}, u32[]{:S(2)}) collective-permute-start(bf16[384,1152]{1,0:T(8,128)(2,1)S(1)} %bitcast.12), channel_id=1, source_target_pairs={{0,1},{1,0},{2,3},{3,2},{4,5},{5,4},{6,7},{7,6},{8,9},{9,8},{10,11... | collective-permute-start | bytes 2654216 | tf_op jit(solution)/shard_map/ppermute | solution.py:34
  24.8 30.3 %collective-permute-start.5 = (bf16[128,1408]{1,0:T(8,128)(2,1)S(1)}, bf16[128,1408]{1,0:T(8,128)(2,1)S(1)}, u32[]{:S(2)}, u32[]{:S(2)}) collective-permute-start(bf16[128,1408]{1,0:T(8,128)(2,1)S(1)} %collective-permute-done.3.refs_3_), channel_id=1, source_target_pairs={{0,2},{2,0},{4,6},{6,4},{8,10},{10,8},{12,14},{14,12},{16,18},{18,... | collective-permute-start | bytes 1081352 | tf_op jit(solution)/shard_map/ppermute | solution.py:34
  25.7 27.1 %collective-permute-start = (f32[16,64]{1,0:T(8,128)S(1)}, f32[16,64]{1,0:T(8,128)S(1)}, u32[]{:S(2)}, u32[]{:S(2)}) collective-permute-start(f32[16,64]{1,0:T(8,128)S(1)} %get-tuple-element.35), channel_id=1, source_target_pairs={{0,1},{1,0},{2,3},{3,2},{4,5},{5,4},{6,7},{7,6},{8,9},{9,8},{10,11... | collective-permute-start | bytes 12296 | tf_op jit(solution)/shard_map/ppermute | solution.py:34
  52.8 16.5 %collective-permute-start.6 = (bf16[256,1152]{1,0:T(8,128)(2,1)S(1)}, bf16[256,1152]{1,0:T(8,128)(2,1)S(1)}, u32[]{:S(2)}, u32[]{:S(2)}) collective-permute-start(bf16[256,1152]{1,0:T(8,128)(2,1)S(1)} %bitcast.13), channel_id=1, source_target_pairs={{0,1},{1,0},{2,3},{3,2},{4,5},{5,4},{6,7},{7,6},{8,9},{9,8},{10,11... | collective-permute-start | bytes 1769480 | tf_op jit(solution)/shard_map/ppermute | solution.py:34
  55.2 17.3 %collective-permute-start.15 = (bf16[128,1152]{1,0:T(8,128)(2,1)S(1)}, bf16[128,1152]{1,0:T(8,128)(2,1)S(1)}, u32[]{:S(2)}, u32[]{:S(2)}) collective-permute-start(bf16[128,1152]{1,0:T(8,128)(2,1)S(1)} %copy-done.2), channel_id=1, source_target_pairs={{0,2},{2,0},{4,6},{6,4},{8,10},{10,8},{12,14},{14,12},{16,18},{18,... | collective-permute-start | bytes 884744 | tf_op jit(solution)/shard_map/ppermute | solution.py:34
  71.9 18.3 %collective-permute-start.9 = (bf16[4,128,1024]{2,1,0:T(8,128)(2,1)S(1)}, bf16[4,128,1024]{2,1,0:T(8,128)(2,1)S(1)}, u32[]{:S(2)}, u32[]{:S(2)}) collective-permute-start(bf16[4,128,1024]{2,1,0:T(8,128)(2,1)S(1)} %get-tuple-element.45), channel_id=1, source_target_pairs={{0,2},{2,0},{4,6},{6,4},{8,10},{10,8},{12,14},{14,12},{16,18},{18,... | collective-permute-start | bytes 3145736 | tf_op jit(solution)/shard_map/ppermute | solution.py:34
  73.1 15.0 %collective-permute-start.16 = (bf16[128,1920]{1,0:T(8,128)(2,1)S(1)}, bf16[128,1920]{1,0:T(8,128)(2,1)S(1)}, u32[]{:S(2)}, u32[]{:S(2)}) collective-permute-start(bf16[128,1920]{1,0:T(8,128)(2,1)S(1)} %get-tuple-element.59), channel_id=1, source_target_pairs={{0,4},{4,8},{8,12},{12,16},{16,20},{20,24},{24,28},{6,2},{10,6},{1... | collective-permute-start | bytes 1474568 | tf_op jit(solution)/shard_map/ppermute | solution.py:440
  76.6 11.5 %collective-permute-start.17 = (bf16[128,1408]{1,0:T(8,128)(2,1)S(1)}, bf16[128,1408]{1,0:T(8,128)(2,1)S(1)}, u32[]{:S(2)}, u32[]{:S(2)}) collective-permute-start(bf16[128,1408]{1,0:T(8,128)(2,1)S(1)} %get-tuple-element.60), channel_id=1, source_target_pairs={{0,8},{4,12},{8,16},{12,20},{16,24},{20,28},{10,2},{14,6},{18,10},... | collective-permute-start | bytes 1081352 | tf_op jit(solution)/shard_map/ppermute | solution.py:440
  88.1 8.9 %collective-permute-start.18 = (bf16[128,1920]{1,0:T(8,128)(2,1)S(1)}, bf16[128,1920]{1,0:T(8,128)(2,1)S(1)}, u32[]{:S(2)}, u32[]{:S(2)}) collective-permute-start(bf16[128,1920]{1,0:T(8,128)(2,1)S(1)} %collective-permute-done.16.refs_2_), channel_id=1, source_target_pairs={{0,2},{2,0},{4,6},{6,4},{8,10},{10,8},{12,14},{14,12},{16,18},{18,... | collective-permute-start | bytes 1474568 | tf_op jit(solution)/shard_map/ppermute | solution.py:34
  88.1 8.9 %collective-permute-start.19 = (bf16[128,1408]{1,0:T(8,128)(2,1)S(1)}, bf16[128,1408]{1,0:T(8,128)(2,1)S(1)}, u32[]{:S(2)}, u32[]{:S(2)}) collective-permute-start(bf16[128,1408]{1,0:T(8,128)(2,1)S(1)} %collective-permute-done.17.refs_3_), channel_id=1, source_target_pairs={{0,2},{2,0},{4,6},{6,4},{8,10},{10,8},{12,14},{14,12},{16,18},{18,... | collective-permute-start | bytes 1081352 | tf_op jit(solution)/shard_map/ppermute | solution.py:34
  91.3 28.6 %collective-permute-start.10 = (bf16[128,1024]{1,0:T(8,128)(2,1)S(1)}, bf16[128,1024]{1,0:T(8,128)(2,1)S(1)}, u32[]{:S(2)}, u32[]{:S(2)}) collective-permute-start(bf16[128,1024]{1,0:T(8,128)(2,1)S(1)} %get-tuple-element.53), channel_id=1, source_target_pairs={{0,4},{2,6},{4,8},{6,10},{8,12},{10,14},{12,16},{14,18},{16,20},{1... | collective-permute-start | bytes 786440 | tf_op jit(solution)/shard_map/ppermute | solution.py:30
  95.7 24.2 %collective-permute-start.11 = (bf16[128,1024]{1,0:T(8,128)(2,1)S(1)}, bf16[128,1024]{1,0:T(8,128)(2,1)S(1)}, u32[]{:S(2)}, u32[]{:S(2)}) collective-permute-start(bf16[128,1024]{1,0:T(8,128)(2,1)S(1)} %get-tuple-element.54), channel_id=1, source_target_pairs={{4,0},{6,2},{8,4},{10,6},{12,8},{14,10},{16,12},{18,14},{20,16},{2... | collective-permute-start | bytes 786440 | tf_op jit(solution)/shard_map/ppermute | solution.py:30
  101.7 18.2 %collective-permute-start.12 = (bf16[128,768]{1,0:T(8,128)(2,1)S(1)}, bf16[128,768]{1,0:T(8,128)(2,1)S(1)}, u32[]{:S(2)}, u32[]{:S(2)}) collective-permute-start(bf16[128,768]{1,0:T(8,128)(2,1)S(1)} %get-tuple-element.55), channel_id=1, source_target_pairs={{0,8},{2,10},{4,12},{6,14},{8,16},{10,18},{12,20},{14,22},{16,24},... | collective-permute-start | bytes 589832 | tf_op jit(solution)/shard_map/ppermute | solution.py:30
  106.3 13.6 %collective-permute-start.13 = (bf16[128,768]{1,0:T(8,128)(2,1)S(1)}, bf16[128,768]{1,0:T(8,128)(2,1)S(1)}, u32[]{:S(2)}, u32[]{:S(2)}) collective-permute-start(bf16[128,768]{1,0:T(8,128)(2,1)S(1)} %get-tuple-element.56), channel_id=1, source_target_pairs={{8,0},{10,2},{12,4},{14,6},{16,8},{18,10},{20,12},{22,14},{24,16},... | collective-permute-start | bytes 589832 | tf_op jit(solution)/shard_map/ppermute | solution.py:30
  115.0 4.4 %collective-permute-start.20 = (f32[32,32]{1,0:T(8,128)S(1)}, f32[32,32]{1,0:T(8,128)S(1)}, u32[]{:S(2)}, u32[]{:S(2)}) collective-permute-start(f32[32,32]{1,0:T(8,128)S(1)} %shard_map.93), channel_id=1, source_target_pairs={{0,8},{2,10},{4,12},{6,14},{8,0},{10,2},{12,4},{14,6},{16,24},{18,... | collective-permute-start | bytes 12296 | tf_op jit(solution)/shard_map/ppermute | solution.py:34
  119.4 3.7 %collective-permute-start.21 = (f32[16,32]{1,0:T(8,128)S(1)}, f32[16,32]{1,0:T(8,128)S(1)}, u32[]{:S(2)}, u32[]{:S(2)}) collective-permute-start(f32[16,32]{1,0:T(8,128)S(1)} %slice.9), channel_id=1, source_target_pairs={{0,1},{1,0},{2,3},{3,2},{4,5},{5,4},{6,7},{7,6},{8,9},{9,8},{10,11... | collective-permute-start | bytes 6152 | tf_op jit(solution)/shard_map/ppermute | solution.py:34
  120.6 11.9 %collective-permute-start.14 = (bf16[64,1152]{1,0:T(8,128)(2,1)S(1)}, bf16[64,1152]{1,0:T(8,128)(2,1)S(1)}, u32[]{:S(2)}, u32[]{:S(2)}) collective-permute-start(bf16[64,1152]{1,0:T(8,128)(2,1)S(1)} %get-tuple-element.58), channel_id=1, source_target_pairs={{0,1},{1,0},{2,3},{3,2},{4,5},{5,4},{6,7},{7,6},{8,9},{9,8},{10,11... | collective-permute-start | bytes 442376 | tf_op jit(solution)/shard_map/ppermute | solution.py:34
  123.1 1.2 collective-permute-start.22
  124.2 3.7 %collective-permute-start.23 = (f32[16,32]{1,0:T(8,128)S(1)}, f32[16,32]{1,0:T(8,128)S(1)}, u32[]{:S(2)}, u32[]{:S(2)}) collective-permute-start(f32[16,32]{1,0:T(8,128)S(1)} %add.14), channel_id=1, source_target_pairs={{0,4},{2,6},{4,0},{6,2},{8,12},{10,14},{12,8},{14,10},{16,20},{18,... | collective-permute-start | bytes 6152 | tf_op jit(solution)/shard_map/ppermute | solution.py:34
  127.9 4.5 %collective-permute-start.24 = (f32[16,32]{1,0:T(8,128)S(1)}, f32[16,32]{1,0:T(8,128)S(1)}, u32[]{:S(2)}, u32[]{:S(2)}) collective-permute-start(f32[16,32]{1,0:T(8,128)S(1)} %add.15.pk_ref), channel_id=1, source_target_pairs={{0,16},{2,18},{4,20},{6,22},{8,24},{10,26},{12,28},{14,30},{16,0},... | collective-permute-start | bytes 6152 | tf_op jit(solution)/shard_map/ppermute | solution.py:34

commit v3 on v2

--- a/solution.py
+++ b/solution.py
@@ -22,12 +22,6 @@
 
 def columns_to(offset):
     return 6 if abs(offset) == 4 else 8
-
-
-def passed_along(block, axis, distance):
-    devices = range(lax.axis_size(axis))
-    route = [(i - distance, i) for i in devices if i - distance in devices]
-    return lax.ppermute(block, axis, route)
 
 
 def swapped(block, axis, bit=1):
@@ -223,18 +217,16 @@
         resp_ref[span + g * half : span + (g + 1) * half, :] = resp[half:]
 
 
-def early_kernel(spans, so_ref, *refs):
-    count = len(spans)
+def early_kernel(rows, so_ref, s_ref, resp_ref, *refs):
     out_ref = refs[-1]
     third = out_ref.shape[0] // 3
     for m in range(3):
         cols = slice(m * third, (m + 1) * third)
-        acc = None
-        for rows, s_ref, resp_ref in zip(spans, refs[:count], refs[count:]):
-            both = jnp.concatenate([so_ref[rows, cols], s_ref[:, cols]], 0)
-            part = dot_rows(both, resp_ref[...])
-            acc = part if acc is None else acc + part
-        out_ref[cols, :] = acc
+        both = jnp.concatenate([so_ref[rows, cols], s_ref[:, cols]], 0)
+        part = dot_rows(both, resp_ref[...])
+        for before_ref in refs[:-1]:
+            part = part + before_ref[cols, :]
+        out_ref[cols, :] = part
 
 
 def terms_of(offsets, first, early_ref, so_ref, sr_ref, resp_ref, block):
@@ -287,25 +279,38 @@
             out[:, c * block : (c + 1) * block] = tile
 
 
+def upward_first(position, distance):
+    return lax.rem(position // distance, 2) == 0
+
+
 def combine_kernel(at_ref, pack_ref, own_ref, u2_ref, d2_ref, u4_ref, d4_ref, *outs):
+    mid_ref, first2_ref, second2_ref, first4_ref, second4_ref = outs
     block = own_ref.shape[0]
     ins = {0: own_ref, 2: u2_ref, -2: d2_ref, 4: u4_ref, -4: d4_ref}
-    to = dict(zip((0, 2, -2, 4, -4), outs))
-    odd = lax.rem(at_ref[0], 2) == 1
+    position = at_ref[0]
+    odd = lax.rem(position, 2) == 1
 
     def merge(sources):
-        for offset, out in to.items():
+        def tile_of(offset, c):
             first = 0 if offset == 0 else FIRST_COLUMN[offset]
-            for c in range(out.shape[1] // block):
+            value = ins[offset][:, c * block : (c + 1) * block]
+            if offset in sources:
+                n = sources[offset]
+                at = c + first - FIRST_COLUMN[ODD[n]]
+                if 0 <= at < 8:
+                    value = value + pack_ref[n, :, at * block : (at + 1) * block].astype(F32)
+            return value
+
+        for c in range(SLOTS):
+            mid_ref[:, c * block : (c + 1) * block] = tile_of(0, c)
+        for distance, out1, out2 in ((2, first2_ref, second2_ref), (4, first4_ref, second4_ref)):
+            upward = upward_first(position, distance)
+            for c in range(out1.shape[1] // block):
                 columns = slice(c * block, (c + 1) * block)
-                value = ins[offset][:, columns]
-                if offset in sources:
-                    n = sources[offset]
-                    at = c + first - FIRST_COLUMN[ODD[n]]
-                    if 0 <= at < 8:
-                        tile = pack_ref[n, :, at * block : (at + 1) * block]
-                        value = value + tile.astype(F32)
-                out[:, columns] = value.astype(out.dtype)
+                up = tile_of(distance, c)
+                down = tile_of(-distance, c)
+                out1[:, columns] = jnp.where(upward, up, down).astype(BF16)
+                out2[:, columns] = jnp.where(upward, down, up).astype(BF16)
 
     @pl.when(jnp.logical_not(odd))
     def _():
@@ -316,20 +321,24 @@
         merge({-4: 0, -2: 1, 0: 2, 2: 3})
 
 
-def gather_kernel(at_ref, own_ref, u2_ref, d2_ref, u4_ref, d4_ref, keep_ref, send_ref):
+def gather_kernel(at_ref, own_ref, *refs):
+    pieces, (keep_ref, send_ref) = {2: refs[:2], 4: refs[2:4]}, refs[4:]
     block = own_ref.shape[0]
     rows = keep_ref.shape[0]
-    half = at_ref[1]
-    parts = {2: u2_ref, -2: d2_ref, 4: u4_ref, -4: d4_ref}
+    position, half = at_ref[0], at_ref[1]
     for target, which in ((send_ref, 1 - half), (keep_ref, half)):
         window = pl.ds(pl.multiple_of(which * rows, rows), rows)
         for c in range(SLOTS):
             columns = slice(c * block, (c + 1) * block)
             total = own_ref[window, columns]
-            for offset, part in parts.items():
-                at = c - FIRST_COLUMN[offset]
-                if 0 <= at < columns_to(offset):
-                    total = total + part[window, at * block : (at + 1) * block].astype(F32)
+            for distance, (one, two) in pieces.items():
+                upward = upward_first(position, distance)
+                for offset, above, below in ((distance, two, one), (-distance, one, two)):
+                    at = c - FIRST_COLUMN[offset]
+                    if 0 <= at < columns_to(offset):
+                        tile = slice(at * block, (at + 1) * block)
+                        part = jnp.where(upward, above[window, tile], below[window, tile])
+                        total = total + part.astype(F32)
             target[:, columns] = total.astype(target.dtype)
 
 
@@ -480,12 +489,15 @@
         )
         partner_got.append(pr)
         responses.append(resp)
-    (early,) = run(
-        functools.partial(early_kernel, [slice(f, f + n) for f, n in zip(firsts[:2], counts)]),
-        [own, *got[:2], *responses],
-        [shaped((width, width), F32)],
-        flops=2 * firsts[2] * per_row,
-    )
+    early = []
+    for c in range(2):
+        early = run(
+            functools.partial(early_kernel, slice(firsts[c], firsts[c] + counts[c])),
+            [own, got[c], responses[c], *early],
+            [shaped((width, width), F32)],
+            flops=2 * counts[c] * per_row,
+        )
+    (early,) = early
     pr, resp, pack = run(
         functools.partial(odd_kernel, nblocks, firsts[2]),
         [at, profile, mixed, vir_stack, got[2], partner_own, own, early],
@@ -514,7 +526,12 @@
         [shaped((block, width), F32)] + [shaped((block, columns_to(d) * block)) for d in offsets],
         smem=1,
     )
-    arrived = [passed_along(s, "chain", d) for s, d in zip(sends, offsets)]
+    arrived = []
+    for n, send in enumerate(sends):
+        distance, parity = (2, 2, 4, 4)[n], n % 2
+        lower = [i for i in range(nblocks - distance) if i // distance % 2 == parity]
+        route = [pair for i in lower for pair in ((i, i + distance), (i + distance, i))]
+        arrived.append(lax.ppermute(send, "chain", route))
     keep, send = run(
         gather_kernel,
         [at, mid, *arrived],

time: 134 us -> 131 us (0.978)
  starting transfers between devices: 43.1 us -> 39 us
    ppermute x4, starting transfers between devices: 11.5 us -> 6.74 us  [step(): arrived.append(lax.ppermute(send, 'chain', route))]
    ppermute x17, waiting for transfers between devices: 35.8 us -> 38.1 us  [swapped(): lax.ppermute(block, axis, [(i, i ^ bit) for i in range(lax.axis_size(axis...]
    pallas_call x16 -> x17, Pallas kernels: 35.6 us -> 35.8 us  [run(): pl.pallas_call(kernel, out_shape=outs, in_specs=[SMEM] * smem + [VMEM] *...]
  transfers between devices with their start and end apart: 25 -> 25, of which waited for: 9 -> 9; matrix products, arithmetic and copies ran while one was open for 0% -> 0% of each run, Pallas kernels for 28% -> 29%
where the time goes in v3:
time: 131 us
  waiting for transfers between devices  49.7 us (38%)
  Pallas kernels  40.2 us (31%)
  starting transfers between devices  39 us (30%)
    ppermute x17, waiting for transfers between devices, swapped(): lax.ppermute(block, axis, [(i, i ^ bit) for i in range(lax.axis_size(axis...  38.1 us
    pallas_call x17, Pallas kernels, run(): pl.pallas_call(kernel, out_shape=outs, in_specs=[SMEM] * smem + [VMEM] *...  35.8 us
    ppermute x17, starting transfers between devices, swapped(): lax.ppermute(block, axis, [(i, i ^ bit) for i in range(lax.axis_size(axis...  16.8 us
    ppermute x4, starting transfers between devices, halo(): hops.append(lax.ppermute(pack, 'chain', up + down))  15.4 us
    ppermute x4, waiting for transfers between devices, halo(): hops.append(lax.ppermute(pack, 'chain', up + down))  11.6 us
    ppermute x4, starting transfers between devices, step(): arrived.append(lax.ppermute(send, 'chain', route))  6.74 us
    pallas_call x2, Pallas kernels, cut(): parts = call(at, integrals)  4.42 us
  transfers between devices with their start and end apart: 25, of which 9 were waited for; matrix products, arithmetic and copies ran while one was open for 0% of the time, Pallas kernels for 29%

profile of v3, /device:TPU:0, one launch (start us, length us, event | category | flops | bytes accessed | tf_op | source)
XLA Modules:
  0.0 130.9 jit_solution(15993730277412574335)
XLA Ops:
  0.6 0.6 collective-permute-start.1
  1.2 0.1 pad_add_fusion.at_ref
  1.3 1.3 %collective-permute-done.1.mid_ref.refs_1_ = bf16[128,1152]{1,0:T(8,128)(2,1)S(1)} collective-permute-done((bf16[128,1152]{1,0:T(8,128)(2,1)}, bf16[128,1152]{1,0:T(8,128)(2,1)S(1)}, u32[]{:S(2)}, u32[]{:S(2)}) %collective-permute-start.1) | collective-permute-done | bytes 294944 | tf_op jit(solution)/shard_map/ppermute | solution.py:28
  2.6 1.0 copy-done
  3.6 0.6 shard_map.79
  4.2 4.8 %collective-permute-start.2 = (bf16[128,1920]{1,0:T(8,128)(2,1)S(1)}, bf16[128,1920]{1,0:T(8,128)(2,1)S(1)}, u32[]{:S(2)}, u32[]{:S(2)}) collective-permute-start(bf16[128,1920]{1,0:T(8,128)(2,1)S(1)} %get-tuple-element.36), channel_id=1, source_target_pairs={{0,4},{4,8},{8,12},{12,16},{16,20},{20,24},{24,28},{6,2},{10,6},{1... | collective-permute-start | bytes 1474568 | tf_op jit(solution)/shard_map/ppermute | solution.py:449
  9.0 3.5 %collective-permute-start.3 = (bf16[128,1408]{1,0:T(8,128)(2,1)S(1)}, bf16[128,1408]{1,0:T(8,128)(2,1)S(1)}, u32[]{:S(2)}, u32[]{:S(2)}) collective-permute-start(bf16[128,1408]{1,0:T(8,128)(2,1)S(1)} %get-tuple-element.37), channel_id=1, source_target_pairs={{0,8},{4,12},{8,16},{12,20},{16,24},{20,28},{10,2},{14,6},{18,10},... | collective-permute-start | bytes 1081352 | tf_op jit(solution)/shard_map/ppermute | solution.py:449
  12.5 2.7 %shard_map.80 = (bf16[3,16,8,1152]{3,2,1,0:T(8,128)(2,1)S(1)}, bf16[2,16,8,1152]{3,2,1,0:T(8,128)(2,1)S(1)}, bf16[8,16,8,1152]{3,2,1,0:T(8,128)(2,1)S(1)}) custom-call(s32[2]{0:T(128)S(1)} %pad_add_fusion.at_ref, bf16[16,128,1152]{2,1,0:T(8,128)(2,1)} %three_ref.3), custom_call_target="tpu_custom_call" | custom-call | bytes 7667712 | tf_op jit(solution)/shard_map/pallas_call | solution.py:434
  15.2 0.0 copy-start.4
  15.2 0.0 copy-start.5
  15.2 0.0 copy-start.2
  15.2 0.0 copy-start.1
  15.3 0.0 copy-start.3
  15.3 1.6 %collective-permute-start.7 = (bf16[384,1152]{1,0:T(8,128)(2,1)S(1)}, bf16[384,1152]{1,0:T(8,128)(2,1)S(1)}, u32[]{:S(2)}, u32[]{:S(2)}) collective-permute-start(bf16[384,1152]{1,0:T(8,128)(2,1)S(1)} %bitcast.13), channel_id=1, source_target_pairs={{0,1},{1,0},{2,3},{3,2},{4,5},{5,4},{6,7},{7,6},{8,9},{9,8},{10,11... | collective-permute-start | bytes 2654216 | tf_op jit(solution)/shard_map/ppermute | solution.py:28
  16.8 3.8 %collective-permute-done.2.refs_2_ = bf16[128,1920]{1,0:T(8,128)(2,1)S(1)} collective-permute-done((bf16[128,1920]{1,0:T(8,128)(2,1)S(1)}, bf16[128,1920]{1,0:T(8,128)(2,1)S(1)}, u32[]{:S(2)}, u32[]{:S(2)}) %collective-permute-start.2) | collective-permute-done | bytes 491552 | tf_op jit(solution)/shard_map/ppermute | solution.py:449
  20.6 0.0 collective-permute-start.4
  20.6 1.7 %shard_map.83 = bf16[3,16,8,1152]{3,2,1,0:T(8,128)(2,1)S(1)} custom-call(s32[2]{0:T(128)S(1)} %pad_add_fusion.at_ref, bf16[16,128,1152]{2,1,0:T(8,128)(2,1)} %three_ref.3), custom_call_target="tpu_custom_call" | custom-call | bytes 1769472 | tf_op jit(solution)/shard_map/pallas_call | solution.py:434
  22.3 1.6 %collective-permute-start.8 = (bf16[384,1152]{1,0:T(8,128)(2,1)S(1)}, bf16[384,1152]{1,0:T(8,128)(2,1)S(1)}, u32[]{:S(2)}, u32[]{:S(2)}) collective-permute-start(bf16[384,1152]{1,0:T(8,128)(2,1)S(1)} %bitcast.12), channel_id=1, source_target_pairs={{0,1},{1,0},{2,3},{3,2},{4,5},{5,4},{6,7},{7,6},{8,9},{9,8},{10,11... | collective-permute-start | bytes 2654216 | tf_op jit(solution)/shard_map/ppermute | solution.py:28
  23.9 0.0 collective-permute-done.3.refs_3_
  23.9 0.2 collective-permute-start.5
  24.1 0.7 shard_map.77
  24.7 0.5 collective-permute-start
  25.3 28.7 %collective-permute-done.theirs_ref = f32[16,64]{1,0:T(8,128)S(1)} collective-permute-done((f32[16,64]{1,0:T(8,128)S(1)}, f32[16,64]{1,0:T(8,128)S(1)}, u32[]{:S(2)}, u32[]{:S(2)}) %collective-permute-start) | collective-permute-done | bytes 4128 | tf_op jit(solution)/shard_map/ppermute | solution.py:28
  54.0 1.7 %collective-permute-start.6 = (bf16[256,1152]{1,0:T(8,128)(2,1)S(1)}, bf16[256,1152]{1,0:T(8,128)(2,1)S(1)}, u32[]{:S(2)}, u32[]{:S(2)}) collective-permute-start(bf16[256,1152]{1,0:T(8,128)(2,1)S(1)} %bitcast.14), channel_id=1, source_target_pairs={{0,1},{1,0},{2,3},{3,2},{4,5},{5,4},{6,7},{7,6},{8,9},{9,8},{10,11... | collective-permute-start | bytes 1769480 | tf_op jit(solution)/shard_map/ppermute | solution.py:28
  55.8 0.4 shard_map.78.mixed_ref
  56.2 0.0 collective-permute-done.5.refs_5_
  56.2 0.1 collective-permute-start.15
  56.2 0.0 collective-permute-done.4.refs_4_
  56.3 4.9 %shard_map.81 = (bf16[1152,1152]{1,0:T(8,128)(2,1)S(1)}, bf16[1024,1152]{1,0:T(8,128)(2,1)S(1)}) custom-call(s32[2]{0:T(128)S(1)} %pad_add_fusion.at_ref, s32[16]{0:T(128)S(1)} %copy-done.3, bf16[128,1152]{1,0:T(8,128)(2,1)S(1)} %copy-done.1, bf16[128,1152]{1,0:T(8,128)(2,1)S(1)} %collective-permute-done.1.mid_ref.refs_1_, ...), custom_call_target="tpu_custom_call" | custom-call | flops 2717908992 | bytes 9666632 | tf_op jit(solution)/shard_map/pallas_call | solution.py:41
  61.2 0.0 collective-permute-done.7.s_ref.refs_2_
  61.2 2.1 %shard_map.82 = (bf16[384,1152]{1,0:T(8,128)(2,1)S(1)}, bf16[768,1152]{1,0:T(8,128)(2,1)S(1)}) custom-call(bf16[256,256]{1,0:T(8,128)(2,1)S(1)} %shard_map.78.mixed_ref, bf16[1152,1152]{1,0:T(8,128)(2,1)S(1)} %get-tuple-element.39.v_ref, bf16[384,1152]{1,0:T(8,128)(2,1)S(1)} %collective-permute-done.7.s_ref.refs_2_, ...), custom_call_target="tpu_custom_call" | custom-call | flops 2038431744 | bytes 8683520 | tf_op jit(solution)/shard_map/pallas_call | solution.py:41
  63.3 2.1 %shard_map.84 = (bf16[384,1152]{1,0:T(8,128)(2,1)S(1)}, bf16[768,1152]{1,0:T(8,128)(2,1)S(1)}) custom-call(bf16[256,256]{1,0:T(8,128)(2,1)S(1)} %shard_map.78.mixed_ref, bf16[1152,1152]{1,0:T(8,128)(2,1)S(1)} %get-tuple-element.39.v_ref, bf16[384,1152]{1,0:T(8,128)(2,1)S(1)} %collective-permute-done.8.s_ref.refs_0_, ...), custom_call_target="tpu_custom_call" | custom-call | flops 2038431744 | bytes 8683520 | tf_op jit(solution)/shard_map/pallas_call | solution.py:41
  65.4 2.5 %shard_map.85.refs_0_ = f32[1152,1152]{1,0:T(8,128)S(1)} custom-call(bf16[1024,1152]{1,0:T(8,128)(2,1)S(1)} %bitcast.7, bf16[384,1152]{1,0:T(8,128)(2,1)S(1)} %collective-permute-done.8.s_ref.refs_0_, bf16[768,1152]{1,0:T(8,128)(2,1)S(1)} %get-tuple-element.44.resp_ref), custom_call_target="tpu_custom_call" | custom-call | flops 2038431744 | bytes 10321920 | tf_op jit(solution)/shard_map/pallas_call | solution.py:41
  67.9 2.5 %shard_map.86.early_ref = f32[1152,1152]{1,0:T(8,128)S(1)} custom-call(bf16[1024,1152]{1,0:T(8,128)(2,1)S(1)} %bitcast.8, bf16[384,1152]{1,0:T(8,128)(2,1)S(1)} %collective-permute-done.7.s_ref.refs_2_, bf16[768,1152]{1,0:T(8,128)(2,1)S(1)} %get-tuple-element.43.resp_ref, f32[1152,1152]{1,0:T(8,128)S(1)} %shard_map.85.refs_0_), custom_call_target="tpu_custom_call" | custom-call | flops 2038431744 | bytes 15630336 | tf_op jit(solution)/shard_map/pallas_call | solution.py:41
  70.5 2.6 %shard_map.87 = (bf16[256,1152]{1,0:T(8,128)(2,1)S(1)}, bf16[512,1152]{1,0:T(8,128)(2,1)S(1)}, bf16[4,128,1024]{2,1,0:T(8,128)(2,1)S(1)}) custom-call(s32[2]{0:T(128)S(1)} %pad_add_fusion.at_ref, s32[16]{0:T(128)S(1)} %copy-done.3, bf16[256,256]{1,0:T(8,128)(2,1)S(1)} %shard_map.78.mixed_ref, bf16[1152,1152]{1,0:T(8,128)(2,1)S(1)} %get-tuple-element.39.v_ref, ...), custom_call_target="tpu_custom_call" | custom-call | flops 1358954496 | bytes 16220232 | tf_op jit(solution)/shard_map/pallas_call | solution.py:41
  73.1 0.5 collective-permute-start.9
  73.7 0.0 collective-permute-done.15.mid_ref.refs_1_
  73.7 0.6 shard_map.91
  74.3 3.5 %collective-permute-start.16 = (bf16[128,1920]{1,0:T(8,128)(2,1)S(1)}, bf16[128,1920]{1,0:T(8,128)(2,1)S(1)}, u32[]{:S(2)}, u32[]{:S(2)}) collective-permute-start(bf16[128,1920]{1,0:T(8,128)(2,1)S(1)} %get-tuple-element.59), channel_id=1, source_target_pairs={{0,4},{4,8},{8,12},{12,16},{16,20},{20,24},{24,28},{6,2},{10,6},{1... | collective-permute-start | bytes 1474568 | tf_op jit(solution)/shard_map/ppermute | solution.py:449
  77.7 3.7 %collective-permute-start.17 = (bf16[128,1408]{1,0:T(8,128)(2,1)S(1)}, bf16[128,1408]{1,0:T(8,128)(2,1)S(1)}, u32[]{:S(2)}, u32[]{:S(2)}) collective-permute-start(bf16[128,1408]{1,0:T(8,128)(2,1)S(1)} %get-tuple-element.60), channel_id=1, source_target_pairs={{0,8},{4,12},{8,16},{12,20},{16,24},{20,28},{10,2},{14,6},{18,10},... | collective-permute-start | bytes 1081352 | tf_op jit(solution)/shard_map/ppermute | solution.py:449
  81.4 7.8 %collective-permute-done.16.refs_2_ = bf16[128,1920]{1,0:T(8,128)(2,1)S(1)} collective-permute-done((bf16[128,1920]{1,0:T(8,128)(2,1)S(1)}, bf16[128,1920]{1,0:T(8,128)(2,1)S(1)}, u32[]{:S(2)}, u32[]{:S(2)}) %collective-permute-start.16) | collective-permute-done | bytes 491552 | tf_op jit(solution)/shard_map/ppermute | solution.py:449
  89.3 0.5 collective-permute-start.19
  89.8 1.6 %shard_map.88 = (f32[128,1152]{1,0:T(8,128)S(1)}, f32[128,1024]{1,0:T(8,128)S(1)}, f32[128,1024]{1,0:T(8,128)S(1)}, f32[128,768]{1,0:T(8,128)S(1)}, f32[128,768]{1,0:T(8,128)S(1)}) custom-call(s32[2]{0:T(128)S(1)} %pad_add_fusion.at_ref, s32[16]{0:T(128)S(1)} %copy-done.3, bf16[1024,1152]{1,0:T(8,128)(2,1)S(1)} %bitcast.10, ...), custom_call_target="tpu_custom_call" | custom-call | flops 679477248 | bytes 11862088 | tf_op jit(solution)/shard_map/pallas_call | solution.py:41
  91.4 0.9 shard_map.89
  92.3 2.5 %collective-permute-start.10 = (bf16[128,1024]{1,0:T(8,128)(2,1)S(1)}, bf16[128,1024]{1,0:T(8,128)(2,1)S(1)}, u32[]{:S(2)}, u32[]{:S(2)}) collective-permute-start(bf16[128,1024]{1,0:T(8,128)(2,1)S(1)} %get-tuple-element.53), channel_id=1, source_target_pairs={{0,4},{4,0},{2,6},{6,2},{8,12},{12,8},{10,14},{14,10},{16,20},{20,... | collective-permute-start | bytes 786440 | tf_op jit(solution)/shard_map/ppermute | solution.py:534
  94.9 0.7 collective-permute-start.11
  95.5 4.7 %shard_map.92 = (bf16[1152,1152]{1,0:T(8,128)(2,1)S(1)}, bf16[1024,1152]{1,0:T(8,128)(2,1)S(1)}) custom-call(s32[2]{0:T(128)S(1)} %pad_add_fusion.at_ref, s32[16]{0:T(128)S(1)} %copy-done.3, bf16[128,1152]{1,0:T(8,128)(2,1)S(1)} %copy-done.2, bf16[128,1152]{1,0:T(8,128)(2,1)S(1)} %collective-permute-done.15.mid_ref.refs_1_, ...), custom_call_target="tpu_custom_call" | custom-call | flops 2717908992 | bytes 9666632 | tf_op jit(solution)/shard_map/pallas_call | solution.py:41
  100.3 2.9 %collective-permute-start.12 = (bf16[128,768]{1,0:T(8,128)(2,1)S(1)}, bf16[128,768]{1,0:T(8,128)(2,1)S(1)}, u32[]{:S(2)}, u32[]{:S(2)}) collective-permute-start(bf16[128,768]{1,0:T(8,128)(2,1)S(1)} %get-tuple-element.55), channel_id=1, source_target_pairs={{0,8},{8,0},{2,10},{10,2},{4,12},{12,4},{6,14},{14,6},{16,24},{24,... | collective-permute-start | bytes 589832 | tf_op jit(solution)/shard_map/ppermute | solution.py:534
  103.1 0.7 collective-permute-start.13
  103.8 4.8 %shard_map.93.gram_ref = f32[256,256]{1,0:T(8,128)S(1)} custom-call(bf16[1152,1152]{1,0:T(8,128)(2,1)S(1)} %get-tuple-element.61.x_ref, bf16[1024,1152]{1,0:T(8,128)(2,1)S(1)} %get-tuple-element.62.co_ref, bf16[1024,1152]{1,0:T(8,128)(2,1)S(1)} %get-tuple-element.41.po_ref, bf16[384,1152]{1,0:T(8,128)(2,1)S(1)} %collective-permute-done.8.s_ref.refs_0_, ...), custom_call_target="tpu_custom_call" | custom-call | flops 2038431744 | bytes 11173888 | tf_op jit(solution)/shard_map/pallas_call | solution.py:41
  108.6 2.6 %shard_map.94 = f32[32,32]{1,0:T(8,128)S(1)} custom-call(s32[2]{0:T(128)S(1)} %pad_add_fusion.at_ref, bf16[1152,1152]{1,0:T(8,128)(2,1)S(1)} %get-tuple-element.61.x_ref, bf16[1024,1152]{1,0:T(8,128)(2,1)S(1)} %get-tuple-element.62.co_ref, bf16[1024,1152]{1,0:T(8,128)(2,1)S(1)} %get-tuple-element.41.po_ref, f32[256,256]{1,0:T(8,128)S(1)} %shard_map.93.gram_ref, ...), custom_call_target="tpu_custom_call" | custom-call | flops 679477248 | bytes 8826888 | tf_op jit(solution)/shard_map/pallas_call | solution.py:41
  111.2 3.5 %collective-permute-start.20 = (f32[32,32]{1,0:T(8,128)S(1)}, f32[32,32]{1,0:T(8,128)S(1)}, u32[]{:S(2)}, u32[]{:S(2)}) collective-permute-start(f32[32,32]{1,0:T(8,128)S(1)} %shard_map.94), channel_id=1, source_target_pairs={{0,8},{2,10},{4,12},{6,14},{8,0},{10,2},{12,4},{14,6},{16,24},{18,... | collective-permute-start | bytes 12296 | tf_op jit(solution)/shard_map/ppermute | solution.py:28
  114.8 1.7 %collective-permute-done.20 = f32[32,32]{1,0:T(8,128)S(1)} collective-permute-done((f32[32,32]{1,0:T(8,128)S(1)}, f32[32,32]{1,0:T(8,128)S(1)}, u32[]{:S(2)}, u32[]{:S(2)}) %collective-permute-start.20) | collective-permute-done | bytes 4128 | tf_op jit(solution)/shard_map/ppermute | solution.py:28
  116.5 0.5 collective-permute-start.21
  117.0 0.0 collective-permute-done.12.refs_2_
  117.1 0.8 shard_map.90
  117.8 1.6 %collective-permute-start.14 = (bf16[64,1152]{1,0:T(8,128)(2,1)S(1)}, bf16[64,1152]{1,0:T(8,128)(2,1)S(1)}, u32[]{:S(2)}, u32[]{:S(2)}) collective-permute-start(bf16[64,1152]{1,0:T(8,128)(2,1)S(1)} %get-tuple-element.58), channel_id=1, source_target_pairs={{0,1},{1,0},{2,3},{3,2},{4,5},{5,4},{6,7},{7,6},{8,9},{9,8},{10,11... | collective-permute-start | bytes 442376 | tf_op jit(solution)/shard_map/ppermute | solution.py:28
  119.4 0.8 collective-permute-done.21
  120.2 1.2 collective-permute-done.22
  121.4 1.2 collective-permute-start.23
  122.6 2.4 %collective-permute-done.23 = f32[16,32]{1,0:T(8,128)S(1)} collective-permute-done((f32[16,32]{1,0:T(8,128)S(1)}, f32[16,32]{1,0:T(8,128)S(1)}, u32[]{:S(2)}, u32[]{:S(2)}) %collective-permute-start.23) | collective-permute-done | bytes 2080 | tf_op jit(solution)/shard_map/ppermute | solution.py:28
  125.0 2.7 %collective-permute-start.24 = (f32[16,32]{1,0:T(8,128)S(1)}, f32[16,32]{1,0:T(8,128)S(1)}, u32[]{:S(2)}, u32[]{:S(2)}) collective-permute-start(f32[16,32]{1,0:T(8,128)S(1)} %add.15.pk_ref), channel_id=1, source_target_pairs={{0,16},{2,18},{4,20},{6,22},{8,24},{10,26},{12,28},{14,30},{16,0},... | collective-permute-start | bytes 6152 | tf_op jit(solution)/shard_map/ppermute | solution.py:28
  127.7 1.9 %collective-permute-done.24.pg_ref = f32[16,32]{1,0:T(8,128)S(1)} collective-permute-done((f32[16,32]{1,0:T(8,128)S(1)}, f32[16,32]{1,0:T(8,128)S(1)}, u32[]{:S(2)}, u32[]{:S(2)}) %collective-permute-start.24) | collective-permute-done | bytes 2080 | tf_op jit(solution)/shard_map/ppermute | solution.py:28
  129.6 1.3 %shard_map.95 = (f32[64,1152]{1,0:T(8,128)}, f32[16,32]{1,0:T(8,128)}) custom-call(s32[2]{0:T(128)S(1)} %pad_add_fusion.at_ref, s32[16]{0:T(128)S(1)} %copy-done.3, f32[64,1152]{1,0:T(8,128)S(1)} %get-tuple-element.57.keep_ref, bf16[64,1152]{1,0:T(8,128)(2,1)S(1)} %collective-permute-done.14.got_ref, f32[16,32]{1,0:T(8,128)S(1)} %add.15.pk_ref, ...), custom_call_target="tpu_custom_call" | custom-call | bytes 743496 | tf_op jit(solution)/shard_map/pallas_call | solution.py:41
  (23 shorter events, 0.1 us)
Async XLA Ops:
  0.6 2.0 %collective-permute-start.1 = (bf16[128,1152]{1,0:T(8,128)(2,1)}, bf16[128,1152]{1,0:T(8,128)(2,1)S(1)}, u32[]{:S(2)}, u32[]{:S(2)}) collective-permute-start(bf16[128,1152]{1,0:T(8,128)(2,1)} %refs_0_.2), channel_id=1, source_target_pairs={{0,2},{2,0},{4,6},{6,4},{8,10},{10,8},{12,14},{14,12},{16,18},{18,... | collective-permute-start | bytes 884744 | tf_op jit(solution)/shard_map/ppermute | solution.py:28
  2.6 1.0 copy-start
  4.2 16.4 %collective-permute-start.2 = (bf16[128,1920]{1,0:T(8,128)(2,1)S(1)}, bf16[128,1920]{1,0:T(8,128)(2,1)S(1)}, u32[]{:S(2)}, u32[]{:S(2)}) collective-permute-start(bf16[128,1920]{1,0:T(8,128)(2,1)S(1)} %get-tuple-element.36), channel_id=1, source_target_pairs={{0,4},{4,8},{8,12},{12,16},{16,20},{20,24},{24,28},{6,2},{10,6},{1... | collective-permute-start | bytes 1474568 | tf_op jit(solution)/shard_map/ppermute | solution.py:449
  9.0 14.8 %collective-permute-start.3 = (bf16[128,1408]{1,0:T(8,128)(2,1)S(1)}, bf16[128,1408]{1,0:T(8,128)(2,1)S(1)}, u32[]{:S(2)}, u32[]{:S(2)}) collective-permute-start(bf16[128,1408]{1,0:T(8,128)(2,1)S(1)} %get-tuple-element.37), channel_id=1, source_target_pairs={{0,8},{4,12},{8,16},{12,20},{16,24},{20,28},{10,2},{14,6},{18,10},... | collective-permute-start | bytes 1081352 | tf_op jit(solution)/shard_map/ppermute | solution.py:449
  15.2 8.9 %copy-start.4 = (bf16[16,32]{1,0:T(8,128)(2,1)S(1)}, bf16[16,32]{1,0:T(8,128)(2,1)}, u32[]{:S(2)}) copy-start(bf16[16,32]{1,0:T(8,128)(2,1)} %k_ref.1) | copy-start | bytes 3076
  15.2 8.9 %copy-start.5 = (s32[16]{0:T(128)S(1)}, s32[16]{0:T(128)}, u32[]{:S(2)}) copy-start(s32[16]{0:T(128)} %atom_ref.1) | copy-start | bytes 196
  15.2 40.9 %copy-start.2 = (bf16[128,1152]{1,0:T(8,128)(2,1)S(1)}, bf16[128,1152]{1,0:T(8,128)(2,1)}, u32[]{:S(2)}) copy-start(bf16[128,1152]{1,0:T(8,128)(2,1)} %refs_0_.3) | copy-start | bytes 884740
  15.2 41.0 %copy-start.1 = (bf16[128,1152]{1,0:T(8,128)(2,1)S(1)}, bf16[128,1152]{1,0:T(8,128)(2,1)}, u32[]{:S(2)}) copy-start(bf16[128,1152]{1,0:T(8,128)(2,1)} %refs_0_.2) | copy-start | bytes 884740
  15.3 41.0 %copy-start.3 = (s32[16]{0:T(128)S(1)}, s32[16]{0:T(128)}, u32[]{:S(2)}) copy-start(s32[16]{0:T(128)} %prof_ref.9) | copy-start | bytes 196
  15.3 45.9 %collective-permute-start.7 = (bf16[384,1152]{1,0:T(8,128)(2,1)S(1)}, bf16[384,1152]{1,0:T(8,128)(2,1)S(1)}, u32[]{:S(2)}, u32[]{:S(2)}) collective-permute-start(bf16[384,1152]{1,0:T(8,128)(2,1)S(1)} %bitcast.13), channel_id=1, source_target_pairs={{0,1},{1,0},{2,3},{3,2},{4,5},{5,4},{6,7},{7,6},{8,9},{9,8},{10,11... | collective-permute-start | bytes 2654216 | tf_op jit(solution)/shard_map/ppermute | solution.py:28
  20.6 35.7 %collective-permute-start.4 = (bf16[128,1920]{1,0:T(8,128)(2,1)S(1)}, bf16[128,1920]{1,0:T(8,128)(2,1)S(1)}, u32[]{:S(2)}, u32[]{:S(2)}) collective-permute-start(bf16[128,1920]{1,0:T(8,128)(2,1)S(1)} %collective-permute-done.2.refs_2_), channel_id=1, source_target_pairs={{0,2},{2,0},{4,6},{6,4},{8,10},{10,8},{12,14},{14,12},{16,18},{18,... | collective-permute-start | bytes 1474568 | tf_op jit(solution)/shard_map/ppermute | solution.py:28
  22.3 41.0 %collective-permute-start.8 = (bf16[384,1152]{1,0:T(8,128)(2,1)S(1)}, bf16[384,1152]{1,0:T(8,128)(2,1)S(1)}, u32[]{:S(2)}, u32[]{:S(2)}) collective-permute-start(bf16[384,1152]{1,0:T(8,128)(2,1)S(1)} %bitcast.12), channel_id=1, source_target_pairs={{0,1},{1,0},{2,3},{3,2},{4,5},{5,4},{6,7},{7,6},{8,9},{9,8},{10,11... | collective-permute-start | bytes 2654216 | tf_op jit(solution)/shard_map/ppermute | solution.py:28
  23.9 32.3 %collective-permute-start.5 = (bf16[128,1408]{1,0:T(8,128)(2,1)S(1)}, bf16[128,1408]{1,0:T(8,128)(2,1)S(1)}, u32[]{:S(2)}, u32[]{:S(2)}) collective-permute-start(bf16[128,1408]{1,0:T(8,128)(2,1)S(1)} %collective-permute-done.3.refs_3_), channel_id=1, source_target_pairs={{0,2},{2,0},{4,6},{6,4},{8,10},{10,8},{12,14},{14,12},{16,18},{18,... | collective-permute-start | bytes 1081352 | tf_op jit(solution)/shard_map/ppermute | solution.py:28
  24.7 29.3 %collective-permute-start = (f32[16,64]{1,0:T(8,128)S(1)}, f32[16,64]{1,0:T(8,128)S(1)}, u32[]{:S(2)}, u32[]{:S(2)}) collective-permute-start(f32[16,64]{1,0:T(8,128)S(1)} %get-tuple-element.35), channel_id=1, source_target_pairs={{0,1},{1,0},{2,3},{3,2},{4,5},{5,4},{6,7},{7,6},{8,9},{9,8},{10,11... | collective-permute-start | bytes 12296 | tf_op jit(solution)/shard_map/ppermute | solution.py:28
  54.0 16.5 %collective-permute-start.6 = (bf16[256,1152]{1,0:T(8,128)(2,1)S(1)}, bf16[256,1152]{1,0:T(8,128)(2,1)S(1)}, u32[]{:S(2)}, u32[]{:S(2)}) collective-permute-start(bf16[256,1152]{1,0:T(8,128)(2,1)S(1)} %bitcast.14), channel_id=1, source_target_pairs={{0,1},{1,0},{2,3},{3,2},{4,5},{5,4},{6,7},{7,6},{8,9},{9,8},{10,11... | collective-permute-start | bytes 1769480 | tf_op jit(solution)/shard_map/ppermute | solution.py:28
  56.2 17.5 %collective-permute-start.15 = (bf16[128,1152]{1,0:T(8,128)(2,1)S(1)}, bf16[128,1152]{1,0:T(8,128)(2,1)S(1)}, u32[]{:S(2)}, u32[]{:S(2)}) collective-permute-start(bf16[128,1152]{1,0:T(8,128)(2,1)S(1)} %copy-done.2), channel_id=1, source_target_pairs={{0,2},{2,0},{4,6},{6,4},{8,10},{10,8},{12,14},{14,12},{16,18},{18,... | collective-permute-start | bytes 884744 | tf_op jit(solution)/shard_map/ppermute | solution.py:28
  73.1 18.3 %collective-permute-start.9 = (bf16[4,128,1024]{2,1,0:T(8,128)(2,1)S(1)}, bf16[4,128,1024]{2,1,0:T(8,128)(2,1)S(1)}, u32[]{:S(2)}, u32[]{:S(2)}) collective-permute-start(bf16[4,128,1024]{2,1,0:T(8,128)(2,1)S(1)} %get-tuple-element.45), channel_id=1, source_target_pairs={{0,2},{2,0},{4,6},{6,4},{8,10},{10,8},{12,14},{14,12},{16,18},{18,... | collective-permute-start | bytes 3145736 | tf_op jit(solution)/shard_map/ppermute | solution.py:28
  74.3 15.0 %collective-permute-start.16 = (bf16[128,1920]{1,0:T(8,128)(2,1)S(1)}, bf16[128,1920]{1,0:T(8,128)(2,1)S(1)}, u32[]{:S(2)}, u32[]{:S(2)}) collective-permute-start(bf16[128,1920]{1,0:T(8,128)(2,1)S(1)} %get-tuple-element.59), channel_id=1, source_target_pairs={{0,4},{4,8},{8,12},{12,16},{16,20},{20,24},{24,28},{6,2},{10,6},{1... | collective-permute-start | bytes 1474568 | tf_op jit(solution)/shard_map/ppermute | solution.py:449
  77.7 11.5 %collective-permute-start.17 = (bf16[128,1408]{1,0:T(8,128)(2,1)S(1)}, bf16[128,1408]{1,0:T(8,128)(2,1)S(1)}, u32[]{:S(2)}, u32[]{:S(2)}) collective-permute-start(bf16[128,1408]{1,0:T(8,128)(2,1)S(1)} %get-tuple-element.60), channel_id=1, source_target_pairs={{0,8},{4,12},{8,16},{12,20},{16,24},{20,28},{10,2},{14,6},{18,10},... | collective-permute-start | bytes 1081352 | tf_op jit(solution)/shard_map/ppermute | solution.py:449
  89.3 6.3 %collective-permute-start.18 = (bf16[128,1920]{1,0:T(8,128)(2,1)S(1)}, bf16[128,1920]{1,0:T(8,128)(2,1)S(1)}, u32[]{:S(2)}, u32[]{:S(2)}) collective-permute-start(bf16[128,1920]{1,0:T(8,128)(2,1)S(1)} %collective-permute-done.16.refs_2_), channel_id=1, source_target_pairs={{0,2},{2,0},{4,6},{6,4},{8,10},{10,8},{12,14},{14,12},{16,18},{18,... | collective-permute-start | bytes 1474568 | tf_op jit(solution)/shard_map/ppermute | solution.py:28
  89.3 6.3 %collective-permute-start.19 = (bf16[128,1408]{1,0:T(8,128)(2,1)S(1)}, bf16[128,1408]{1,0:T(8,128)(2,1)S(1)}, u32[]{:S(2)}, u32[]{:S(2)}) collective-permute-start(bf16[128,1408]{1,0:T(8,128)(2,1)S(1)} %collective-permute-done.17.refs_3_), channel_id=1, source_target_pairs={{0,2},{2,0},{4,6},{6,4},{8,10},{10,8},{12,14},{14,12},{16,18},{18,... | collective-permute-start | bytes 1081352 | tf_op jit(solution)/shard_map/ppermute | solution.py:28
  92.3 24.7 %collective-permute-start.10 = (bf16[128,1024]{1,0:T(8,128)(2,1)S(1)}, bf16[128,1024]{1,0:T(8,128)(2,1)S(1)}, u32[]{:S(2)}, u32[]{:S(2)}) collective-permute-start(bf16[128,1024]{1,0:T(8,128)(2,1)S(1)} %get-tuple-element.53), channel_id=1, source_target_pairs={{0,4},{4,0},{2,6},{6,2},{8,12},{12,8},{10,14},{14,10},{16,20},{20,... | collective-permute-start | bytes 786440 | tf_op jit(solution)/shard_map/ppermute | solution.py:534
  94.9 22.2 %collective-permute-start.11 = (bf16[128,1024]{1,0:T(8,128)(2,1)S(1)}, bf16[128,1024]{1,0:T(8,128)(2,1)S(1)}, u32[]{:S(2)}, u32[]{:S(2)}) collective-permute-start(bf16[128,1024]{1,0:T(8,128)(2,1)S(1)} %get-tuple-element.54), channel_id=1, source_target_pairs={{4,8},{8,4},{6,10},{10,6},{12,16},{16,12},{14,18},{18,14},{20,24},... | collective-permute-start | bytes 786440 | tf_op jit(solution)/shard_map/ppermute | solution.py:534
  100.3 16.8 %collective-permute-start.12 = (bf16[128,768]{1,0:T(8,128)(2,1)S(1)}, bf16[128,768]{1,0:T(8,128)(2,1)S(1)}, u32[]{:S(2)}, u32[]{:S(2)}) collective-permute-start(bf16[128,768]{1,0:T(8,128)(2,1)S(1)} %get-tuple-element.55), channel_id=1, source_target_pairs={{0,8},{8,0},{2,10},{10,2},{4,12},{12,4},{6,14},{14,6},{16,24},{24,... | collective-permute-start | bytes 589832 | tf_op jit(solution)/shard_map/ppermute | solution.py:534
  103.1 13.9 %collective-permute-start.13 = (bf16[128,768]{1,0:T(8,128)(2,1)S(1)}, bf16[128,768]{1,0:T(8,128)(2,1)S(1)}, u32[]{:S(2)}, u32[]{:S(2)}) collective-permute-start(bf16[128,768]{1,0:T(8,128)(2,1)S(1)} %get-tuple-element.56), channel_id=1, source_target_pairs={{8,16},{16,8},{10,18},{18,10},{12,20},{20,12},{14,22},{22,14},{9,1... | collective-permute-start | bytes 589832 | tf_op jit(solution)/shard_map/ppermute | solution.py:534
  111.2 5.2 %collective-permute-start.20 = (f32[32,32]{1,0:T(8,128)S(1)}, f32[32,32]{1,0:T(8,128)S(1)}, u32[]{:S(2)}, u32[]{:S(2)}) collective-permute-start(f32[32,32]{1,0:T(8,128)S(1)} %shard_map.94), channel_id=1, source_target_pairs={{0,8},{2,10},{4,12},{6,14},{8,0},{10,2},{12,4},{14,6},{16,24},{18,... | collective-permute-start | bytes 12296 | tf_op jit(solution)/shard_map/ppermute | solution.py:28
  116.5 3.7 %collective-permute-start.21 = (f32[16,32]{1,0:T(8,128)S(1)}, f32[16,32]{1,0:T(8,128)S(1)}, u32[]{:S(2)}, u32[]{:S(2)}) collective-permute-start(f32[16,32]{1,0:T(8,128)S(1)} %slice.9), channel_id=1, source_target_pairs={{0,1},{1,0},{2,3},{3,2},{4,5},{5,4},{6,7},{7,6},{8,9},{9,8},{10,11... | collective-permute-start | bytes 6152 | tf_op jit(solution)/shard_map/ppermute | solution.py:28
  117.8 11.7 %collective-permute-start.14 = (bf16[64,1152]{1,0:T(8,128)(2,1)S(1)}, bf16[64,1152]{1,0:T(8,128)(2,1)S(1)}, u32[]{:S(2)}, u32[]{:S(2)}) collective-permute-start(bf16[64,1152]{1,0:T(8,128)(2,1)S(1)} %get-tuple-element.58), channel_id=1, source_target_pairs={{0,1},{1,0},{2,3},{3,2},{4,5},{5,4},{6,7},{7,6},{8,9},{9,8},{10,11... | collective-permute-start | bytes 442376 | tf_op jit(solution)/shard_map/ppermute | solution.py:28
  120.2 1.2 collective-permute-start.22
  121.4 3.7 %collective-permute-start.23 = (f32[16,32]{1,0:T(8,128)S(1)}, f32[16,32]{1,0:T(8,128)S(1)}, u32[]{:S(2)}, u32[]{:S(2)}) collective-permute-start(f32[16,32]{1,0:T(8,128)S(1)} %add.14), channel_id=1, source_target_pairs={{0,4},{2,6},{4,0},{6,2},{8,12},{10,14},{12,8},{14,10},{16,20},{18,... | collective-permute-start | bytes 6152 | tf_op jit(solution)/shard_map/ppermute | solution.py:28
  125.0 4.5 %collective-permute-start.24 = (f32[16,32]{1,0:T(8,128)S(1)}, f32[16,32]{1,0:T(8,128)S(1)}, u32[]{:S(2)}, u32[]{:S(2)}) collective-permute-start(f32[16,32]{1,0:T(8,128)S(1)} %add.15.pk_ref), channel_id=1, source_target_pairs={{0,16},{2,18},{4,20},{6,22},{8,24},{10,26},{12,28},{14,30},{16,0},... | collective-permute-start | bytes 6152 | tf_op jit(solution)/shard_map/ppermute | solution.py:28

commit v4 on v3

--- a/solution.py
+++ b/solution.py
@@ -321,37 +321,41 @@
         merge({-4: 0, -2: 1, 0: 2, 2: 3})
 
 
+def gathered(position, which, c, own_ref, pieces):
+    block = own_ref.shape[0]
+    rows = block // 2
+    window = pl.ds(pl.multiple_of(which * rows, rows), rows)
+    total = own_ref[window, c * block : (c + 1) * block]
+    for distance, one, two in ((2, *pieces[:2]), (4, *pieces[2:])):
+        upward = upward_first(position, distance)
+        for offset, above, below in ((distance, two, one), (-distance, one, two)):
+            at = c - FIRST_COLUMN[offset]
+            if 0 <= at < columns_to(offset):
+                tile = slice(at * block, (at + 1) * block)
+                part = jnp.where(upward, above[window, tile], below[window, tile])
+                total = total + part.astype(F32)
+    return total
+
+
 def gather_kernel(at_ref, own_ref, *refs):
-    pieces, (keep_ref, send_ref) = {2: refs[:2], 4: refs[2:4]}, refs[4:]
     block = own_ref.shape[0]
-    rows = keep_ref.shape[0]
-    position, half = at_ref[0], at_ref[1]
-    for target, which in ((send_ref, 1 - half), (keep_ref, half)):
-        window = pl.ds(pl.multiple_of(which * rows, rows), rows)
-        for c in range(SLOTS):
-            columns = slice(c * block, (c + 1) * block)
-            total = own_ref[window, columns]
-            for distance, (one, two) in pieces.items():
-                upward = upward_first(position, distance)
-                for offset, above, below in ((distance, two, one), (-distance, one, two)):
-                    at = c - FIRST_COLUMN[offset]
-                    if 0 <= at < columns_to(offset):
-                        tile = slice(at * block, (at + 1) * block)
-                        part = jnp.where(upward, above[window, tile], below[window, tile])
-                        total = total + part.astype(F32)
-            target[:, columns] = total.astype(target.dtype)
+    send_ref = refs[4]
+    for c in range(SLOTS):
+        total = gathered(at_ref[0], 1 - at_ref[1], c, own_ref, refs[:4])
+        send_ref[:, c * block : (c + 1) * block] = total.astype(BF16)
 
 
 def finish_kernel(
-    nblocks, block, scale, polar_scale, at_ref, prof_ref, keep_ref, got_ref, pk_ref, pg_ref,
-    out_ref, polar_ref,
+    nblocks, block, scale, polar_scale, at_ref, prof_ref, own_ref, *refs
 ):
+    *pieces, got_ref, pk_ref, pg_ref, out_ref, polar_ref = refs
     polar_ref[...] = (pk_ref[...] + pg_ref[...]) * polar_scale
     position = at_ref[0]
     for c in range(SLOTS):
         columns = slice(c * block, (c + 1) * block)
         ok = permitted(prof_ref, nblocks, position, position + c - SPREAD)
-        value = (keep_ref[:, columns] + got_ref[:, columns].astype(F32)) * scale
+        kept = gathered(position, at_ref[1], c, own_ref, pieces)
+        value = (kept + got_ref[:, columns].astype(F32)) * scale
         out_ref[:, columns] = jnp.where(ok, value, jnp.zeros_like(value))
 
 
@@ -532,12 +536,8 @@
         lower = [i for i in range(nblocks - distance) if i // distance % 2 == parity]
         route = [pair for i in lower for pair in ((i, i + distance), (i + distance, i))]
         arrived.append(lax.ppermute(send, "chain", route))
-    keep, send = run(
-        gather_kernel,
-        [at, mid, *arrived],
-        [shaped((rows, width), F32), shaped((rows, width))],
-        smem=1,
-    )
+    (send,) = run(gather_kernel, [at, mid, *arrived], [shaped((rows, width))], smem=1)
+
     occ_stack, coupled_own = contracted(near_occ)
     size = every * SUB
     (gram,) = run(
@@ -569,7 +569,7 @@
             1.0 / math.sqrt(block * every),
             1.0 / math.sqrt(block * nblocks * width),
         ),
-        [at, profile, keep, swapped(send, "aux"), polar, other],
+        [at, profile, mid, *arrived, swapped(send, "aux"), polar, other],
         [shaped((rows, width), F32), shaped((here, every), F32)],
         smem=2,
     )

time: 131 us -> 131 us (level)
  no operation moved by 1% of the time
where the time goes in v4:
time: 131 us
  waiting for transfers between devices  49.7 us (38%)
  Pallas kernels  40.2 us (31%)
  starting transfers between devices  39 us (30%)
    ppermute x17, waiting for transfers between devices, swapped(): lax.ppermute(block, axis, [(i, i ^ bit) for i in range(lax.axis_size(axis...  38.1 us
    pallas_call x17, Pallas kernels, run(): pl.pallas_call(kernel, out_shape=outs, in_specs=[SMEM] * smem + [VMEM] *...  35.8 us
    ppermute x17, starting transfers between devices, swapped(): lax.ppermute(block, axis, [(i, i ^ bit) for i in range(lax.axis_size(axis...  16.9 us
    ppermute x4, starting transfers between devices, halo(): hops.append(lax.ppermute(pack, 'chain', up + down))  15.4 us
    ppermute x4, waiting for transfers between devices, halo(): hops.append(lax.ppermute(pack, 'chain', up + down))  11.6 us
    ppermute x4, starting transfers between devices, step(): arrived.append(lax.ppermute(send, 'chain', route))  6.74 us
    pallas_call x2, Pallas kernels, cut(): parts = call(at, integrals)  4.42 us
  transfers between devices with their start and end apart: 25, of which 9 were waited for; matrix products, arithmetic and copies ran while one was open for 0% of the time, Pallas kernels for 29%

profile of v4, /device:TPU:0, one launch (start us, length us, event | category | flops | bytes accessed | tf_op | source)
XLA Modules:
  0.0 131.0 jit_solution(10669375206362102823)
XLA Ops:
  0.6 0.6 collective-permute-start.1
  1.2 0.1 pad_add_fusion.at_ref
  1.3 1.3 %collective-permute-done.1.mid_ref.refs_1_ = bf16[128,1152]{1,0:T(8,128)(2,1)S(1)} collective-permute-done((bf16[128,1152]{1,0:T(8,128)(2,1)}, bf16[128,1152]{1,0:T(8,128)(2,1)S(1)}, u32[]{:S(2)}, u32[]{:S(2)}) %collective-permute-start.1) | collective-permute-done | bytes 294944 | tf_op jit(solution)/shard_map/ppermute | solution.py:28
  2.6 1.0 copy-done
  3.6 0.6 shard_map.79
  4.2 4.8 %collective-permute-start.2 = (bf16[128,1920]{1,0:T(8,128)(2,1)S(1)}, bf16[128,1920]{1,0:T(8,128)(2,1)S(1)}, u32[]{:S(2)}, u32[]{:S(2)}) collective-permute-start(bf16[128,1920]{1,0:T(8,128)(2,1)S(1)} %get-tuple-element.34), channel_id=1, source_target_pairs={{0,4},{4,8},{8,12},{12,16},{16,20},{20,24},{24,28},{6,2},{10,6},{1... | collective-permute-start | bytes 1474568 | tf_op jit(solution)/shard_map/ppermute | solution.py:453
  9.0 3.5 %collective-permute-start.3 = (bf16[128,1408]{1,0:T(8,128)(2,1)S(1)}, bf16[128,1408]{1,0:T(8,128)(2,1)S(1)}, u32[]{:S(2)}, u32[]{:S(2)}) collective-permute-start(bf16[128,1408]{1,0:T(8,128)(2,1)S(1)} %get-tuple-element.35), channel_id=1, source_target_pairs={{0,8},{4,12},{8,16},{12,20},{16,24},{20,28},{10,2},{14,6},{18,10},... | collective-permute-start | bytes 1081352 | tf_op jit(solution)/shard_map/ppermute | solution.py:453
  12.5 2.7 %shard_map.80 = (bf16[3,16,8,1152]{3,2,1,0:T(8,128)(2,1)S(1)}, bf16[2,16,8,1152]{3,2,1,0:T(8,128)(2,1)S(1)}, bf16[8,16,8,1152]{3,2,1,0:T(8,128)(2,1)S(1)}) custom-call(s32[2]{0:T(128)S(1)} %pad_add_fusion.at_ref, bf16[16,128,1152]{2,1,0:T(8,128)(2,1)} %three_ref.3), custom_call_target="tpu_custom_call" | custom-call | bytes 7667712 | tf_op jit(solution)/shard_map/pallas_call | solution.py:438
  15.2 0.0 copy-start.4
  15.2 0.0 copy-start.5
  15.2 0.0 copy-start.2
  15.2 0.0 copy-start.1
  15.3 0.0 copy-start.3
  15.3 1.6 %collective-permute-start.7 = (bf16[384,1152]{1,0:T(8,128)(2,1)S(1)}, bf16[384,1152]{1,0:T(8,128)(2,1)S(1)}, u32[]{:S(2)}, u32[]{:S(2)}) collective-permute-start(bf16[384,1152]{1,0:T(8,128)(2,1)S(1)} %bitcast.13), channel_id=1, source_target_pairs={{0,1},{1,0},{2,3},{3,2},{4,5},{5,4},{6,7},{7,6},{8,9},{9,8},{10,11... | collective-permute-start | bytes 2654216 | tf_op jit(solution)/shard_map/ppermute | solution.py:28
  16.8 3.8 %collective-permute-done.2.refs_2_ = bf16[128,1920]{1,0:T(8,128)(2,1)S(1)} collective-permute-done((bf16[128,1920]{1,0:T(8,128)(2,1)S(1)}, bf16[128,1920]{1,0:T(8,128)(2,1)S(1)}, u32[]{:S(2)}, u32[]{:S(2)}) %collective-permute-start.2) | collective-permute-done | bytes 491552 | tf_op jit(solution)/shard_map/ppermute | solution.py:453
  20.6 0.0 collective-permute-start.4
  20.6 1.7 %shard_map.83 = bf16[3,16,8,1152]{3,2,1,0:T(8,128)(2,1)S(1)} custom-call(s32[2]{0:T(128)S(1)} %pad_add_fusion.at_ref, bf16[16,128,1152]{2,1,0:T(8,128)(2,1)} %three_ref.3), custom_call_target="tpu_custom_call" | custom-call | bytes 1769472 | tf_op jit(solution)/shard_map/pallas_call | solution.py:438
  22.3 1.6 %collective-permute-start.8 = (bf16[384,1152]{1,0:T(8,128)(2,1)S(1)}, bf16[384,1152]{1,0:T(8,128)(2,1)S(1)}, u32[]{:S(2)}, u32[]{:S(2)}) collective-permute-start(bf16[384,1152]{1,0:T(8,128)(2,1)S(1)} %bitcast.12), channel_id=1, source_target_pairs={{0,1},{1,0},{2,3},{3,2},{4,5},{5,4},{6,7},{7,6},{8,9},{9,8},{10,11... | collective-permute-start | bytes 2654216 | tf_op jit(solution)/shard_map/ppermute | solution.py:28
  23.9 0.0 collective-permute-done.3.refs_3_
  23.9 0.2 collective-permute-start.5
  24.1 0.7 shard_map.77
  24.7 0.5 collective-permute-start
  25.3 28.7 %collective-permute-done.theirs_ref = f32[16,64]{1,0:T(8,128)S(1)} collective-permute-done((f32[16,64]{1,0:T(8,128)S(1)}, f32[16,64]{1,0:T(8,128)S(1)}, u32[]{:S(2)}, u32[]{:S(2)}) %collective-permute-start) | collective-permute-done | bytes 4128 | tf_op jit(solution)/shard_map/ppermute | solution.py:28
  54.0 1.7 %collective-permute-start.6 = (bf16[256,1152]{1,0:T(8,128)(2,1)S(1)}, bf16[256,1152]{1,0:T(8,128)(2,1)S(1)}, u32[]{:S(2)}, u32[]{:S(2)}) collective-permute-start(bf16[256,1152]{1,0:T(8,128)(2,1)S(1)} %bitcast.14), channel_id=1, source_target_pairs={{0,1},{1,0},{2,3},{3,2},{4,5},{5,4},{6,7},{7,6},{8,9},{9,8},{10,11... | collective-permute-start | bytes 1769480 | tf_op jit(solution)/shard_map/ppermute | solution.py:28
  55.8 0.4 shard_map.78.mixed_ref
  56.2 0.0 collective-permute-done.5.refs_5_
  56.2 0.1 collective-permute-start.15
  56.2 0.0 collective-permute-done.4.refs_4_
  56.3 4.9 %shard_map.81 = (bf16[1152,1152]{1,0:T(8,128)(2,1)S(1)}, bf16[1024,1152]{1,0:T(8,128)(2,1)S(1)}) custom-call(s32[2]{0:T(128)S(1)} %pad_add_fusion.at_ref, s32[16]{0:T(128)S(1)} %copy-done.3, bf16[128,1152]{1,0:T(8,128)(2,1)S(1)} %copy-done.1, bf16[128,1152]{1,0:T(8,128)(2,1)S(1)} %collective-permute-done.1.mid_ref.refs_1_, ...), custom_call_target="tpu_custom_call" | custom-call | flops 2717908992 | bytes 9666632 | tf_op jit(solution)/shard_map/pallas_call | solution.py:41
  61.2 0.0 collective-permute-done.7.s_ref.refs_2_
  61.2 2.1 %shard_map.82 = (bf16[384,1152]{1,0:T(8,128)(2,1)S(1)}, bf16[768,1152]{1,0:T(8,128)(2,1)S(1)}) custom-call(bf16[256,256]{1,0:T(8,128)(2,1)S(1)} %shard_map.78.mixed_ref, bf16[1152,1152]{1,0:T(8,128)(2,1)S(1)} %get-tuple-element.37.v_ref, bf16[384,1152]{1,0:T(8,128)(2,1)S(1)} %collective-permute-done.7.s_ref.refs_2_, ...), custom_call_target="tpu_custom_call" | custom-call | flops 2038431744 | bytes 8683520 | tf_op jit(solution)/shard_map/pallas_call | solution.py:41
  63.3 2.1 %shard_map.84 = (bf16[384,1152]{1,0:T(8,128)(2,1)S(1)}, bf16[768,1152]{1,0:T(8,128)(2,1)S(1)}) custom-call(bf16[256,256]{1,0:T(8,128)(2,1)S(1)} %shard_map.78.mixed_ref, bf16[1152,1152]{1,0:T(8,128)(2,1)S(1)} %get-tuple-element.37.v_ref, bf16[384,1152]{1,0:T(8,128)(2,1)S(1)} %collective-permute-done.8.s_ref.refs_0_, ...), custom_call_target="tpu_custom_call" | custom-call | flops 2038431744 | bytes 8683520 | tf_op jit(solution)/shard_map/pallas_call | solution.py:41
  65.4 2.5 %shard_map.85.refs_0_ = f32[1152,1152]{1,0:T(8,128)S(1)} custom-call(bf16[1024,1152]{1,0:T(8,128)(2,1)S(1)} %bitcast.7, bf16[384,1152]{1,0:T(8,128)(2,1)S(1)} %collective-permute-done.8.s_ref.refs_0_, bf16[768,1152]{1,0:T(8,128)(2,1)S(1)} %get-tuple-element.42.resp_ref), custom_call_target="tpu_custom_call" | custom-call | flops 2038431744 | bytes 10321920 | tf_op jit(solution)/shard_map/pallas_call | solution.py:41
  67.9 2.5 %shard_map.86.early_ref = f32[1152,1152]{1,0:T(8,128)S(1)} custom-call(bf16[1024,1152]{1,0:T(8,128)(2,1)S(1)} %bitcast.8, bf16[384,1152]{1,0:T(8,128)(2,1)S(1)} %collective-permute-done.7.s_ref.refs_2_, bf16[768,1152]{1,0:T(8,128)(2,1)S(1)} %get-tuple-element.41.resp_ref, f32[1152,1152]{1,0:T(8,128)S(1)} %shard_map.85.refs_0_), custom_call_target="tpu_custom_call" | custom-call | flops 2038431744 | bytes 15630336 | tf_op jit(solution)/shard_map/pallas_call | solution.py:41
  70.5 2.6 %shard_map.87 = (bf16[256,1152]{1,0:T(8,128)(2,1)S(1)}, bf16[512,1152]{1,0:T(8,128)(2,1)S(1)}, bf16[4,128,1024]{2,1,0:T(8,128)(2,1)S(1)}) custom-call(s32[2]{0:T(128)S(1)} %pad_add_fusion.at_ref, s32[16]{0:T(128)S(1)} %copy-done.3, bf16[256,256]{1,0:T(8,128)(2,1)S(1)} %shard_map.78.mixed_ref, bf16[1152,1152]{1,0:T(8,128)(2,1)S(1)} %get-tuple-element.37.v_ref, ...), custom_call_target="tpu_custom_call" | custom-call | flops 1358954496 | bytes 16220232 | tf_op jit(solution)/shard_map/pallas_call | solution.py:41
  73.1 0.5 collective-permute-start.9
  73.7 0.0 collective-permute-done.15.mid_ref.refs_1_
  73.7 0.6 shard_map.91
  74.3 3.5 %collective-permute-start.16 = (bf16[128,1920]{1,0:T(8,128)(2,1)S(1)}, bf16[128,1920]{1,0:T(8,128)(2,1)S(1)}, u32[]{:S(2)}, u32[]{:S(2)}) collective-permute-start(bf16[128,1920]{1,0:T(8,128)(2,1)S(1)} %get-tuple-element.55), channel_id=1, source_target_pairs={{0,4},{4,8},{8,12},{12,16},{16,20},{20,24},{24,28},{6,2},{10,6},{1... | collective-permute-start | bytes 1474568 | tf_op jit(solution)/shard_map/ppermute | solution.py:453
  77.7 3.7 %collective-permute-start.17 = (bf16[128,1408]{1,0:T(8,128)(2,1)S(1)}, bf16[128,1408]{1,0:T(8,128)(2,1)S(1)}, u32[]{:S(2)}, u32[]{:S(2)}) collective-permute-start(bf16[128,1408]{1,0:T(8,128)(2,1)S(1)} %get-tuple-element.56), channel_id=1, source_target_pairs={{0,8},{4,12},{8,16},{12,20},{16,24},{20,28},{10,2},{14,6},{18,10},... | collective-permute-start | bytes 1081352 | tf_op jit(solution)/shard_map/ppermute | solution.py:453
  81.4 7.8 %collective-permute-done.16.refs_2_ = bf16[128,1920]{1,0:T(8,128)(2,1)S(1)} collective-permute-done((bf16[128,1920]{1,0:T(8,128)(2,1)S(1)}, bf16[128,1920]{1,0:T(8,128)(2,1)S(1)}, u32[]{:S(2)}, u32[]{:S(2)}) %collective-permute-start.16) | collective-permute-done | bytes 491552 | tf_op jit(solution)/shard_map/ppermute | solution.py:453
  89.3 0.5 collective-permute-start.19
  89.8 1.6 %shard_map.88 = (f32[128,1152]{1,0:T(8,128)S(1)}, f32[128,1024]{1,0:T(8,128)S(1)}, f32[128,1024]{1,0:T(8,128)S(1)}, f32[128,768]{1,0:T(8,128)S(1)}, f32[128,768]{1,0:T(8,128)S(1)}) custom-call(s32[2]{0:T(128)S(1)} %pad_add_fusion.at_ref, s32[16]{0:T(128)S(1)} %copy-done.3, bf16[1024,1152]{1,0:T(8,128)(2,1)S(1)} %bitcast.10, ...), custom_call_target="tpu_custom_call" | custom-call | flops 679477248 | bytes 11862088 | tf_op jit(solution)/shard_map/pallas_call | solution.py:41
  91.4 0.9 shard_map.89
  92.3 2.5 %collective-permute-start.10 = (bf16[128,1024]{1,0:T(8,128)(2,1)S(1)}, bf16[128,1024]{1,0:T(8,128)(2,1)S(1)}, u32[]{:S(2)}, u32[]{:S(2)}) collective-permute-start(bf16[128,1024]{1,0:T(8,128)(2,1)S(1)} %get-tuple-element.51), channel_id=1, source_target_pairs={{0,4},{4,0},{2,6},{6,2},{8,12},{12,8},{10,14},{14,10},{16,20},{20,... | collective-permute-start | bytes 786440 | tf_op jit(solution)/shard_map/ppermute | solution.py:538
  94.9 0.7 collective-permute-start.11
  95.5 0.0 collective-permute-done.18.refs_4_
  95.6 4.7 %shard_map.92 = (bf16[1152,1152]{1,0:T(8,128)(2,1)S(1)}, bf16[1024,1152]{1,0:T(8,128)(2,1)S(1)}) custom-call(s32[2]{0:T(128)S(1)} %pad_add_fusion.at_ref, s32[16]{0:T(128)S(1)} %copy-done.3, bf16[128,1152]{1,0:T(8,128)(2,1)S(1)} %copy-done.2, bf16[128,1152]{1,0:T(8,128)(2,1)S(1)} %collective-permute-done.15.mid_ref.refs_1_, ...), custom_call_target="tpu_custom_call" | custom-call | flops 2717908992 | bytes 9666632 | tf_op jit(solution)/shard_map/pallas_call | solution.py:41
  100.3 2.9 %collective-permute-start.12 = (bf16[128,768]{1,0:T(8,128)(2,1)S(1)}, bf16[128,768]{1,0:T(8,128)(2,1)S(1)}, u32[]{:S(2)}, u32[]{:S(2)}) collective-permute-start(bf16[128,768]{1,0:T(8,128)(2,1)S(1)} %get-tuple-element.53), channel_id=1, source_target_pairs={{0,8},{8,0},{2,10},{10,2},{4,12},{12,4},{6,14},{14,6},{16,24},{24,... | collective-permute-start | bytes 589832 | tf_op jit(solution)/shard_map/ppermute | solution.py:538
  103.1 0.7 collective-permute-start.13
  103.8 4.8 %shard_map.93.gram_ref = f32[256,256]{1,0:T(8,128)S(1)} custom-call(bf16[1152,1152]{1,0:T(8,128)(2,1)S(1)} %get-tuple-element.57.x_ref, bf16[1024,1152]{1,0:T(8,128)(2,1)S(1)} %get-tuple-element.58.co_ref, bf16[1024,1152]{1,0:T(8,128)(2,1)S(1)} %get-tuple-element.39.po_ref, bf16[384,1152]{1,0:T(8,128)(2,1)S(1)} %collective-permute-done.8.s_ref.refs_0_, ...), custom_call_target="tpu_custom_call" | custom-call | flops 2038431744 | bytes 11173888 | tf_op jit(solution)/shard_map/pallas_call | solution.py:41
  108.7 2.6 %shard_map.94 = f32[32,32]{1,0:T(8,128)S(1)} custom-call(s32[2]{0:T(128)S(1)} %pad_add_fusion.at_ref, bf16[1152,1152]{1,0:T(8,128)(2,1)S(1)} %get-tuple-element.57.x_ref, bf16[1024,1152]{1,0:T(8,128)(2,1)S(1)} %get-tuple-element.58.co_ref, bf16[1024,1152]{1,0:T(8,128)(2,1)S(1)} %get-tuple-element.39.po_ref, f32[256,256]{1,0:T(8,128)S(1)} %shard_map.93.gram_ref, ...), custom_call_target="tpu_custom_call" | custom-call | flops 679477248 | bytes 8826888 | tf_op jit(solution)/shard_map/pallas_call | solution.py:41
  111.3 3.5 %collective-permute-start.20 = (f32[32,32]{1,0:T(8,128)S(1)}, f32[32,32]{1,0:T(8,128)S(1)}, u32[]{:S(2)}, u32[]{:S(2)}) collective-permute-start(f32[32,32]{1,0:T(8,128)S(1)} %shard_map.94), channel_id=1, source_target_pairs={{0,8},{2,10},{4,12},{6,14},{8,0},{10,2},{12,4},{14,6},{16,24},{18,... | collective-permute-start | bytes 12296 | tf_op jit(solution)/shard_map/ppermute | solution.py:28
  114.8 1.7 %collective-permute-done.20 = f32[32,32]{1,0:T(8,128)S(1)} collective-permute-done((f32[32,32]{1,0:T(8,128)S(1)}, f32[32,32]{1,0:T(8,128)S(1)}, u32[]{:S(2)}, u32[]{:S(2)}) %collective-permute-start.20) | collective-permute-done | bytes 4128 | tf_op jit(solution)/shard_map/ppermute | solution.py:28
  116.5 0.5 collective-permute-start.21
  117.1 0.7 shard_map.90
  117.8 1.6 %collective-permute-start.14 = (bf16[64,1152]{1,0:T(8,128)(2,1)S(1)}, bf16[64,1152]{1,0:T(8,128)(2,1)S(1)}, u32[]{:S(2)}, u32[]{:S(2)}) collective-permute-start(bf16[64,1152]{1,0:T(8,128)(2,1)S(1)} %shard_map.90), channel_id=1, source_target_pairs={{0,1},{1,0},{2,3},{3,2},{4,5},{5,4},{6,7},{7,6},{8,9},{9,8},{10,11... | collective-permute-start | bytes 442376 | tf_op jit(solution)/shard_map/ppermute | solution.py:28
  119.3 0.8 collective-permute-done.21
  120.2 1.2 collective-permute-done.22
  121.3 1.3 collective-permute-start.23
  122.6 2.4 %collective-permute-done.23 = f32[16,32]{1,0:T(8,128)S(1)} collective-permute-done((f32[16,32]{1,0:T(8,128)S(1)}, f32[16,32]{1,0:T(8,128)S(1)}, u32[]{:S(2)}, u32[]{:S(2)}) %collective-permute-start.23) | collective-permute-done | bytes 2080 | tf_op jit(solution)/shard_map/ppermute | solution.py:28
  125.0 2.7 %collective-permute-start.24 = (f32[16,32]{1,0:T(8,128)S(1)}, f32[16,32]{1,0:T(8,128)S(1)}, u32[]{:S(2)}, u32[]{:S(2)}) collective-permute-start(f32[16,32]{1,0:T(8,128)S(1)} %add.15.refs_5_), channel_id=1, source_target_pairs={{0,16},{2,18},{4,20},{6,22},{8,24},{10,26},{12,28},{14,30},{16,0},... | collective-permute-start | bytes 6152 | tf_op jit(solution)/shard_map/ppermute | solution.py:28
  127.7 1.8 %collective-permute-done.24.refs_6_ = f32[16,32]{1,0:T(8,128)S(1)} collective-permute-done((f32[16,32]{1,0:T(8,128)S(1)}, f32[16,32]{1,0:T(8,128)S(1)}, u32[]{:S(2)}, u32[]{:S(2)}) %collective-permute-start.24) | collective-permute-done | bytes 2080 | tf_op jit(solution)/shard_map/ppermute | solution.py:28
  129.5 1.4 %shard_map.95 = (f32[64,1152]{1,0:T(8,128)}, f32[16,32]{1,0:T(8,128)}) custom-call(s32[2]{0:T(128)S(1)} %pad_add_fusion.at_ref, s32[16]{0:T(128)S(1)} %copy-done.3, f32[128,1152]{1,0:T(8,128)S(1)} %get-tuple-element.50.own_ref, bf16[128,1024]{1,0:T(8,128)(2,1)S(1)} %collective-permute-done.10.refs_0_, bf16[128,1024]{1,0:T(8,128)(2,1)S(1)} %collective-permute-done.11.refs_1_, ...), custom_call_target="tpu_custom_call" | custom-call | bytes 1955912 | tf_op jit(solution)/shard_map/pallas_call | solution.py:41
  (23 shorter events, 0.1 us)
Async XLA Ops:
  0.6 2.0 %collective-permute-start.1 = (bf16[128,1152]{1,0:T(8,128)(2,1)}, bf16[128,1152]{1,0:T(8,128)(2,1)S(1)}, u32[]{:S(2)}, u32[]{:S(2)}) collective-permute-start(bf16[128,1152]{1,0:T(8,128)(2,1)} %refs_0_.2), channel_id=1, source_target_pairs={{0,2},{2,0},{4,6},{6,4},{8,10},{10,8},{12,14},{14,12},{16,18},{18,... | collective-permute-start | bytes 884744 | tf_op jit(solution)/shard_map/ppermute | solution.py:28
  2.6 1.0 copy-start
  4.2 16.4 %collective-permute-start.2 = (bf16[128,1920]{1,0:T(8,128)(2,1)S(1)}, bf16[128,1920]{1,0:T(8,128)(2,1)S(1)}, u32[]{:S(2)}, u32[]{:S(2)}) collective-permute-start(bf16[128,1920]{1,0:T(8,128)(2,1)S(1)} %get-tuple-element.34), channel_id=1, source_target_pairs={{0,4},{4,8},{8,12},{12,16},{16,20},{20,24},{24,28},{6,2},{10,6},{1... | collective-permute-start | bytes 1474568 | tf_op jit(solution)/shard_map/ppermute | solution.py:453
  9.0 14.8 %collective-permute-start.3 = (bf16[128,1408]{1,0:T(8,128)(2,1)S(1)}, bf16[128,1408]{1,0:T(8,128)(2,1)S(1)}, u32[]{:S(2)}, u32[]{:S(2)}) collective-permute-start(bf16[128,1408]{1,0:T(8,128)(2,1)S(1)} %get-tuple-element.35), channel_id=1, source_target_pairs={{0,8},{4,12},{8,16},{12,20},{16,24},{20,28},{10,2},{14,6},{18,10},... | collective-permute-start | bytes 1081352 | tf_op jit(solution)/shard_map/ppermute | solution.py:453
  15.2 8.9 %copy-start.4 = (bf16[16,32]{1,0:T(8,128)(2,1)S(1)}, bf16[16,32]{1,0:T(8,128)(2,1)}, u32[]{:S(2)}) copy-start(bf16[16,32]{1,0:T(8,128)(2,1)} %k_ref.1) | copy-start | bytes 3076
  15.2 8.9 %copy-start.5 = (s32[16]{0:T(128)S(1)}, s32[16]{0:T(128)}, u32[]{:S(2)}) copy-start(s32[16]{0:T(128)} %atom_ref.1) | copy-start | bytes 196
  15.2 40.9 %copy-start.2 = (bf16[128,1152]{1,0:T(8,128)(2,1)S(1)}, bf16[128,1152]{1,0:T(8,128)(2,1)}, u32[]{:S(2)}) copy-start(bf16[128,1152]{1,0:T(8,128)(2,1)} %refs_0_.3) | copy-start | bytes 884740
  15.2 41.0 %copy-start.1 = (bf16[128,1152]{1,0:T(8,128)(2,1)S(1)}, bf16[128,1152]{1,0:T(8,128)(2,1)}, u32[]{:S(2)}) copy-start(bf16[128,1152]{1,0:T(8,128)(2,1)} %refs_0_.2) | copy-start | bytes 884740
  15.3 41.0 %copy-start.3 = (s32[16]{0:T(128)S(1)}, s32[16]{0:T(128)}, u32[]{:S(2)}) copy-start(s32[16]{0:T(128)} %prof_ref.9) | copy-start | bytes 196
  15.3 45.9 %collective-permute-start.7 = (bf16[384,1152]{1,0:T(8,128)(2,1)S(1)}, bf16[384,1152]{1,0:T(8,128)(2,1)S(1)}, u32[]{:S(2)}, u32[]{:S(2)}) collective-permute-start(bf16[384,1152]{1,0:T(8,128)(2,1)S(1)} %bitcast.13), channel_id=1, source_target_pairs={{0,1},{1,0},{2,3},{3,2},{4,5},{5,4},{6,7},{7,6},{8,9},{9,8},{10,11... | collective-permute-start | bytes 2654216 | tf_op jit(solution)/shard_map/ppermute | solution.py:28
  20.6 35.7 %collective-permute-start.4 = (bf16[128,1920]{1,0:T(8,128)(2,1)S(1)}, bf16[128,1920]{1,0:T(8,128)(2,1)S(1)}, u32[]{:S(2)}, u32[]{:S(2)}) collective-permute-start(bf16[128,1920]{1,0:T(8,128)(2,1)S(1)} %collective-permute-done.2.refs_2_), channel_id=1, source_target_pairs={{0,2},{2,0},{4,6},{6,4},{8,10},{10,8},{12,14},{14,12},{16,18},{18,... | collective-permute-start | bytes 1474568 | tf_op jit(solution)/shard_map/ppermute | solution.py:28
  22.3 41.0 %collective-permute-start.8 = (bf16[384,1152]{1,0:T(8,128)(2,1)S(1)}, bf16[384,1152]{1,0:T(8,128)(2,1)S(1)}, u32[]{:S(2)}, u32[]{:S(2)}) collective-permute-start(bf16[384,1152]{1,0:T(8,128)(2,1)S(1)} %bitcast.12), channel_id=1, source_target_pairs={{0,1},{1,0},{2,3},{3,2},{4,5},{5,4},{6,7},{7,6},{8,9},{9,8},{10,11... | collective-permute-start | bytes 2654216 | tf_op jit(solution)/shard_map/ppermute | solution.py:28
  23.9 32.3 %collective-permute-start.5 = (bf16[128,1408]{1,0:T(8,128)(2,1)S(1)}, bf16[128,1408]{1,0:T(8,128)(2,1)S(1)}, u32[]{:S(2)}, u32[]{:S(2)}) collective-permute-start(bf16[128,1408]{1,0:T(8,128)(2,1)S(1)} %collective-permute-done.3.refs_3_), channel_id=1, source_target_pairs={{0,2},{2,0},{4,6},{6,4},{8,10},{10,8},{12,14},{14,12},{16,18},{18,... | collective-permute-start | bytes 1081352 | tf_op jit(solution)/shard_map/ppermute | solution.py:28
  24.7 29.3 %collective-permute-start = (f32[16,64]{1,0:T(8,128)S(1)}, f32[16,64]{1,0:T(8,128)S(1)}, u32[]{:S(2)}, u32[]{:S(2)}) collective-permute-start(f32[16,64]{1,0:T(8,128)S(1)} %get-tuple-element.33), channel_id=1, source_target_pairs={{0,1},{1,0},{2,3},{3,2},{4,5},{5,4},{6,7},{7,6},{8,9},{9,8},{10,11... | collective-permute-start | bytes 12296 | tf_op jit(solution)/shard_map/ppermute | solution.py:28
  54.0 16.5 %collective-permute-start.6 = (bf16[256,1152]{1,0:T(8,128)(2,1)S(1)}, bf16[256,1152]{1,0:T(8,128)(2,1)S(1)}, u32[]{:S(2)}, u32[]{:S(2)}) collective-permute-start(bf16[256,1152]{1,0:T(8,128)(2,1)S(1)} %bitcast.14), channel_id=1, source_target_pairs={{0,1},{1,0},{2,3},{3,2},{4,5},{5,4},{6,7},{7,6},{8,9},{9,8},{10,11... | collective-permute-start | bytes 1769480 | tf_op jit(solution)/shard_map/ppermute | solution.py:28
  56.2 17.5 %collective-permute-start.15 = (bf16[128,1152]{1,0:T(8,128)(2,1)S(1)}, bf16[128,1152]{1,0:T(8,128)(2,1)S(1)}, u32[]{:S(2)}, u32[]{:S(2)}) collective-permute-start(bf16[128,1152]{1,0:T(8,128)(2,1)S(1)} %copy-done.2), channel_id=1, source_target_pairs={{0,2},{2,0},{4,6},{6,4},{8,10},{10,8},{12,14},{14,12},{16,18},{18,... | collective-permute-start | bytes 884744 | tf_op jit(solution)/shard_map/ppermute | solution.py:28
  73.1 18.3 %collective-permute-start.9 = (bf16[4,128,1024]{2,1,0:T(8,128)(2,1)S(1)}, bf16[4,128,1024]{2,1,0:T(8,128)(2,1)S(1)}, u32[]{:S(2)}, u32[]{:S(2)}) collective-permute-start(bf16[4,128,1024]{2,1,0:T(8,128)(2,1)S(1)} %get-tuple-element.43), channel_id=1, source_target_pairs={{0,2},{2,0},{4,6},{6,4},{8,10},{10,8},{12,14},{14,12},{16,18},{18,... | collective-permute-start | bytes 3145736 | tf_op jit(solution)/shard_map/ppermute | solution.py:28
  74.3 15.0 %collective-permute-start.16 = (bf16[128,1920]{1,0:T(8,128)(2,1)S(1)}, bf16[128,1920]{1,0:T(8,128)(2,1)S(1)}, u32[]{:S(2)}, u32[]{:S(2)}) collective-permute-start(bf16[128,1920]{1,0:T(8,128)(2,1)S(1)} %get-tuple-element.55), channel_id=1, source_target_pairs={{0,4},{4,8},{8,12},{12,16},{16,20},{20,24},{24,28},{6,2},{10,6},{1... | collective-permute-start | bytes 1474568 | tf_op jit(solution)/shard_map/ppermute | solution.py:453
  77.7 11.5 %collective-permute-start.17 = (bf16[128,1408]{1,0:T(8,128)(2,1)S(1)}, bf16[128,1408]{1,0:T(8,128)(2,1)S(1)}, u32[]{:S(2)}, u32[]{:S(2)}) collective-permute-start(bf16[128,1408]{1,0:T(8,128)(2,1)S(1)} %get-tuple-element.56), channel_id=1, source_target_pairs={{0,8},{4,12},{8,16},{12,20},{16,24},{20,28},{10,2},{14,6},{18,10},... | collective-permute-start | bytes 1081352 | tf_op jit(solution)/shard_map/ppermute | solution.py:453
  89.3 6.3 %collective-permute-start.18 = (bf16[128,1920]{1,0:T(8,128)(2,1)S(1)}, bf16[128,1920]{1,0:T(8,128)(2,1)S(1)}, u32[]{:S(2)}, u32[]{:S(2)}) collective-permute-start(bf16[128,1920]{1,0:T(8,128)(2,1)S(1)} %collective-permute-done.16.refs_2_), channel_id=1, source_target_pairs={{0,2},{2,0},{4,6},{6,4},{8,10},{10,8},{12,14},{14,12},{16,18},{18,... | collective-permute-start | bytes 1474568 | tf_op jit(solution)/shard_map/ppermute | solution.py:28
  89.3 6.3 %collective-permute-start.19 = (bf16[128,1408]{1,0:T(8,128)(2,1)S(1)}, bf16[128,1408]{1,0:T(8,128)(2,1)S(1)}, u32[]{:S(2)}, u32[]{:S(2)}) collective-permute-start(bf16[128,1408]{1,0:T(8,128)(2,1)S(1)} %collective-permute-done.17.refs_3_), channel_id=1, source_target_pairs={{0,2},{2,0},{4,6},{6,4},{8,10},{10,8},{12,14},{14,12},{16,18},{18,... | collective-permute-start | bytes 1081352 | tf_op jit(solution)/shard_map/ppermute | solution.py:28
  92.3 24.7 %collective-permute-start.10 = (bf16[128,1024]{1,0:T(8,128)(2,1)S(1)}, bf16[128,1024]{1,0:T(8,128)(2,1)S(1)}, u32[]{:S(2)}, u32[]{:S(2)}) collective-permute-start(bf16[128,1024]{1,0:T(8,128)(2,1)S(1)} %get-tuple-element.51), channel_id=1, source_target_pairs={{0,4},{4,0},{2,6},{6,2},{8,12},{12,8},{10,14},{14,10},{16,20},{20,... | collective-permute-start | bytes 786440 | tf_op jit(solution)/shard_map/ppermute | solution.py:538
  94.9 22.2 %collective-permute-start.11 = (bf16[128,1024]{1,0:T(8,128)(2,1)S(1)}, bf16[128,1024]{1,0:T(8,128)(2,1)S(1)}, u32[]{:S(2)}, u32[]{:S(2)}) collective-permute-start(bf16[128,1024]{1,0:T(8,128)(2,1)S(1)} %get-tuple-element.52), channel_id=1, source_target_pairs={{4,8},{8,4},{6,10},{10,6},{12,16},{16,12},{14,18},{18,14},{20,24},... | collective-permute-start | bytes 786440 | tf_op jit(solution)/shard_map/ppermute | solution.py:538
  100.3 16.8 %collective-permute-start.12 = (bf16[128,768]{1,0:T(8,128)(2,1)S(1)}, bf16[128,768]{1,0:T(8,128)(2,1)S(1)}, u32[]{:S(2)}, u32[]{:S(2)}) collective-permute-start(bf16[128,768]{1,0:T(8,128)(2,1)S(1)} %get-tuple-element.53), channel_id=1, source_target_pairs={{0,8},{8,0},{2,10},{10,2},{4,12},{12,4},{6,14},{14,6},{16,24},{24,... | collective-permute-start | bytes 589832 | tf_op jit(solution)/shard_map/ppermute | solution.py:538
  103.1 13.9 %collective-permute-start.13 = (bf16[128,768]{1,0:T(8,128)(2,1)S(1)}, bf16[128,768]{1,0:T(8,128)(2,1)S(1)}, u32[]{:S(2)}, u32[]{:S(2)}) collective-permute-start(bf16[128,768]{1,0:T(8,128)(2,1)S(1)} %get-tuple-element.54), channel_id=1, source_target_pairs={{8,16},{16,8},{10,18},{18,10},{12,20},{20,12},{14,22},{22,14},{9,1... | collective-permute-start | bytes 589832 | tf_op jit(solution)/shard_map/ppermute | solution.py:538
  111.3 5.2 %collective-permute-start.20 = (f32[32,32]{1,0:T(8,128)S(1)}, f32[32,32]{1,0:T(8,128)S(1)}, u32[]{:S(2)}, u32[]{:S(2)}) collective-permute-start(f32[32,32]{1,0:T(8,128)S(1)} %shard_map.94), channel_id=1, source_target_pairs={{0,8},{2,10},{4,12},{6,14},{8,0},{10,2},{12,4},{14,6},{16,24},{18,... | collective-permute-start | bytes 12296 | tf_op jit(solution)/shard_map/ppermute | solution.py:28
  116.5 3.7 %collective-permute-start.21 = (f32[16,32]{1,0:T(8,128)S(1)}, f32[16,32]{1,0:T(8,128)S(1)}, u32[]{:S(2)}, u32[]{:S(2)}) collective-permute-start(f32[16,32]{1,0:T(8,128)S(1)} %slice.9), channel_id=1, source_target_pairs={{0,1},{1,0},{2,3},{3,2},{4,5},{5,4},{6,7},{7,6},{8,9},{9,8},{10,11... | collective-permute-start | bytes 6152 | tf_op jit(solution)/shard_map/ppermute | solution.py:28
  117.8 11.8 %collective-permute-start.14 = (bf16[64,1152]{1,0:T(8,128)(2,1)S(1)}, bf16[64,1152]{1,0:T(8,128)(2,1)S(1)}, u32[]{:S(2)}, u32[]{:S(2)}) collective-permute-start(bf16[64,1152]{1,0:T(8,128)(2,1)S(1)} %shard_map.90), channel_id=1, source_target_pairs={{0,1},{1,0},{2,3},{3,2},{4,5},{5,4},{6,7},{7,6},{8,9},{9,8},{10,11... | collective-permute-start | bytes 442376 | tf_op jit(solution)/shard_map/ppermute | solution.py:28
  120.2 1.2 collective-permute-start.22
  121.3 3.7 %collective-permute-start.23 = (f32[16,32]{1,0:T(8,128)S(1)}, f32[16,32]{1,0:T(8,128)S(1)}, u32[]{:S(2)}, u32[]{:S(2)}) collective-permute-start(f32[16,32]{1,0:T(8,128)S(1)} %add.14), channel_id=1, source_target_pairs={{0,4},{2,6},{4,0},{6,2},{8,12},{10,14},{12,8},{14,10},{16,20},{18,... | collective-permute-start | bytes 6152 | tf_op jit(solution)/shard_map/ppermute | solution.py:28
  125.0 4.5 %collective-permute-start.24 = (f32[16,32]{1,0:T(8,128)S(1)}, f32[16,32]{1,0:T(8,128)S(1)}, u32[]{:S(2)}, u32[]{:S(2)}) collective-permute-start(f32[16,32]{1,0:T(8,128)S(1)} %add.15.refs_5_), channel_id=1, source_target_pairs={{0,16},{2,18},{4,20},{6,22},{8,24},{10,26},{12,28},{14,30},{16,0},... | collective-permute-start | bytes 6152 | tf_op jit(solution)/shard_map/ppermute | solution.py:28
